TPU v7x, 32 devices: a whole 2x2x4 slice. The times are simulated.
32 devices in a mesh: wide: 8 (over z, core), narrow: 4 (over y, x).
Axes of the slice: x: 2, y: 2, z: 4, core: 2. Of those that a mesh axis runs over, the one named last changes fastest.
Arguments:
- inputs: bfloat16 [4096, 1024], P(('wide', 'narrow')), may hold values from -6 to 6
- cotangent: bfloat16 [4096, 1024], P(('wide', 'narrow')), may hold values from -6 to 6
- seq_len: int32 [32], replicated, may hold values from 16 to 128, as said below
- shallow_routes: int32 [4096, 1], replicated, may hold values from 0 to 7; in each aligned block of 128 rows (0 to 127, 128 to 255, ...) at most 24 rows name the same one
- deep_routes: int32 [4096, 1], replicated, may hold values from 0 to 15; in each aligned block of 128 rows (0 to 127, 128 to 255, ...) at most 12 rows name the same one
- shallow_norm_first: bfloat16 [1024], P('wide'), may hold values from 0.5 to 1.5
- shallow_attention_in: bfloat16 [1024, 3072], P('wide'), may hold values from -0.1875 to 0.1875
- shallow_attention_out: bfloat16 [1024, 1024], P('wide'), may hold values from -1 to 1
- shallow_norm_second: bfloat16 [1024], P('wide'), may hold values from 0.5 to 1.5
- shallow_dense_up: bfloat16 [1024, 4096], P(None, 'wide'), may hold values from -0.1875 to 0.1875
- shallow_dense_down: bfloat16 [4096, 1024], P('wide'), may hold values from -0.1875 to 0.1875
- shallow_mixer: bfloat16 [1024, 2], P('wide'), may hold values from -0.09375 to 0.09375
- shallow_expert_up: bfloat16 [32, 1024, 1024], P(('wide', 'narrow')), may hold values from -0.1875 to 0.1875
- shallow_expert_down: bfloat16 [32, 1024, 1024], P(('wide', 'narrow')), may hold values from -0.1875 to 0.1875
- deep_norm_first: bfloat16 [1024], P('wide'), may hold values from 0.5 to 1.5
- deep_attention_in: bfloat16 [1024, 3072], P('wide'), may hold values from -0.1875 to 0.1875
- deep_attention_out: bfloat16 [1024, 1024], P('wide'), may hold values from -1 to 1
- deep_norm_second: bfloat16 [1024], P('wide'), may hold values from 0.5 to 1.5
- deep_dense_up: bfloat16 [1024, 4096], P(None, 'wide'), may hold values from -0.1875 to 0.1875
- deep_dense_down: bfloat16 [4096, 1024], P('wide'), may hold values from -0.1875 to 0.1875
- deep_mixer: bfloat16 [1024, 2], P('wide'), may hold values from -0.09375 to 0.09375
- deep_expert_up: bfloat16 [32, 1024, 2048], P(('wide', 'narrow')), may hold values from -0.1875 to 0.1875
- deep_expert_down: bfloat16 [32, 2048, 1024], P(('wide', 'narrow')), may hold values from -0.1875 to 0.1875
Outputs:
- result: bfloat16 [4096, 1024], P(('wide', 'narrow'))
- grad_inputs: float32 [4096, 1024], P(('wide', 'narrow'))
- grad_shallow_norm_first: float32 [1024], P('wide')
- grad_shallow_attention_in: float32 [1024, 3072], P('wide')
- grad_shallow_attention_out: float32 [1024, 1024], P('wide')
- grad_shallow_norm_second: float32 [1024], P('wide')
- grad_shallow_dense_up: float32 [1024, 4096], P(None, 'wide')
- grad_shallow_dense_down: float32 [4096, 1024], P('wide')
- grad_shallow_mixer: float32 [1024, 2], P('wide')
- grad_shallow_expert_up: float32 [32, 1024, 1024], P(('wide', 'narrow'))
- grad_shallow_expert_down: float32 [32, 1024, 1024], P(('wide', 'narrow'))
- grad_deep_norm_first: float32 [1024], P('wide')
- grad_deep_attention_in: float32 [1024, 3072], P('wide')
- grad_deep_attention_out: float32 [1024, 1024], P('wide')
- grad_deep_norm_second: float32 [1024], P('wide')
- grad_deep_dense_up: float32 [1024, 4096], P(None, 'wide')
- grad_deep_dense_down: float32 [4096, 1024], P('wide')
- grad_deep_mixer: float32 [1024, 2], P('wide')
- grad_deep_expert_up: float32 [32, 1024, 2048], P(('wide', 'narrow'))
- grad_deep_expert_down: float32 [32, 2048, 1024], P(('wide', 'narrow'))
Inputs may be any that keep to these rules, and one draw needn't show every extreme that they name: Sequence s holds real tokens in its first seq_len[s] slots; some sequence fills all 128. `shallow_routes`: among the 128 rows of one sequence (aligned blocks), no expert is named more than 24 times, and in some sequence one is named exactly that often. `deep_routes`: among the 128 rows of one sequence (aligned blocks), no expert is named more than 12 times, and in some sequence one is named exactly that often.
All inputs are finite; a program needn't handle non-finite values.
Results may differ from a plain program's by a relative error of at most 0.03.
Values may be sent and summed in bfloat16 or wider, within the bound.
No kernel may reach another device: no remote copies, remote signals or barrier semaphores. Data moves between devices by JAX's collectives and lax.ppermute only.
A program may use at most 320 MiB of HBM per device.

v0:
```python
from functools import partial

import jax
import jax.numpy as jnp
from jax import lax
from jax.sharding import PartitionSpec as P

HEAD_DIM = 64
GROUP_SHALLOW = 4
GROUP_DEEP = 2


def from_partner(array, axis, apart):
    return lax.ppermute(array, axis, [(i, i ^ 1 << apart) for i in range(lax.axis_size(axis))])


def shortened(array):

    def short(part):
        return part.astype(jnp.bfloat16) if part.dtype == jnp.float32 else part

    return jax.tree.map(short, array)


def layer_norm(source, gain_vector):
    centre = source - jnp.mean(source, axis=-1, keepdims=True)
    inverse = lax.rsqrt(jnp.mean(centre * centre, axis=-1, keepdims=True) + 1e-05)
    scaled = centre * inverse
    return (scaled * gain_vector, scaled, inverse)


def norm_back(upstream, scaled, inverse, gain_vector):
    grad_scaled = upstream * gain_vector
    mean_first = jnp.mean(grad_scaled, axis=-1, keepdims=True)
    mean_second = jnp.mean(grad_scaled * scaled, axis=-1, keepdims=True)
    return (
        inverse * (grad_scaled - mean_first - scaled * mean_second),
        jnp.sum(upstream * scaled, axis=0),
    )


def activate(source):
    return jax.nn.gelu(source)


def activation_back(source, upstream):
    return jax.vjp(activate, source)[1](upstream)[0]


def left_product(former, latter):
    return lax.dot_general(
        former, latter, (((0,), (0,)), ((), ())), preferred_element_type=jnp.float32
    )


def right_product(former, latter):
    return lax.dot_general(
        former, latter, (((1,), (1,)), ((), ())), preferred_element_type=jnp.float32
    )


def select_tree(condition, former, latter):
    return jax.tree.map(partial(jnp.where, condition), former, latter)


def attention_parts(packed, length):
    slot_count, triple = packed.shape
    features = triple // 3
    head_count = features // HEAD_DIM
    queries = packed[:, :features].reshape(slot_count, head_count, HEAD_DIM)
    key_rows = packed[:, features : 2 * features].reshape(slot_count, head_count, HEAD_DIM)
    values = packed[:, 2 * features :].reshape(slot_count, head_count, HEAD_DIM)
    rows_at = lax.broadcasted_iota(jnp.int32, (slot_count, slot_count), 0)
    cols_at = lax.broadcasted_iota(jnp.int32, (slot_count, slot_count), 1)
    allowed = (cols_at <= rows_at) & (cols_at < length)
    scores = jnp.einsum(
        "qhd,khd->hqk", queries, key_rows, preferred_element_type=jnp.float32
    ) * HEAD_DIM ** (-0.5)
    return (jnp.where(allowed[None], scores, -1e30), queries, key_rows, values)


def section_bit():
    return lax.axis_size("narrow").bit_length() - 2


def pair_hand(value):
    return from_partner(value, "narrow", section_bit())


def pair_link(value):
    return from_partner(shortened(value), "narrow", section_bit()).astype(value.dtype)


def dispatch(buffer):
    return lax.all_to_all(buffer, ("wide", "narrow"), split_axis=0, concat_axis=0, tiled=True)


def combine(buffer):
    return lax.all_to_all(buffer, ("wide", "narrow"), split_axis=0, concat_axis=0, tiled=True)


def swap_rows(value, bit_level):
    return from_partner(value, "narrow", bit_level)


def swap_sums(value, bit_level):
    return from_partner(value.astype(jnp.bfloat16), "narrow", bit_level).astype(value.dtype)


def wide_rows(value):
    return lax.all_gather(value, "wide", axis=0, tiled=True)


def wide_sums(value):
    return lax.psum_scatter(
        value.astype(jnp.bfloat16), "wide", scatter_dimension=0, tiled=True
    ).astype(jnp.float32)


def member_bit(bit_level):
    return lax.axis_index("narrow") >> bit_level & 1 == 1


def ordered(own_block, partner_block, upper_bit):
    return jnp.where(
        upper_bit, jnp.stack([partner_block, own_block]), jnp.stack([own_block, partner_block])
    )


def collect(arrived, live_layers):
    devices, rows_each, features = arrived.shape
    wide_count = lax.axis_size("wide")
    half_count = lax.axis_size("narrow") // 2
    arranged = arrived.reshape((wide_count, 2, half_count, rows_each, features))
    lower_end = 0 if live_layers[0] else 1
    upper_end = 2 if live_layers[1] else 1
    portion = arranged[:, lower_end:upper_end]
    paired = ordered(portion, swap_rows(portion, 0), member_bit(0))
    shallow_rows, deep_rows = (None, None)
    if live_layers[0]:
        leading = paired[:, :, 0]
        quartet = ordered(leading, swap_rows(leading, 1), member_bit(1))
        shallow_rows = quartet.reshape(-1, features)
    if live_layers[1]:
        deep_rows = paired[:, :, upper_end - lower_end - 1].reshape(-1, features)
    return (shallow_rows, deep_rows)


def spread(shallow_part, deep_part, live_layers, arrived_shape):
    devices, rows_each, features = arrived_shape
    wide_count = lax.axis_size("wide")
    half_count = lax.axis_size("narrow") // 2
    pieces = []
    if live_layers[0]:
        quartet = shallow_part.reshape((2, 2, wide_count, half_count, rows_each, features))
        upper_high = member_bit(1)
        retained = jnp.where(upper_high, quartet[1], quartet[0])
        outgoing = jnp.where(upper_high, quartet[0], quartet[1])
        pieces.append(retained + swap_sums(outgoing, 1))
    if live_layers[1]:
        pieces.append(deep_part.reshape((2, wide_count, half_count, rows_each, features)))
    stacked = jnp.stack(pieces, axis=2)
    upper_low = member_bit(0)
    retained = jnp.where(upper_low, stacked[1], stacked[0])
    outgoing = jnp.where(upper_low, stacked[0], stacked[1])
    summed = retained + swap_sums(outgoing, 0)
    padding = jnp.zeros_like(summed)
    if not live_layers[0]:
        summed = jnp.concatenate([padding, summed], axis=1)
    if not live_layers[1]:
        summed = jnp.concatenate([summed, padding], axis=1)
    return summed.reshape(devices, rows_each, features)


def expert_apply(row_block, weight_up, weight_down):
    pre_act = jnp.dot(row_block, weight_up[0], preferred_element_type=jnp.float32)
    activated = activate(pre_act).astype(jnp.bfloat16)
    return (
        jnp.dot(activated, weight_down[0], preferred_element_type=jnp.float32),
        (row_block, pre_act, activated),
    )


def expert_grad(grad_rows, layer_kept, weight_up, weight_down):
    row_block, pre_act, activated = layer_kept
    grad_pre = activation_back(pre_act, right_product(grad_rows, weight_down[0])).astype(
        jnp.bfloat16
    )
    grads = (left_product(row_block, grad_pre)[None], left_product(activated, grad_rows)[None])
    return (right_product(grad_pre, weight_up[0]), grads)


def experts_forward(arrived, live_layers, expert_weights):
    shallow_up, shallow_down, deep_up, deep_down = expert_weights
    shallow_rows, deep_rows = collect(arrived, live_layers)
    shallow_out, shallow_kept, deep_out, deep_kept = (None, None, None, None)
    if live_layers[0]:
        shallow_out, shallow_kept = expert_apply(shallow_rows, shallow_up, shallow_down)
    if live_layers[1]:
        deep_out, deep_kept = expert_apply(deep_rows, deep_up, deep_down)
    summed = spread(shallow_out, deep_out, live_layers, arrived.shape)
    return (summed.astype(jnp.bfloat16), (shallow_kept, deep_kept))


def experts_backward(grad_arrived, live_layers, expert_kept, expert_weights):
    shallow_up, shallow_down, deep_up, deep_down = expert_weights
    shallow_rows, deep_rows = collect(grad_arrived, live_layers)
    shallow_back, shallow_grads, deep_back, deep_grads = (None, None, None, None)
    if live_layers[0]:
        shallow_back, shallow_grads = expert_grad(
            shallow_rows, expert_kept[0], shallow_up, shallow_down
        )
    if live_layers[1]:
        deep_back, deep_grads = expert_grad(deep_rows, expert_kept[1], deep_up, deep_down)
    summed = spread(shallow_back, deep_back, live_layers, grad_arrived.shape)
    return (summed.astype(jnp.bfloat16), (shallow_grads, deep_grads))


def ffn_forward(second_low, dense_up, dense_down):
    row_block = wide_rows(second_low)
    pre_act = jnp.dot(row_block, dense_up, preferred_element_type=jnp.float32)
    activated = activate(pre_act).astype(jnp.bfloat16)
    partial_sums = jnp.dot(activated, dense_down, preferred_element_type=jnp.float32)
    summed = wide_sums(partial_sums)
    return (summed, (row_block, pre_act, activated))


def ffn_backward(grad_dense, dense_kept, dense_up, dense_down):
    row_block, pre_act, activated = dense_kept
    grad_rows = wide_rows(grad_dense)
    grad_down = left_product(activated, grad_rows)
    grad_pre = activation_back(pre_act, right_product(grad_rows, dense_down)).astype(jnp.bfloat16)
    grad_up = left_product(row_block, grad_pre)
    partial_sums = right_product(grad_pre, dense_up)
    summed = wide_sums(partial_sums)
    return (summed, grad_up, grad_down)


def gather_layer(local_set):
    norm_first, attention_in, attention_out, norm_second, mixer, dense_up, dense_down = local_set
    gathered = (
        lax.all_gather(shortened(norm_first), "wide", axis=0, tiled=True).astype(norm_first.dtype),
        lax.all_gather(shortened(attention_in), "wide", axis=0, tiled=True).astype(
            attention_in.dtype
        ),
        lax.all_gather(shortened(attention_out), "wide", axis=0, tiled=True).astype(
            attention_out.dtype
        ),
        lax.all_gather(shortened(norm_second), "wide", axis=0, tiled=True).astype(
            norm_second.dtype
        ),
        lax.all_gather(shortened(mixer), "wide", axis=0, tiled=True).astype(mixer.dtype),
    )
    return tuple(gathered) + (dense_up, dense_down)


def share_grads(grads):
    norm_first, attention_in, attention_out, norm_second, mixer, dense_up, dense_down = grads
    shared = (
        lax.psum_scatter(
            norm_first.astype(jnp.bfloat16), "wide", scatter_dimension=0, tiled=True
        ).astype(jnp.float32),
        lax.psum_scatter(
            attention_in.astype(jnp.bfloat16), "wide", scatter_dimension=0, tiled=True
        ).astype(jnp.float32),
        lax.psum_scatter(
            attention_out.astype(jnp.bfloat16), "wide", scatter_dimension=0, tiled=True
        ).astype(jnp.float32),
        lax.psum_scatter(
            norm_second.astype(jnp.bfloat16), "wide", scatter_dimension=0, tiled=True
        ).astype(jnp.float32),
        lax.psum_scatter(
            mixer.astype(jnp.bfloat16), "wide", scatter_dimension=0, tiled=True
        ).astype(jnp.float32),
    )
    return tuple(shared) + (dense_up, dense_down)


def micro_plan(
    seq_index, section_first, seq_len, shallow_routes, deep_routes, slot_count, rows_each, devices
):
    start_row = seq_index * slot_count
    shallow_part = lax.dynamic_slice_in_dim(shallow_routes[:, 0], start_row, slot_count)
    deep_part = lax.dynamic_slice_in_dim(deep_routes[:, 0], start_row, slot_count)
    labels = jnp.where(section_first, shallow_part, deep_part)
    capacity = jnp.where(section_first, GROUP_SHALLOW * rows_each, GROUP_DEEP * rows_each)
    one_hot = (
        labels[:, None] == jnp.arange(devices // GROUP_DEEP, dtype=jnp.int32)[None, :]
    ).astype(jnp.int32)
    ranking = jnp.sum(jnp.cumsum(one_hot, axis=0) * one_hot, axis=1) - 1
    length = lax.dynamic_index_in_dim(seq_len, seq_index, keepdims=False)
    return (length, labels * capacity + ranking)


def forward_slot(source, plan_pair, weights, expert_weights, live_layers):
    length, slot_index = plan_pair
    norm_first, attention_in, attention_out, norm_second, mixer, dense_up, dense_down = weights
    slot_count, features = source.shape
    normed, scaled_one, inverse_one = layer_norm(source, norm_first.astype(jnp.float32))
    normed_low = normed.astype(jnp.bfloat16)
    packed = jnp.dot(normed_low, attention_in, preferred_element_type=jnp.float32).astype(
        jnp.bfloat16
    )
    scores, queries, key_rows, values = attention_parts(packed, length)
    row_peak = jnp.max(scores, axis=-1, keepdims=True)
    raised = jnp.exp(scores - row_peak)
    row_total = jnp.sum(raised, axis=-1, keepdims=True)
    softened = (raised / row_total).astype(jnp.bfloat16)
    log_total = row_peak + jnp.log(row_total)
    context = jnp.einsum("hqk,khd->qhd", softened, values, preferred_element_type=jnp.float32)
    context = context.reshape(slot_count, features).astype(jnp.bfloat16)
    middle = source + jnp.dot(context, attention_out, preferred_element_type=jnp.float32)
    second, scaled_two, inverse_two = layer_norm(middle, norm_second.astype(jnp.float32))
    second_low = second.astype(jnp.bfloat16)
    dense_result, dense_kept = ffn_forward(second_low, dense_up, dense_down)
    mixing = jax.nn.softmax(jnp.dot(second_low, mixer, preferred_element_type=jnp.float32), axis=-1)
    devices = lax.axis_size("wide") * lax.axis_size("narrow")
    rows_each = max(1, 3 * slot_count // (2 * devices))
    buffer = jnp.zeros((devices * rows_each, features), jnp.bfloat16).at[slot_index].set(second_low)
    arrived = dispatch(buffer.reshape(devices, rows_each, features))
    outcome, expert_kept = experts_forward(arrived, live_layers, expert_weights)
    returned = combine(outcome)
    expert_result = returned.reshape(-1, features)[slot_index].astype(jnp.float32)
    output = middle + mixing[:, :1] * dense_result + mixing[:, 1:] * expert_result
    stored = (
        normed_low,
        scaled_one,
        inverse_one,
        packed,
        log_total,
        context,
        scaled_two,
        inverse_two,
        second_low,
        dense_kept,
        dense_result,
        mixing,
        slot_index,
        expert_result,
        length,
    )
    return (output, stored, expert_kept)


def backward_slot(upstream, stored, weights, expert_weights, expert_kept, live_layers):
    (
        normed_low,
        scaled_one,
        inverse_one,
        packed,
        log_total,
        context,
        scaled_two,
        inverse_two,
        second_low,
        dense_kept,
        dense_result,
        mixing,
        slot_index,
        expert_result,
        length,
    ) = stored
    norm_first, attention_in, attention_out, norm_second, mixer, dense_up, dense_down = weights
    slot_count, features = upstream.shape
    head_count = features // HEAD_DIM
    grad_mixing = jnp.stack(
        [jnp.sum(upstream * dense_result, axis=1), jnp.sum(upstream * expert_result, axis=1)],
        axis=1,
    )
    grad_logits = mixing * (grad_mixing - jnp.sum(mixing * grad_mixing, axis=1, keepdims=True))
    grad_logits = grad_logits.astype(jnp.bfloat16)
    grad_mixer = left_product(second_low, grad_logits)
    grad_second = right_product(grad_logits, mixer)
    grad_dense = (upstream * mixing[:, :1]).astype(jnp.bfloat16)
    dense_second, grad_dense_up, grad_dense_down = ffn_backward(
        grad_dense, dense_kept, dense_up, dense_down
    )
    grad_second = grad_second + dense_second
    devices = lax.axis_size("wide") * lax.axis_size("narrow")
    rows_each = max(1, 3 * slot_count // (2 * devices))
    grad_expert = (upstream * mixing[:, 1:]).astype(jnp.bfloat16)
    buffer = (
        jnp.zeros((devices * rows_each, features), jnp.bfloat16).at[slot_index].set(grad_expert)
    )
    grad_arrived = dispatch(buffer.reshape(devices, rows_each, features))
    outcome, expert_grads = experts_backward(grad_arrived, live_layers, expert_kept, expert_weights)
    returned = combine(outcome)
    grad_second = grad_second + returned.reshape(-1, features)[slot_index].astype(jnp.float32)
    grad_norm_part, grad_norm_second = norm_back(
        grad_second, scaled_two, inverse_two, norm_second.astype(jnp.float32)
    )
    grad_middle = upstream + grad_norm_part
    grad_attended = grad_middle.astype(jnp.bfloat16)
    grad_attention_out = left_product(context, grad_attended)
    grad_context = right_product(grad_attended, attention_out).astype(jnp.bfloat16)
    grad_context = grad_context.reshape(slot_count, head_count, HEAD_DIM)
    scores, queries, key_rows, values = attention_parts(packed, length)
    softened = jnp.exp(scores - log_total)
    grad_soft = jnp.einsum("qhd,khd->hqk", grad_context, values, preferred_element_type=jnp.float32)
    grad_scores = softened * (grad_soft - jnp.sum(softened * grad_soft, axis=-1, keepdims=True))
    grad_scores = grad_scores.astype(jnp.bfloat16)
    scaling = HEAD_DIM ** (-0.5)
    grad_queries = (
        jnp.einsum("hqk,khd->qhd", grad_scores, key_rows, preferred_element_type=jnp.float32)
        * scaling
    )
    grad_keys = (
        jnp.einsum("hqk,qhd->khd", grad_scores, queries, preferred_element_type=jnp.float32)
        * scaling
    )
    grad_values = jnp.einsum(
        "hqk,qhd->khd",
        softened.astype(jnp.bfloat16),
        grad_context,
        preferred_element_type=jnp.float32,
    )
    grad_packed = jnp.concatenate(
        [
            grad_queries.reshape(slot_count, features),
            grad_keys.reshape(slot_count, features),
            grad_values.reshape(slot_count, features),
        ],
        axis=1,
    ).astype(jnp.bfloat16)
    grad_attention_in = left_product(normed_low, grad_packed)
    grad_norm_part, grad_norm_first = norm_back(
        right_product(grad_packed, attention_in),
        scaled_one,
        inverse_one,
        norm_first.astype(jnp.float32),
    )
    grad_inputs = grad_middle + grad_norm_part
    dense_grads = (
        grad_norm_first,
        grad_attention_in,
        grad_attention_out,
        grad_norm_second,
        grad_mixer,
        grad_dense_up,
        grad_dense_down,
    )
    return (grad_inputs, dense_grads, expert_grads)


def body(
    inputs,
    cotangent,
    seq_len,
    shallow_routes,
    deep_routes,
    shallow_norm_first,
    shallow_attention_in,
    shallow_attention_out,
    shallow_norm_second,
    shallow_dense_up,
    shallow_dense_down,
    shallow_mixer,
    shallow_expert_up,
    shallow_expert_down,
    deep_norm_first,
    deep_attention_in,
    deep_attention_out,
    deep_norm_second,
    deep_dense_up,
    deep_dense_down,
    deep_mixer,
    deep_expert_up,
    deep_expert_down,
):
    narrow_count = lax.axis_size("narrow")
    wide_count = lax.axis_size("wide")
    half_count = narrow_count // 2
    devices = wide_count * narrow_count
    slot_count, features = inputs.shape
    rows_each = max(1, 3 * slot_count // (2 * devices))
    section_index = lax.axis_index("narrow") // half_count
    section_first = section_index == 0
    lead_seq = (
        lax.axis_index("wide") * narrow_count
        + lax.axis_index("narrow")
        - section_index * half_count
    )
    trail_seq = lead_seq + half_count
    shallow_local = (
        shallow_norm_first,
        shallow_attention_in,
        shallow_attention_out,
        shallow_norm_second,
        shallow_mixer,
        shallow_dense_up,
        shallow_dense_down,
    )
    deep_local = (
        deep_norm_first,
        deep_attention_in,
        deep_attention_out,
        deep_norm_second,
        deep_mixer,
        deep_dense_up,
        deep_dense_down,
    )
    weights = gather_layer(select_tree(section_first, shallow_local, deep_local))
    expert_weights = (shallow_expert_up, shallow_expert_down, deep_expert_up, deep_expert_down)

    def plan_for(seq_index):
        return micro_plan(
            seq_index,
            section_first,
            seq_len,
            shallow_routes,
            deep_routes,
            slot_count,
            rows_each,
            devices,
        )

    plan_zero = plan_for(lead_seq)
    plan_one = plan_for(jnp.where(section_first, trail_seq, lead_seq))
    plan_two = plan_for(trail_seq)
    source = inputs.astype(jnp.float32)
    own_cotangent = cotangent.astype(jnp.float32)
    blank_rows = jnp.zeros_like(source)
    handed = pair_hand(jnp.where(section_first, cotangent, inputs)).astype(jnp.float32)
    forward_zero, stash_zero, expert_zero = forward_slot(
        jnp.where(section_first, source, blank_rows),
        plan_zero,
        weights,
        expert_weights,
        (True, False),
    )
    linked = pair_link(jnp.where(section_first, forward_zero, blank_rows))
    forward_one, stash_one, expert_one = forward_slot(
        jnp.where(section_first, handed, linked), plan_one, weights, expert_weights, (True, True)
    )
    backward_one, dense_one, grads_one = backward_slot(
        jnp.where(section_first, blank_rows, handed),
        stash_one,
        weights,
        expert_weights,
        (None, expert_one[1]),
        (False, True),
    )
    linked = pair_link(jnp.where(section_first, forward_one, backward_one))
    forward_two, stash_two, expert_two = forward_slot(
        linked, plan_two, weights, expert_weights, (False, True)
    )
    stash_middle = select_tree(section_first, stash_zero, stash_two)
    backward_two, dense_two, grads_two = backward_slot(
        jnp.where(section_first, linked, own_cotangent),
        stash_middle,
        weights,
        expert_weights,
        (expert_zero[0], expert_two[1]),
        (True, True),
    )
    linked = pair_link(jnp.where(section_first, blank_rows, backward_two))
    backward_three, dense_three, grads_three = backward_slot(
        jnp.where(section_first, linked, blank_rows),
        stash_one,
        weights,
        expert_weights,
        (expert_one[0], None),
        (True, False),
    )
    returned = pair_link(jnp.where(section_first, backward_three, forward_one))
    result = jnp.where(section_first, returned, forward_two).astype(jnp.bfloat16)
    grad_inputs = jnp.where(section_first, backward_two, returned)
    dense_total = jax.tree.map(jnp.add, jax.tree.map(jnp.add, dense_one, dense_two), dense_three)
    shares = share_grads(dense_total)
    zero_shares = tuple((jnp.zeros_like(member) for member in shares))
    shallow_side = select_tree(section_first, shares, zero_shares)
    deep_side = select_tree(section_first, zero_shares, shares)
    totals = (
        lax.psum(shallow_side[0].astype(jnp.bfloat16), "narrow").astype(jnp.float32),
        lax.psum(shallow_side[1].astype(jnp.bfloat16), "narrow").astype(jnp.float32),
        lax.psum(shallow_side[2].astype(jnp.bfloat16), "narrow").astype(jnp.float32),
        lax.psum(shallow_side[3].astype(jnp.bfloat16), "narrow").astype(jnp.float32),
        lax.psum(shallow_side[4].astype(jnp.bfloat16), "narrow").astype(jnp.float32),
        lax.psum(shallow_side[5].astype(jnp.bfloat16), "narrow").astype(jnp.float32),
        lax.psum(shallow_side[6].astype(jnp.bfloat16), "narrow").astype(jnp.float32),
        lax.psum(deep_side[0].astype(jnp.bfloat16), "narrow").astype(jnp.float32),
        lax.psum(deep_side[1].astype(jnp.bfloat16), "narrow").astype(jnp.float32),
        lax.psum(deep_side[2].astype(jnp.bfloat16), "narrow").astype(jnp.float32),
        lax.psum(deep_side[3].astype(jnp.bfloat16), "narrow").astype(jnp.float32),
        lax.psum(deep_side[4].astype(jnp.bfloat16), "narrow").astype(jnp.float32),
        lax.psum(deep_side[5].astype(jnp.bfloat16), "narrow").astype(jnp.float32),
        lax.psum(deep_side[6].astype(jnp.bfloat16), "narrow").astype(jnp.float32),
    )
    shallow_up_grad = grads_two[0][0] + grads_three[0][0]
    shallow_down_grad = grads_two[0][1] + grads_three[0][1]
    deep_up_grad = grads_one[1][0] + grads_two[1][0]
    deep_down_grad = grads_one[1][1] + grads_two[1][1]
    return (
        result,
        grad_inputs,
        totals[0],
        totals[1],
        totals[2],
        totals[3],
        totals[5],
        totals[6],
        totals[4],
        shallow_up_grad,
        shallow_down_grad,
        totals[7],
        totals[8],
        totals[9],
        totals[10],
        totals[12],
        totals[13],
        totals[11],
        deep_up_grad,
        deep_down_grad,
    )


def solution(mesh):
    return jax.shard_map(
        body,
        mesh=mesh,
        in_specs=(
            P(("wide", "narrow"), None),
            P(("wide", "narrow"), None),
            P(),
            P(),
            P(),
            P("wide"),
            P("wide", None),
            P("wide", None),
            P("wide"),
            P(None, "wide"),
            P("wide", None),
            P("wide", None),
            P(("wide", "narrow"), None, None),
            P(("wide", "narrow"), None, None),
            P("wide"),
            P("wide", None),
            P("wide", None),
            P("wide"),
            P(None, "wide"),
            P("wide", None),
            P("wide", None),
            P(("wide", "narrow"), None, None),
            P(("wide", "narrow"), None, None),
        ),
        out_specs=(
            P(("wide", "narrow"), None),
            P(("wide", "narrow"), None),
            P("wide"),
            P("wide", None),
            P("wide", None),
            P("wide"),
            P(None, "wide"),
            P("wide", None),
            P("wide", None),
            P(("wide", "narrow"), None, None),
            P(("wide", "narrow"), None, None),
            P("wide"),
            P("wide", None),
            P("wide", None),
            P("wide"),
            P(None, "wide"),
            P("wide", None),
            P("wide", None),
            P(("wide", "narrow"), None, None),
            P(("wide", "narrow"), None, None),
        ),
        check_vma=False,
    )
```

profile of v0, /device:TPU:0, one launch (start us, length us, event | category | flops | bytes accessed | tf_op | source)
XLA Modules:
  0.0 1289.6 jit_solution(13716590472087124080)
XLA Ops:
  10.6 13.5 %all-gather.1 = bf16[8,1,128]{2,1,0:T(2,128)(2,1)S(1)} all-gather(bf16[1,1,128]{2,1,0:T(2,128)(2,1)S(1)} %fusion.242), channel_id=1, replica_groups=mesh['wide'=8,'narrow'=4] {'wide'}, dimensions={0}, use_global_device_ids=true | all-gather | bytes 2304 | tf_op jit(solution)/shard_map/all_gather | solution.py:249
  24.1 9.2 all-gather
  35.0 42.8 %all-gather.11.cloned.1.call-done = bf16[1024,3072]{1,0:T(8,128)(2,1)} async-done(((bf16[128,3072]{1,0:T(8,128)(2,1)}), bf16[1024,3072]{1,0:T(8,128)(2,1)}) %all-gather.11.cloned.1.call-update) | async-done | bytes 6291472 | tf_op jit(solution)/shard_map/all_gather | solution.py:243
  84.2 23.5 %all-gather.13.cloned.1.call-done = bf16[1024,1024]{1,0:T(8,128)(2,1)} async-done(((bf16[128,1024]{1,0:T(8,128)(2,1)}), bf16[1024,1024]{1,0:T(8,128)(2,1)}) %all-gather.13.cloned.1.call-update) | async-done | bytes 2097168 | tf_op jit(solution)/shard_map/all_gather | solution.py:246
  124.5 24.6 %all-to-all-done = bf16[32,6,1024]{2,1,0:T(8,128)(2,1)} async-done(((bf16[32,6,1024]{2,1,0:T(8,128)(2,1)}), bf16[32,6,1024]{2,1,0:T(8,128)(2,1)}, u32[]{:S(2)}, u32[]{:S(2)}) %all-to-all-start) | async-done | bytes 393248 | tf_op jit(solution)/shard_map/all_to_all | solution.py:95
  162.5 9.5 collective-permute-done.2
  191.7 7.8 collective-permute-done.3
  202.6 9.7 all_gather.37
  217.2 15.7 %all-to-all-done.1 = bf16[32,6,1024]{2,1,0:T(8,128)(2,1)} async-done(((bf16[32,6,1024]{2,1,0:T(8,128)(2,1)}), bf16[32,6,1024]{2,1,0:T(8,128)(2,1)}, u32[]{:S(2)}, u32[]{:S(2)}) %all-to-all-start.1) | async-done | bytes 393248 | tf_op jit(solution)/shard_map/all_to_all | solution.py:99
  237.9 6.3 collective-permute-done.5
  264.8 30.8 %all_to_all.60 = bf16[32,6,1024]{2,1,0:T(8,128)(2,1)S(1)} all-to-all(bf16[32,6,1024]{2,1,0:T(8,128)(2,1)} %reshape.1178), channel_id=1, replica_groups=mesh['wide'=8,'narrow'=4] {'wide','narrow'}, dimensions={0} | all-to-all | bytes 786432 | tf_op jit(solution)/shard_map/all_to_all | solution.py:95
  298.0 9.2 collective-permute-done.6
  360.0 7.7 collective-permute-done.9
  373.5 15.0 %all-to-all-done.3 = bf16[32,6,1024]{2,1,0:T(8,128)(2,1)} async-done(((bf16[32,6,1024]{2,1,0:T(8,128)(2,1)}), bf16[32,6,1024]{2,1,0:T(8,128)(2,1)}, u32[]{:S(2)}, u32[]{:S(2)}) %all-to-all-start.3) | async-done | bytes 393248 | tf_op jit(solution)/shard_map/all_to_all | solution.py:99
  395.4 26.9 %all-gather.19.cloned.1.call-done = bf16[1024,1024]{1,0:T(8,128)(2,1)} async-done(((bf16[128,1024]{1,0:T(8,128)(2,1)}), bf16[1024,1024]{1,0:T(8,128)(2,1)}) %all-gather.19.cloned.1.call-update) | async-done | bytes 2097168 | tf_op jit(solution)/shard_map/all_gather | solution.py:111
  434.8 27.2 %all_to_all.61 = bf16[32,6,1024]{2,1,0:T(8,128)(2,1)S(1)} all-to-all(bf16[32,6,1024]{2,1,0:T(8,128)(2,1)} %reshape.1182), channel_id=1, replica_groups=mesh['wide'=8,'narrow'=4] {'wide','narrow'}, dimensions={0} | all-to-all | bytes 786432 | tf_op jit(solution)/shard_map/all_to_all | solution.py:95
  463.6 6.6 collective-permute-done.10
  473.0 5.1 fusion.84
  496.7 15.8 %all-to-all-done.5 = bf16[32,6,1024]{2,1,0:T(8,128)(2,1)} async-done(((bf16[32,6,1024]{2,1,0:T(8,128)(2,1)}), bf16[32,6,1024]{2,1,0:T(8,128)(2,1)}, u32[]{:S(2)}, u32[]{:S(2)}) %all-to-all-start.5) | async-done | bytes 393248 | tf_op jit(solution)/shard_map/all_to_all | solution.py:99
  529.3 5.9 multiply_reduce_fusion.8
  536.6 6.4 collective-permute-done.12
  557.7 27.4 %all-gather.21.cloned.1.call-done = bf16[1024,1024]{1,0:T(8,128)(2,1)} async-done(((bf16[128,1024]{1,0:T(8,128)(2,1)}), bf16[1024,1024]{1,0:T(8,128)(2,1)}) %all-gather.21.cloned.1.call-update) | async-done | bytes 2097168 | tf_op jit(solution)/shard_map/all_gather | solution.py:111
  597.5 27.1 %all_to_all.62 = bf16[32,6,1024]{2,1,0:T(8,128)(2,1)S(1)} all-to-all(bf16[32,6,1024]{2,1,0:T(8,128)(2,1)} %reshape.1192), channel_id=1, replica_groups=mesh['wide'=8,'narrow'=4] {'wide','narrow'}, dimensions={0} | all-to-all | bytes 786432 | tf_op jit(solution)/shard_map/all_to_all | solution.py:95
  625.9 6.6 collective-permute-done.13
  658.3 15.0 %all-to-all-done.7 = bf16[32,6,1024]{2,1,0:T(8,128)(2,1)} async-done(((bf16[32,6,1024]{2,1,0:T(8,128)(2,1)}), bf16[32,6,1024]{2,1,0:T(8,128)(2,1)}, u32[]{:S(2)}, u32[]{:S(2)}) %all-to-all-start.7) | async-done | bytes 393248 | tf_op jit(solution)/shard_map/all_to_all | solution.py:99
  686.9 31.2 %all_to_all.63 = bf16[32,6,1024]{2,1,0:T(8,128)(2,1)S(1)} all-to-all(bf16[32,6,1024]{2,1,0:T(8,128)(2,1)} %reshape.1195), channel_id=1, replica_groups=mesh['wide'=8,'narrow'=4] {'wide','narrow'}, dimensions={0} | all-to-all | bytes 786432 | tf_op jit(solution)/shard_map/all_to_all | solution.py:95
  720.5 9.1 collective-permute-done.15
  746.0 5.9 fusion.91
  788.2 6.9 collective-permute-done.18
  809.2 8.3 all-to-all-done.9
  834.0 5.8 multiply_reduce_fusion.7
  841.3 7.1 collective-permute-done.19
  853.7 31.6 %all_to_all.64 = bf16[32,6,1024]{2,1,0:T(8,128)(2,1)S(1)} all-to-all(bf16[32,6,1024]{2,1,0:T(8,128)(2,1)} %reshape.1206), channel_id=1, replica_groups=mesh['wide'=8,'narrow'=4] {'wide','narrow'}, dimensions={0} | all-to-all | bytes 786432 | tf_op jit(solution)/shard_map/all_to_all | solution.py:95
  904.6 6.8 collective-permute-done.21
  930.8 7.5 collective-permute-done.22
  964.3 6.3 all-to-all-done.11
  979.8 5.5 add_convert_fusion.1
  985.4 7.7 fusion.181
  993.1 6.6 fusion.179
  1006.9 13.0 %add_convert_fusion = bf16[1024,3072]{1,0:T(8,128)(2,1)} fusion(f32[1024,3072]{1,0:T(8,128)} %fusion.181, f32[1024,3072]{1,0:T(8,128)} %fusion.179, bf16[128,1024]{1,0:T(8,128)(2,1)S(1)} %copy-done.42, bf16[128,1024]{0,1:T(8,128)(2,1)S(1)} %bitcast.482, bf16[128,1024]{0,1:T(8,128)(2,1)S(1)} %bitcast.478, bf16[128,1024]{0,1:T(8,128)(2,1)S(1)} %bitcast.480), kind=kOutput, calls=%fused_computation.12 | convolution fusion | flops 817102848 | bytes 32505856 | tf_op jit(solution)/shard_map/dot_general | solution.py:51
  1038.1 6.5 select_convert_fusion
  1049.2 41.1 %reduce-scatter.24.cloned.1.call-done = bf16[128,3072]{1,0:T(8,128)(2,1)} async-done(((bf16[1024,3072]{1,0:T(8,128)(2,1)}), bf16[128,3072]{1,0:T(8,128)(2,1)}) %reduce-scatter.24.cloned.1.call-update) | async-done | bytes 786448 | tf_op jit(solution)/shard_map/reduce_scatter | solution.py:263
  1115.1 6.7 reduce-scatter.28.cloned.1.call-done
  1122.6 5.9 add_bitcast_fusion.3
  1128.6 5.3 add_bitcast_fusion.2
  1139.2 13.8 %all-reduce.6 = (bf16[1024]{0:T(1024)(128)(2,1)S(1)}, bf16[1024]{0:T(1024)(128)(2,1)S(1)}) all-reduce(bf16[1024]{0:T(1024)(128)(2,1)S(1)} %add_convert_fusion.7, bf16[1024]{0:T(1024)(128)(2,1)S(1)} %add_convert_fusion.6), channel_id=8, replica_groups=mesh['wide'=8,'narrow'=4] {'wide'}, use_global_device_ids=true, to_apply=%region_69.70.clone | all-reduce | flops 2048 | bytes 8192
  1153.0 9.5 all-reduce.7
  1168.2 101.7 %all-reduce.11.cloned.1.call-done = (bf16[128,3072]{1,0:T(8,128)(2,1)}, bf16[128,1024]{1,0:T(8,128)(2,1)}, bf16[1024,512]{1,0:T(8,128)(2,1)}, bf16[512,1024]{1,0...) async-done(((bf16[128,3072]{1,0:T(8,128)(2,1)}, bf16[128,1024]{1,0:T(8,128)(2,1)}, ...) | async-done | bytes 6291472 | tf_op jit(solution)/shard_map/psum | solution.py:575
  (853 shorter events, 525.0 us)
Async XLA Ops:
  7.2 70.5 %all-gather.11.cloned.1.call-start = ((), (), s32[]{:S(2)}) async-start(), calls=%async_computation.21 | async-start | bytes 7077888 | tf_op jit(solution)/shard_map/all_gather | solution.py:243
  9.6 98.1 %all-gather.13.cloned.1.call-start = ((), (), s32[]{:S(2)}) async-start(), calls=%async_computation.22 | async-start | bytes 2359296 | tf_op jit(solution)/shard_map/all_gather | solution.py:246
  10.5 141.4 %all-gather.15.cloned.1.call-start = ((), (), s32[]{:S(2)}) async-start(), calls=%async_computation.23 | async-start | bytes 2359296 | tf_op jit(solution)/shard_map/all_gather | solution.py:111
  116.5 32.6 %all-to-all-start = ((bf16[32,6,1024]{2,1,0:T(8,128)(2,1)}), bf16[32,6,1024]{2,1,0:T(8,128)(2,1)}, u32[]{:S(2)}, u32[]{:S(2)}) async-start(bf16[32,6,1024]{2,1,0:T(8,128)(2,1)} %reshape.1172), calls=%async_computation.1 | async-start | bytes 1048576 | tf_op jit(solution)/shard_map/all_to_all | solution.py:95
  120.6 115.0 %reduce-scatter.12.cloned.1.call-start = ((), (), s32[]{:S(2)}) async-start(), calls=%async_computation.24 | async-start | bytes 2359296 | tf_op jit(solution)/shard_map/reduce_scatter | solution.py:115
  150.3 8.9 collective-permute-start.1
  160.5 11.6 collective-permute-start.2
  184.4 15.1 %collective-permute-start.3 = (bf16[2,8,2,6,1024]{4,3,2,1,0:T(8,128)(2,1)}, bf16[2,8,2,6,1024]{4,3,2,1,0:T(8,128)(2,1)}, u32[]{:S(2)}, u32[]{:S(2)}) collective-permute-start(bf16[2,8,2,6,1024]{4,3,2,1,0:T(8,128)(2,1)} %convert_element_type.565), channel_id=1, source_target_pairs={{0,2},{1,3},{2,0},{3,1},{4,6},{5,7},{6,4},{7,5},{8,10},{9,11},{10,... | collective-permute-start | bytes 1179656 | tf_op jit(solution)/shard_map/ppermute | solution.py:14
  186.6 51.3 %collective-permute-start = (bf16[128,1024]{1,0:T(8,128)(2,1)}, bf16[128,1024]{1,0:T(8,128)(2,1)S(1)}, u32[]{:S(2)}, u32[]{:S(2)}) collective-permute-start(bf16[128,1024]{1,0:T(8,128)(2,1)} %broadcast_select_fusion.15), channel_id=1, source_target_pairs={{0,2},{1,3},{2,0},{3,1},{4,6},{5,7},{6,4},{7,5},{8,10},{9,11},{10,... | collective-permute-start | bytes 786440 | tf_op jit(solution)/shard_map/ppermute | solution.py:14
  201.1 11.2 collective-permute-start.4
  213.3 19.6 %all-to-all-start.1 = ((bf16[32,6,1024]{2,1,0:T(8,128)(2,1)}), bf16[32,6,1024]{2,1,0:T(8,128)(2,1)}, u32[]{:S(2)}, u32[]{:S(2)}) async-start(bf16[32,6,1024]{2,1,0:T(8,128)(2,1)} %bitcast.459), calls=%async_computation.2 | async-start | bytes 1048576 | tf_op jit(solution)/shard_map/all_to_all | solution.py:99
  216.6 98.1 %all-gather.17.cloned.1.call-start = ((), (), s32[]{:S(2)}) async-start(), calls=%async_computation.25 | async-start | bytes 2359296 | tf_op jit(solution)/shard_map/all_gather | solution.py:111
  236.9 7.4 collective-permute-start.5
  258.5 134.7 %reduce-scatter.14.cloned.1.call-start = ((), (), s32[]{:S(2)}) async-start(), calls=%async_computation.26 | async-start | bytes 2359296 | tf_op jit(solution)/shard_map/reduce_scatter | solution.py:115
  296.0 11.2 collective-permute-start.6
  310.4 18.9 %collective-permute-start.7 = (bf16[2,8,2,6,1024]{4,2,1,3,0:T(2,128)(2,1)}, bf16[2,8,2,6,1024]{4,2,1,3,0:T(2,128)(2,1)}, u32[]{:S(2)}, u32[]{:S(2)}) collective-permute-start(bf16[2,8,2,6,1024]{4,2,1,3,0:T(2,128)(2,1)} %get-tuple-element.83), channel_id=1, source_target_pairs={{0,2},{1,3},{2,0},{3,1},{4,6},{5,7},{6,4},{7,5},{8,10},{9,11},{10,... | collective-permute-start | bytes 1179656 | tf_op jit(solution)/shard_map/ppermute | solution.py:14
  346.2 10.3 collective-permute-start.8
  358.5 9.2 collective-permute-start.9
  368.9 19.6 %all-to-all-start.3 = ((bf16[32,6,1024]{2,1,0:T(8,128)(2,1)}), bf16[32,6,1024]{2,1,0:T(8,128)(2,1)}, u32[]{:S(2)}, u32[]{:S(2)}) async-start(bf16[32,6,1024]{2,1,0:T(8,128)(2,1)} %bitcast.457), calls=%async_computation.5 | async-start | bytes 1048576 | tf_op jit(solution)/shard_map/all_to_all | solution.py:99
  372.2 50.0 %all-gather.19.cloned.1.call-start = ((), (), s32[]{:S(2)}) async-start(), calls=%async_computation.27 | async-start | bytes 2359296 | tf_op jit(solution)/shard_map/all_gather | solution.py:111
  395.3 121.8 %reduce-scatter.16.cloned.1.call-start = ((), (), s32[]{:S(2)}) async-start(), calls=%async_computation.28 | async-start | bytes 2359296 | tf_op jit(solution)/shard_map/reduce_scatter | solution.py:115
  462.0 8.1 collective-permute-start.10
  483.0 7.6 collective-permute-start.11
  492.7 19.7 %all-to-all-start.5 = ((bf16[32,6,1024]{2,1,0:T(8,128)(2,1)}), bf16[32,6,1024]{2,1,0:T(8,128)(2,1)}, u32[]{:S(2)}, u32[]{:S(2)}) async-start(bf16[32,6,1024]{2,1,0:T(8,128)(2,1)} %bitcast.461), calls=%async_computation.8 | async-start | bytes 1048576 | tf_op jit(solution)/shard_map/all_to_all | solution.py:99
  496.2 89.0 %all-gather.21.cloned.1.call-start = ((), (), s32[]{:S(2)}) async-start(), calls=%async_computation.29 | async-start | bytes 2359296 | tf_op jit(solution)/shard_map/all_gather | solution.py:111
  535.7 7.3 collective-permute-start.12
  557.7 120.4 %reduce-scatter.18.cloned.1.call-start = ((), (), s32[]{:S(2)}) async-start(), calls=%async_computation.30 | async-start | bytes 2359296 | tf_op jit(solution)/shard_map/reduce_scatter | solution.py:115
  624.7 7.8 collective-permute-start.13
  643.5 7.4 collective-permute-start.14
  652.9 20.4 %all-to-all-start.7 = ((bf16[32,6,1024]{2,1,0:T(8,128)(2,1)}), bf16[32,6,1024]{2,1,0:T(8,128)(2,1)}, u32[]{:S(2)}, u32[]{:S(2)}) async-start(bf16[32,6,1024]{2,1,0:T(8,128)(2,1)} %bitcast.460), calls=%async_computation.11 | async-start | bytes 1048576 | tf_op jit(solution)/shard_map/all_to_all | solution.py:99
  657.1 80.2 %all-gather.23.cloned.1.call-start = ((), (), s32[]{:S(2)}) async-start(), calls=%async_computation.31 | async-start | bytes 2359296 | tf_op jit(solution)/shard_map/all_gather | solution.py:111
  682.5 139.7 %reduce-scatter.20.cloned.1.call-start = ((), (), s32[]{:S(2)}) async-start(), calls=%async_computation.32 | async-start | bytes 2359296 | tf_op jit(solution)/shard_map/reduce_scatter | solution.py:115
  718.5 11.0 collective-permute-start.15
  732.7 21.3 %collective-permute-start.16 = (bf16[2,8,2,6,1024]{4,2,1,3,0:T(2,128)(2,1)}, bf16[2,8,2,6,1024]{4,2,1,3,0:T(2,128)(2,1)}, u32[]{:S(2)}, u32[]{:S(2)}) collective-permute-start(bf16[2,8,2,6,1024]{4,2,1,3,0:T(2,128)(2,1)} %get-tuple-element.77), channel_id=1, source_target_pairs={{0,2},{1,3},{2,0},{3,1},{4,6},{5,7},{6,4},{7,5},{8,10},{9,11},{10,... | collective-permute-start | bytes 1179656 | tf_op jit(solution)/shard_map/ppermute | solution.py:14
  771.8 10.3 collective-permute-start.17
  785.6 9.4 collective-permute-start.18
  797.7 19.7 %all-to-all-start.9 = ((bf16[32,6,1024]{2,1,0:T(8,128)(2,1)}), bf16[32,6,1024]{2,1,0:T(8,128)(2,1)}, u32[]{:S(2)}, u32[]{:S(2)}) async-start(bf16[32,6,1024]{2,1,0:T(8,128)(2,1)} %bitcast.456), calls=%async_computation.14 | async-start | bytes 1048576 | tf_op jit(solution)/shard_map/all_to_all | solution.py:99
  801.2 87.3 %all-gather.25.cloned.1.call-start = ((), (), s32[]{:S(2)}) async-start(), calls=%async_computation.33 | async-start | bytes 2359296 | tf_op jit(solution)/shard_map/all_gather | solution.py:111
  849.4 125.9 %reduce-scatter.22.cloned.1.call-start = ((), (), s32[]{:S(2)}) async-start(), calls=%async_computation.34 | async-start | bytes 2359296 | tf_op jit(solution)/shard_map/reduce_scatter | solution.py:115
  887.0 11.3 collective-permute-start.20
  900.1 11.3 collective-permute-start.21
  924.7 13.6 %collective-permute-start.22 = (bf16[2,8,2,6,1024]{4,3,2,1,0:T(8,128)(2,1)}, bf16[2,8,2,6,1024]{4,3,2,1,0:T(8,128)(2,1)}, u32[]{:S(2)}, u32[]{:S(2)}) collective-permute-start(bf16[2,8,2,6,1024]{4,3,2,1,0:T(8,128)(2,1)} %convert_element_type.663), channel_id=1, source_target_pairs={{0,2},{1,3},{2,0},{3,1},{4,6},{5,7},{6,4},{7,5},{8,10},{9,11},{10,... | collective-permute-start | bytes 1179656 | tf_op jit(solution)/shard_map/ppermute | solution.py:14
  951.0 19.6 %all-to-all-start.11 = ((bf16[32,6,1024]{2,1,0:T(8,128)(2,1)}), bf16[32,6,1024]{2,1,0:T(8,128)(2,1)}, u32[]{:S(2)}, u32[]{:S(2)}) async-start(bf16[32,6,1024]{2,1,0:T(8,128)(2,1)} %bitcast.458), calls=%async_computation.17 | async-start | bytes 1048576 | tf_op jit(solution)/shard_map/all_to_all | solution.py:99
  954.4 93.0 %reduce-scatter.26.cloned.1.call-start = ((), (), s32[]{:S(2)}) async-start(), calls=%async_computation.36 | async-start | bytes 2359296 | tf_op jit(solution)/shard_map/reduce_scatter | solution.py:266
  985.3 105.0 %reduce-scatter.24.cloned.1.call-start = ((), (), s32[]{:S(2)}) async-start(), calls=%async_computation.35 | async-start | bytes 7077888 | tf_op jit(solution)/shard_map/reduce_scatter | solution.py:263
  1020.0 101.8 %reduce-scatter.28.cloned.1.call-start = ((), (), s32[]{:S(2)}) async-start(), calls=%async_computation.37 | async-start | bytes 294912
  1037.8 232.1 %all-reduce.11.cloned.1.call-start = ((), (), s32[]{:S(2)}) async-start(), calls=%async_computation.38 | async-start | bytes 12582912 | tf_op jit(solution)/shard_map/psum | solution.py:575
  1137.7 28.0 %collective-permute-start.24 = (bf16[128,1024]{1,0:T(8,128)(2,1)}, bf16[128,1024]{1,0:T(8,128)(2,1)S(1)}, u32[]{:S(2)}, u32[]{:S(2)}) collective-permute-start(bf16[128,1024]{1,0:T(8,128)(2,1)} %select_convert_fusion.10), channel_id=1, source_target_pairs={{0,2},{1,3},{2,0},{3,1},{4,6},{5,7},{6,4},{7,5},{8,10},{9,11},{10,... | collective-permute-start | bytes 786440 | tf_op jit(solution)/shard_map/ppermute | solution.py:14
  (214 other events, 2936.9 us)
Sparse Core Ops, SparseCore 0:
  10.3 67.4 all-gather.10
  79.9 27.7 all-gather.12
  111.6 40.2 all-gather.14
  159.3 34.8 reduce-scatter.11
  258.6 38.9 all-gather.16
  322.2 33.5 reduce-scatter.13
  395.5 26.7 all-gather.18
  431.0 40.3 reduce-scatter.15
  557.8 27.3 all-gather.20
  592.6 40.4 reduce-scatter.17
  682.6 38.5 all-gather.22
  746.1 33.1 reduce-scatter.19
  849.5 38.9 all-gather.24
  897.3 34.9 reduce-scatter.21
  985.4 33.7 reduce-scatter.25
  1022.0 68.3 reduce-scatter.23
  1092.4 29.3 reduce-scatter.27
  1127.8 142.0 all-reduce.10
where the time goes:
time: 1300 us; the launch traced here: 1290 us
  waiting for transfers between devices  481 us (37%)
  matrix products  241 us (19%)
  blocking collectives  204 us (16%)
  local copies, waits for them, and re-layouts  168 us (13%)
  other arithmetic  119 us (9%)
  starting transfers between devices  57.7 us (4%)
  between operations  19.5 us (2%)
    all_to_all x5, blocking collectives, dispatch(): lax.all_to_all(buffer, ('wide', 'narrow'), split_axis=0, concat_axis=0, t...  148 us
    ppermute x25, waiting for transfers between devices, from_partner(): lax.ppermute(array, axis, [(i, i ^ 1 << apart) for i in range(lax.axis_si...  110 us
    psum x1, waiting for transfers between devices, body(): lax.psum(shallow_side[1].astype(jnp.bfloat16), 'narrow').astype(jnp.float32)  102 us
    dot_general x23, matrix products, left_product(): lax.dot_general(former, latter, (((0,), (0,)), ((), ())), preferred_eleme...  95.1 us
    all_to_all x6, waiting for transfers between devices, combine(): lax.all_to_all(buffer, ('wide', 'narrow'), split_axis=0, concat_axis=0, t...  76 us
    dot_general x23, matrix products, right_product(): lax.dot_general(former, latter, (((1,), (1,)), ((), ())), preferred_eleme...  75.8 us
    all_gather x6, waiting for transfers between devices, wide_rows(): return lax.all_gather(value, 'wide', axis=0, tiled=True)  54.5 us
    all_gather x1, waiting for transfers between devices, gather_layer(): lax.all_gather(shortened(attention_in), 'wide', axis=0, tiled=True)  42.8 us
  transfers between devices with their start and end apart: 50, of which 33 were waited for; matrix products, arithmetic and copies ran while one was open for 30% of the time, Pallas kernels for 0%

commit v1 on v0

v1 whole, which is shorter than its diff:
```python
import jax
import jax.numpy as jnp
from jax import lax
from jax.experimental import pallas as pl
from jax.experimental.pallas import tpu as pltpu
from jax.sharding import PartitionSpec as P

HEAD_DIM = 64
SLICES_SHALLOW = 4
SLICES_DEEP = 2
F32 = jnp.float32
LOW = jnp.bfloat16
VMEM_LIMIT = 60 * 1024 * 1024


def low(value):
    return value.astype(LOW)


def swap(array, axis, distance):
    return lax.ppermute(array, axis, [(i, i ^ distance) for i in range(lax.axis_size(axis))])


def product(left, right, left_dim, right_dim):
    return lax.dot_general(
        left, right, (((left_dim,), (right_dim,)), ((), ())), preferred_element_type=F32
    )


def vmem():
    return pl.BlockSpec(memory_space=pltpu.VMEM)


def smem():
    return pl.BlockSpec(memory_space=pltpu.SMEM)


def call(kernel, outs, scalars, arrays, scratch=(), flops=0):
    moved = sum(a.size * a.dtype.itemsize for a in list(arrays) + list(outs))
    return pl.pallas_call(
        kernel,
        out_shape=tuple(outs),
        in_specs=[smem()] * len(scalars) + [vmem()] * len(arrays),
        out_specs=tuple(vmem() for _ in outs),
        scratch_shapes=list(scratch),
        compiler_params=pltpu.CompilerParams(vmem_limit_bytes=VMEM_LIMIT),
        cost_estimate=pl.CostEstimate(flops=flops, bytes_accessed=moved, transcendentals=0),
    )(*scalars, *arrays)


def shape(dims, kind):
    return jax.ShapeDtypeStruct(dims, kind)


def pack_rows(pieces, base):
    count, (rows, columns) = len(pieces), pieces[0].shape

    def kernel(base_ref, *refs):
        for k in range(count):
            start = pl.multiple_of((base_ref[0] ^ k) * rows, rows)
            refs[count][pl.ds(start, rows), :] = refs[k][...]

    outs = [shape((count * rows, columns), pieces[0].dtype)]
    return call(kernel, outs, [base], pieces)[0]


def join_rows(pieces):
    if len(pieces) == 1:
        return pieces[0]
    count, (rows, columns) = len(pieces), pieces[0].shape

    def kernel(*refs):
        for k in range(count):
            refs[count][k * rows : (k + 1) * rows, :] = refs[k][...]

    return call(kernel, [shape((count * rows, columns), pieces[0].dtype)], [], pieces)[0]


def pack_columns(pieces, base):
    count, (rows, columns) = len(pieces), pieces[0].shape

    def kernel(base_ref, *refs):
        for k in range(count):
            start = pl.multiple_of((base_ref[0] ^ k) * columns, columns)
            refs[count][:, pl.ds(start, columns)] = refs[k][...]

    return call(kernel, [shape((rows, count * columns), pieces[0].dtype)], [base], pieces)[0]


def split_columns(whole, count, base):
    rows, columns = whole.shape[0], whole.shape[1] // count

    def kernel(base_ref, whole_ref, *outs):
        for k in range(count):
            start = pl.multiple_of((base_ref[0] ^ k) * columns, columns)
            outs[k][...] = low(whole_ref[:, pl.ds(start, columns)])

    return call(kernel, [shape((rows, columns), LOW)] * count, [base], [whole])


def reversed_order(count):
    bits = count.bit_length() - 1
    return [sum((i >> b & 1) << (bits - 1 - b) for b in range(bits)) for i in range(count)]


def split_halves(whole, count, base):
    rows, columns = whole.shape[0] // count, whole.shape[1]
    order = reversed_order(count)

    def kernel(base_ref, whole_ref, keep_ref, send_ref):
        for i, k in enumerate(order):
            start = pl.multiple_of((base_ref[0] ^ k) * rows, rows)
            block = low(whole_ref[pl.ds(start, rows), :])
            out, at = (keep_ref, i) if i < count // 2 else (send_ref, i - count // 2)
            out[at * rows : (at + 1) * rows, :] = block

    return call(kernel, [shape((rows * count // 2, columns), LOW)] * 2, [base], [whole])


def scatter_halves(keep, send):
    distance = 1
    wide = lax.axis_size("wide")
    while True:
        total = keep.astype(F32) + swap(send, "wide", distance).astype(F32)
        distance *= 2
        if distance == wide:
            return total
        half = total.shape[0] // 2
        keep, send = total[:half], low(total[half:])


def narrow_sum(value, first):
    narrow = lax.axis_size("narrow")
    bits = narrow.bit_length() - 1
    for b in range(bits):
        value = value + swap(low(value), "narrow", 1 << (b + first) % bits).astype(F32)
    return value


def everywhere_sum(value):
    for axis in ("narrow", "wide"):
        distance = 1
        while distance < lax.axis_size(axis):
            value = value + swap(value, axis, distance)
            distance *= 2
    return value


def layer_norm(source, gain):
    centre = source - jnp.mean(source, axis=-1, keepdims=True)
    inverse = lax.rsqrt(jnp.mean(centre * centre, axis=-1, keepdims=True) + 1e-05)
    scaled = centre * inverse
    return scaled * gain, scaled, inverse


def norm_back(upstream, scaled, inverse, gain):
    grad_scaled = upstream * gain
    mean_first = jnp.mean(grad_scaled, axis=-1, keepdims=True)
    mean_second = jnp.mean(grad_scaled * scaled, axis=-1, keepdims=True)
    return (
        inverse * (grad_scaled - mean_first - scaled * mean_second),
        jnp.sum(upstream * scaled, axis=0),
    )


def activate(source):
    return jax.nn.gelu(source)


def activation_back(source, upstream):
    return jax.vjp(activate, source)[1](upstream)[0]


def softened_scores(queries, keys, allowed):
    scores = product(queries, keys, 1, 1) * HEAD_DIM ** (-0.5)
    scores = jnp.where(allowed, scores, -1e30)
    raised = jnp.exp(scores - jnp.max(scores, axis=-1, keepdims=True))
    return raised / jnp.sum(raised, axis=-1, keepdims=True)


def allowed_of(length, slots):
    rows_at = lax.broadcasted_iota(jnp.int32, (slots, slots), 0)
    cols_at = lax.broadcasted_iota(jnp.int32, (slots, slots), 1)
    return (cols_at <= rows_at) & (cols_at < length)


def head_parts(packed, head, columns):
    return [
        packed[:, part * columns + head * HEAD_DIM : part * columns + (head + 1) * HEAD_DIM]
        for part in range(3)
    ]


def attention(pieces, weight, lengths):
    count, (slots, features) = len(pieces), pieces[0].shape
    columns = weight.shape[1] // 3

    def kernel(lengths_ref, *refs):
        ins, weight_ref, packed_ref, outs = (
            refs[:count], refs[count], refs[count + 1], refs[count + 2 :],
        )
        for j in range(count):
            packed = low(product(ins[j][...], weight_ref[...], 1, 0))
            packed_ref[j] = packed
            allowed = allowed_of(lengths_ref[j], slots)
            found = []
            for head in range(columns // HEAD_DIM):
                queries, keys, values = head_parts(packed, head, columns)
                softened = softened_scores(queries, keys, allowed)
                found.append(product(low(softened), values, 1, 0))
            outs[j][...] = low(jnp.concatenate(found, axis=1))

    outs = [shape((count, slots, 3 * columns), LOW)] + [shape((slots, columns), LOW)] * count
    flops = 2 * count * slots * features * 3 * columns
    packed, *contexts = call(kernel, outs, [lengths], list(pieces) + [weight], flops=flops)
    return packed, contexts


def attention_back(pieces, weight, packed, grads, lengths):
    count, (slots, features) = len(pieces), pieces[0].shape
    columns = weight.shape[1] // 3
    scaling = HEAD_DIM ** (-0.5)

    def kernel(lengths_ref, *refs):
        ins, weight_ref, packed_ref = refs[:count], refs[count], refs[count + 1]
        grad_refs = refs[count + 2 : 2 * count + 2]
        total_ref, outs = refs[2 * count + 2], refs[2 * count + 3 :]
        for j in range(count):
            allowed = allowed_of(lengths_ref[j], slots)
            whole = packed_ref[j]
            grad_whole = grad_refs[j][...]
            found = [[], [], []]
            for head in range(columns // HEAD_DIM):
                queries, keys, values = head_parts(whole, head, columns)
                grad_head = grad_whole[:, head * HEAD_DIM : (head + 1) * HEAD_DIM]
                softened = softened_scores(queries, keys, allowed)
                grad_soft = product(grad_head, values, 1, 1)
                inner = jnp.sum(softened * grad_soft, axis=-1, keepdims=True)
                grad_scores = low(softened * (grad_soft - inner))
                found[0].append(scaling * product(grad_scores, keys, 1, 0))
                found[1].append(scaling * product(grad_scores, queries, 0, 0))
                found[2].append(product(low(softened), grad_head, 0, 0))
            grad_packed = low(jnp.concatenate(found[0] + found[1] + found[2], axis=1))
            added = product(ins[j][...], grad_packed, 0, 0)
            if j == 0:
                total_ref[...] = added
            else:
                total_ref[...] += added
            outs[j][...] = low(product(grad_packed, weight_ref[...], 1, 1))

    outs = [shape((features, 3 * columns), F32)] + [shape((slots, features), LOW)] * count
    flops = 4 * count * slots * features * 3 * columns
    arrays = list(pieces) + [weight, packed] + list(grads)
    total, *parts = call(kernel, outs, [lengths], arrays, flops=flops)
    return total, parts


def chunks_of(wide):
    return [list(range(0, wide, 2))]


def wide_pieces(own):
    across = [own]
    for apart in range(2, lax.axis_size("wide"), 2):
        across.append(swap(own, "wide", apart))
    return across, [swap(piece, "wide", 1) for piece in across]


def wide_join(across, beside, chunk):
    return join_rows([across[a // 2] for a in chunk] + [beside[a // 2] for a in chunk])


def chunk_order(chunk):
    return list(chunk) + [a + 1 for a in chunk]


def wide_sums(chunks, merged, slots):
    total = None
    for chunk, value in zip(chunks, merged):
        half = value.shape[0] // 2
        pair = value[:half] + swap(low(value[half:]), "wide", 1).astype(F32)
        for i, apart in enumerate(chunk):
            part = pair[i * slots : (i + 1) * slots]
            if apart:
                part = swap(low(part), "wide", apart).astype(F32)
            total = part if total is None else total + part
    return total


def place(labels, experts, capacity):
    places = jnp.arange(capacity, dtype=jnp.int32)
    selects = []
    for expert in experts:
        chosen = labels == expert
        rank = jnp.where(chosen, jnp.cumsum(chosen.astype(jnp.int32), axis=1) - 1, -1)
        selects.append(low(rank[:, None, :] == places[None, :, None]))
    return selects


def to_experts(selects, rows, slices):
    features = rows.shape[-1]
    blocks, capacity, slots = selects[0].shape
    rows = rows.reshape(blocks, slots, features)
    sent = [
        low(
            lax.dot_general(s, rows, (((2,), (1,)), ((0,), (0,))), preferred_element_type=F32)
        ).reshape(blocks * capacity, features)
        for s in selects
    ]
    narrow = lax.axis_size("narrow")
    return join_rows(
        [sent[j // slices] if j == 0 else swap(sent[j // slices], "narrow", j) for j in range(narrow)]
    )


def from_experts(selects, outcome, slices):
    blocks, capacity, slots = selects[0].shape
    narrow = lax.axis_size("narrow")
    features = outcome.shape[-1]
    parts = outcome.reshape(narrow, blocks * capacity, features)
    spread = None
    for r, select in enumerate(selects):
        total = None
        for j in range(r * slices, (r + 1) * slices):
            part = parts[j] if j == 0 else swap(low(parts[j]), "narrow", j).astype(F32)
            total = part if total is None else total + part
        rows = low(total).reshape(blocks, capacity, features)
        part = lax.dot_general(
            select, rows, (((1,), (1,)), ((0,), (0,))), preferred_element_type=F32
        )
        spread = part if spread is None else spread + part
    return spread.reshape(-1, features)


def layer_forward(source, weights, selects, lengths, at_narrow, slices):
    norm_first, attention_in, attention_out, norm_second, mixer, up, down, expert_up, expert_down = weights
    slots, features = source.shape
    wide, narrow = lax.axis_size("wide"), lax.axis_size("narrow")
    normed, scaled_one, inverse_one = layer_norm(source, norm_first)
    normed_low = low(normed)
    pieces = [normed_low] + [swap(normed_low, "narrow", j) for j in range(1, narrow)]
    packed, contexts = attention(pieces, attention_in, lengths)
    context = pack_columns(
        [contexts[0]] + [swap(contexts[j], "narrow", j) for j in range(1, narrow)], at_narrow
    )
    middle = source + jnp.dot(context, attention_out, preferred_element_type=F32)
    second, scaled_two, inverse_two = layer_norm(middle, norm_second)
    across, beside = wide_pieces(low(second))
    chunks = chunks_of(wide)
    merged, kept_chunks = [], []
    for chunk, select in zip(chunks, selects):
        rows = wide_join(across, beside, chunk)
        mixing = jax.nn.softmax(jnp.dot(rows, mixer, preferred_element_type=F32), axis=-1)
        expert_rows = to_experts(select, rows, slices)
        expert_pre = jnp.dot(expert_rows, expert_up, preferred_element_type=F32)
        expert_act = low(activate(expert_pre))
        outcome = jnp.dot(expert_act, expert_down, preferred_element_type=F32)
        pre = jnp.dot(rows, up, preferred_element_type=F32)
        act = low(activate(pre))
        dense = jnp.dot(act, down, preferred_element_type=F32)
        spread = from_experts(select, outcome, slices)
        merged.append(mixing[:, :1] * dense + mixing[:, 1:] * spread)
        kept_chunks.append((rows, mixing, expert_rows, expert_pre, expert_act, pre, act))
    output = middle + wide_sums(chunks, merged, slots)
    kept = (scaled_one, inverse_one, pieces, packed, context, scaled_two, inverse_two, kept_chunks)
    return output, kept


def layer_backward(upstream, kept, weights, selects, lengths, at_narrow, at_wide, slices):
    norm_first, attention_in, attention_out, norm_second, mixer, up, down, expert_up, expert_down = weights
    scaled_one, inverse_one, pieces, packed, context, scaled_two, inverse_two, kept_chunks = kept
    slots, features = upstream.shape
    wide, narrow = lax.axis_size("wide"), lax.axis_size("narrow")
    mixer_gap = (mixer[:, 0].astype(F32) - mixer[:, 1].astype(F32))[None]
    across, beside = wide_pieces(low(upstream))
    chunks = chunks_of(wide)
    merged, sums = [], []
    for chunk, select, saved in zip(chunks, selects, kept_chunks):
        rows, mixing, expert_rows, expert_pre, expert_act, pre, act = saved
        grads = wide_join(across, beside, chunk)
        expert_grads = to_experts(select, grads, slices)
        expert_mixing = jax.nn.softmax(
            jnp.dot(expert_rows, mixer, preferred_element_type=F32), axis=-1
        )
        through = product(expert_grads, expert_down, 1, 1)
        expert_dot = jnp.sum(expert_act.astype(F32) * through, axis=1, keepdims=True)
        expert_logit = -expert_mixing[:, :1] * expert_mixing[:, 1:] * expert_dot
        expert_grad_pre = low(activation_back(expert_pre, expert_mixing[:, 1:] * through))
        expert_back = product(expert_grad_pre, expert_up, 1, 1) + expert_logit * mixer_gap
        through = product(grads, down, 1, 1)
        dense_dot = jnp.sum(act.astype(F32) * through, axis=1, keepdims=True)
        dense_logit = mixing[:, :1] * mixing[:, 1:] * dense_dot
        grad_pre = low(activation_back(pre, mixing[:, :1] * through))
        dense_back = product(grad_pre, up, 1, 1) + dense_logit * mixer_gap
        merged.append(dense_back + from_experts(select, expert_back, slices))
        sums.append(
            (
                product(rows, grad_pre, 0, 0),
                product(act, low(mixing[:, :1] * grads.astype(F32)), 0, 0),
                product(expert_rows, expert_grad_pre, 0, 0),
                product(expert_act, low(expert_mixing[:, 1:] * expert_grads.astype(F32)), 0, 0),
                jnp.sum(rows.astype(F32) * dense_logit, axis=0)
                + jnp.sum(expert_rows.astype(F32) * expert_logit, axis=0),
            )
        )
    grad_second = wide_sums(chunks, merged, slots)
    grad_up, grad_down, grad_expert_up, grad_expert_down, grad_gap = [sum(s[1:], s[0]) for s in zip(*sums)]
    grad_up = narrow_sum(grad_up, 0)
    grad_down = narrow_sum(grad_down, 1)
    grad_norm_part, grad_norm_second = norm_back(grad_second, scaled_two, inverse_two, norm_second)
    grad_middle = upstream + grad_norm_part
    grad_attended = low(grad_middle)
    grad_contexts = split_columns(product(grad_attended, attention_out, 1, 1), narrow, at_narrow)
    grad_contexts = [grad_contexts[0]] + [
        swap(grad_contexts[j], "narrow", j) for j in range(1, narrow)
    ]
    grad_out = product(context, grad_attended, 0, 0)
    grad_out = narrow_sum(scatter_halves(*split_halves(grad_out, wide, at_wide)), 0)
    grad_in, parts = attention_back(pieces, attention_in, packed, grad_contexts, lengths)
    grad_in = low(scatter_halves(*split_halves(grad_in, wide, at_wide)))
    grad_in = pack_rows(
        [grad_in] + [swap(grad_in, "narrow", j) for j in range(1, narrow)], at_narrow
    )
    grad_in = jnp.transpose(grad_in.reshape(narrow, features // wide, 3, -1), (1, 2, 0, 3))
    grad_in = grad_in.reshape(features // wide, -1).astype(F32)
    grad_normed = parts[0].astype(F32)
    for j in range(1, narrow):
        grad_normed = grad_normed + swap(parts[j], "narrow", j).astype(F32)
    grad_norm_part, grad_norm_first = norm_back(grad_normed, scaled_one, inverse_one, norm_first)
    return grad_middle + grad_norm_part, (
        grad_in, grad_out, grad_up, grad_down, grad_expert_up[None], grad_expert_down[None],
        grad_norm_first, grad_norm_second, grad_gap,
    )


def narrow_slice(attention_in):
    rows, triple = attention_in.shape
    narrow = lax.axis_size("narrow")
    split = attention_in.reshape(rows, 3, narrow, triple // (3 * narrow))
    own = lax.dynamic_index_in_dim(split, lax.axis_index("narrow"), axis=2, keepdims=False)
    return own.reshape(rows, -1)


def gather_wide(own, at_wide):
    across, beside = wide_pieces(own)
    return pack_rows([p for pair in zip(across, beside) for p in pair], at_wide)


def body(
    inputs, cotangent, seq_len, shallow_routes, deep_routes,
    shallow_norm_first, shallow_attention_in, shallow_attention_out, shallow_norm_second,
    shallow_dense_up, shallow_dense_down, shallow_mixer, shallow_expert_up, shallow_expert_down,
    deep_norm_first, deep_attention_in, deep_attention_out, deep_norm_second,
    deep_dense_up, deep_dense_down, deep_mixer, deep_expert_up, deep_expert_down,
):
    wide, narrow = lax.axis_size("wide"), lax.axis_size("narrow")
    wide_at, narrow_at = lax.axis_index("wide"), lax.axis_index("narrow")
    at_wide, at_narrow = wide_at.reshape(1), narrow_at.reshape(1)
    slots, features = inputs.shape
    small = jnp.stack(
        [
            shallow_norm_first, shallow_norm_second, deep_norm_first, deep_norm_second,
            shallow_mixer[:, 0], shallow_mixer[:, 1], deep_mixer[:, 0], deep_mixer[:, 1],
        ]
    )
    small = jnp.transpose(gather_wide(small, at_wide).reshape(wide, 8, -1), (1, 0, 2)).reshape(8, features)
    gains = small[:4].astype(F32)
    lengths = seq_len[wide_at * narrow + (narrow_at ^ jnp.arange(narrow))]

    def selects_of(routes, slices):
        table = routes.reshape(wide, narrow, slots)
        own = lax.dynamic_index_in_dim(table, narrow_at, axis=1, keepdims=False)
        capacity = slices * max(1, 3 * slots // (2 * wide * narrow))
        groups = narrow // slices
        experts = [wide_at * groups + ((narrow_at // slices) ^ r) for r in range(groups)]
        return [
            place(own[wide_at ^ jnp.array(chunk_order(chunk))], experts, capacity)
            for chunk in chunks_of(wide)
        ]

    shallow_selects = selects_of(shallow_routes, SLICES_SHALLOW)
    deep_selects = selects_of(deep_routes, SLICES_DEEP)
    shallow = (
        gains[0], gather_wide(narrow_slice(shallow_attention_in), at_wide),
        gather_wide(shallow_attention_out, at_wide), gains[1], small[4:6].T,
        shallow_dense_up, shallow_dense_down, shallow_expert_up[0], shallow_expert_down[0],
    )
    deep = (
        gains[2], gather_wide(narrow_slice(deep_attention_in), at_wide),
        gather_wide(deep_attention_out, at_wide), gains[3], small[6:8].T,
        deep_dense_up, deep_dense_down, deep_expert_up[0], deep_expert_down[0],
    )
    passed, kept_shallow = layer_forward(
        inputs.astype(F32), shallow, shallow_selects, lengths, at_narrow, SLICES_SHALLOW
    )
    output, kept_deep = layer_forward(passed, deep, deep_selects, lengths, at_narrow, SLICES_DEEP)
    grad_passed, grads_deep = layer_backward(
        cotangent.astype(F32), kept_deep, deep, deep_selects, lengths, at_narrow, at_wide, SLICES_DEEP
    )
    grad_inputs, grads_shallow = layer_backward(
        grad_passed, kept_shallow, shallow, shallow_selects, lengths, at_narrow, at_wide, SLICES_SHALLOW
    )
    vectors = everywhere_sum(
        jnp.stack(list(grads_shallow[6:9]) + list(grads_deep[6:9]))
    )
    vectors = lax.dynamic_slice_in_dim(vectors, wide_at * (features // wide), features // wide, axis=1)

    def outputs_of(grads, rows):
        grad_mixer = jnp.stack([rows[2], -rows[2]], axis=1)
        return (
            rows[0], grads[0], grads[1], rows[1], grads[2], grads[3], grad_mixer, grads[4], grads[5],
        )

    return (
        (low(output), grad_inputs)
        + outputs_of(grads_shallow, vectors[:3])
        + outputs_of(grads_deep, vectors[3:])
    )


def solution(mesh):
    both = ("wide", "narrow")
    parameters = (
        P("wide"), P("wide", None), P("wide", None), P("wide"), P(None, "wide"),
        P("wide", None), P("wide", None), P(both, None, None), P(both, None, None),
    )
    return jax.shard_map(
        body,
        mesh=mesh,
        in_specs=(P(both, None), P(both, None), P(), P(), P()) + parameters + parameters,
        out_specs=(P(both, None), P(both, None)) + parameters + parameters,
        check_vma=False,
    )
```

time: 1300 us -> 835 us (0.64)
  blocking collectives: 204 us -> 0 us
  waiting for transfers between devices: 481 us -> 305 us
  matrix products: 241 us -> 110 us
  Pallas kernels: 0 us -> 106 us
  starting transfers between devices: 57.7 us -> 148 us
  local copies, waits for them, and re-layouts: 168 us -> 78.4 us
  other arithmetic: 119 us -> 74.3 us
  between operations: 19.5 us -> 3.09 us
    ppermute x25 -> x162, waiting for transfers between devices: 110 us -> 305 us  [swap(): lax.ppermute(array, axis, [(i, i ^ distance) for i in range(lax.axis_size...]
    all_to_all x5 -> x0, blocking collectives: 148 us -> none  [dispatch(): lax.all_to_all(buffer, ('wide', 'narrow'), split_axis=0, concat_axis=0, t...]
    dot_general x88 -> x46, matrix products: 241 us -> 110 us  [the longest x20 64.5 us: product(): lax.dot_general(left, right, (((left_dim,), (right_dim,)), ((), ())), pre...]
    all_gather x8 -> x0, waiting for transfers between devices: 121 us -> none  [the longest x6 54.5 us: wide_rows(): return lax.all_gather(value, 'wide', axis=0, tiled=True)]
    ppermute x25 -> x162, starting transfers between devices: 29.9 us -> 148 us  [swap(): lax.ppermute(array, axis, [(i, i ^ distance) for i in range(lax.axis_size...]
    pallas_call x0 -> x27, Pallas kernels: none -> 106 us  [call(): pl.pallas_call(kernel, out_shape=tuple(outs), in_specs=[smem()] * len(sca...]
    psum x1 -> x0, waiting for transfers between devices: 102 us -> none  [body(): lax.psum(shallow_side[1].astype(jnp.bfloat16), 'narrow').astype(jnp.float32)]
    all_to_all x7 -> x0, waiting for transfers between devices: 101 us -> none  [the longest x6 76 us: combine(): lax.all_to_all(buffer, ('wide', 'narrow'), split_axis=0, concat_axis=0, t...]
  transfers between devices with their start and end apart: 50 -> 162, of which waited for: 33 -> 59; matrix products, arithmetic and copies ran while one was open for 30% -> 25% of each run, Pallas kernels for 0% -> 11%
where the time goes in v1:
time: 835 us; the launch traced here: 824 us
  waiting for transfers between devices  305 us (37%)
  starting transfers between devices  148 us (18%)
  matrix products  110 us (13%)
  Pallas kernels  106 us (13%)
  local copies, waits for them, and re-layouts  78.4 us (9%)
  other arithmetic  74.3 us (9%)
    ppermute x162, waiting for transfers between devices, swap(): lax.ppermute(array, axis, [(i, i ^ distance) for i in range(lax.axis_size...  305 us
    ppermute x162, starting transfers between devices, swap(): lax.ppermute(array, axis, [(i, i ^ distance) for i in range(lax.axis_size...  148 us
    pallas_call x27, Pallas kernels, call(): pl.pallas_call(kernel, out_shape=tuple(outs), in_specs=[smem()] * len(sca...  106 us
    dot_general x20, matrix products, product(): lax.dot_general(left, right, (((left_dim,), (right_dim,)), ((), ())), pre...  64.5 us
    unnamed x326, local copies, waits for them, and re-layouts  38.5 us
    convert_element_type x23, other arithmetic, low(): return value.astype(LOW)  30.6 us
    add x6, other arithmetic, narrow_sum(): value + swap(low(value), 'narrow', 1 << (b + first) % bits).astype(F32)  17.9 us
  transfers between devices with their start and end apart: 162, of which 59 were waited for; matrix products, arithmetic and copies ran while one was open for 25% of the time, Pallas kernels for 11%

profile of v1, /device:TPU:0, one launch (start us, length us, event | category | flops | bytes accessed | tf_op | source)
XLA Modules:
  0.0 823.9 jit_solution(5118981010049781513)
XLA Ops:
  2.3 5.1 collective-permute-start.5
  13.9 3.8 collective-permute-start.15
  24.6 16.2 %collective-permute-done.13.refs_4_ = bf16[128,768]{1,0:T(8,128)(2,1)S(1)} collective-permute-done((bf16[128,768]{1,0:T(8,128)(2,1)S(1)}, bf16[128,768]{1,0:T(8,128)(2,1)S(1)}, u32[]{:S(2)}, u32[]{:S(2)}) %collective-permute-start.13) | collective-permute-done | bytes 196640 | tf_op jit(solution)/shard_map/ppermute | solution.py:21
  42.3 3.8 collective-permute-done.23.refs_4_
  59.6 3.9 collective-permute-done.8.refs_2_
  63.6 8.0 shard_map.394
  100.6 5.2 collective-permute-done.29.refs_3_
  105.7 9.6 %collective-permute-done.28.refs_2_ = bf16[128,1024]{1,0:T(8,128)(2,1)} collective-permute-done((bf16[128,1024]{1,0:T(8,128)(2,1)S(1)}, bf16[128,1024]{1,0:T(8,128)(2,1)}, u32[]{:S(2)}, u32[]{:S(2)}) %collective-permute-start.28) | collective-permute-done | bytes 262176 | tf_op jit(solution)/shard_map/ppermute | solution.py:21
  127.0 8.7 %collective-permute-done.36.refs_3_ = bf16[192,1024]{1,0:T(8,128)(2,1)S(1)} collective-permute-done((bf16[192,1024]{1,0:T(8,128)(2,1)S(1)}, bf16[192,1024]{1,0:T(8,128)(2,1)S(1)}, u32[]{:S(2)}, u32[]{:S(2)}) %collective-permute-start.36) | collective-permute-done | bytes 393248 | tf_op jit(solution)/shard_map/ppermute | solution.py:21
  135.7 7.6 collective-permute-done.35.refs_2_
  146.6 3.9 fusion.46
  159.6 7.1 collective-permute-done.37
  166.8 8.5 %collective-permute-done.39 = bf16[192,1024]{1,0:T(8,128)(2,1)S(1)} collective-permute-done((bf16[192,1024]{1,0:T(8,128)(2,1)S(1)}, bf16[192,1024]{1,0:T(8,128)(2,1)S(1)}, u32[]{:S(2)}, u32[]{:S(2)}) %collective-permute-start.39) | collective-permute-done | bytes 393248 | tf_op jit(solution)/shard_map/ppermute | solution.py:21
  193.2 5.8 collective-permute-start.82
  199.0 15.0 %collective-permute-done.50.refs_4_ = bf16[128,768]{1,0:T(8,128)(2,1)} collective-permute-done((bf16[128,768]{1,0:T(8,128)(2,1)S(1)}, bf16[128,768]{1,0:T(8,128)(2,1)}, u32[]{:S(2)}, u32[]{:S(2)}) %collective-permute-start.50) | collective-permute-done | bytes 196640 | tf_op jit(solution)/shard_map/ppermute | solution.py:21
  214.6 3.8 fusion.163
  218.9 5.9 collective-permute-done.82.refs_2_
  243.6 23.8 %collective-permute-done.42 = bf16[128,1024]{1,0:T(8,128)(2,1)S(1)} collective-permute-done((bf16[128,1024]{1,0:T(8,128)(2,1)}, bf16[128,1024]{1,0:T(8,128)(2,1)S(1)}, u32[]{:S(2)}, u32[]{:S(2)}) %collective-permute-start.42) | collective-permute-done | bytes 262176 | tf_op jit(solution)/shard_map/ppermute | solution.py:21
  275.8 5.3 collective-permute-done.46.refs_3_
  288.4 8.2 shard_map.400
  313.3 4.3 collective-permute-start.64
  318.2 6.1 collective-permute-done.66.refs_3_
  324.3 10.7 %collective-permute-done.65.refs_2_ = bf16[128,1024]{1,0:T(8,128)(2,1)S(1)} collective-permute-done((bf16[128,1024]{1,0:T(8,128)(2,1)S(1)}, bf16[128,1024]{1,0:T(8,128)(2,1)S(1)}, u32[]{:S(2)}, u32[]{:S(2)}) %collective-permute-start.65) | collective-permute-done | bytes 262176 | tf_op jit(solution)/shard_map/ppermute | solution.py:21
  369.1 4.6 fusion.7
  382.5 6.1 convolution_bitcast_fusion
  391.4 5.8 convolution_bitcast_fusion.1
  437.9 5.0 collective-permute-done.95
  442.9 6.3 collective-permute-done.97
  450.4 19.2 %collective-permute-done.96 = bf16[128,1024]{1,0:T(8,128)(2,1)S(1)} collective-permute-done((bf16[128,1024]{1,0:T(8,128)(2,1)S(1)}, bf16[128,1024]{1,0:T(8,128)(2,1)S(1)}, u32[]{:S(2)}, u32[]{:S(2)}) %collective-permute-start.96) | collective-permute-done | bytes 262176 | tf_op jit(solution)/shard_map/ppermute | solution.py:21
  470.1 11.9 %collective-permute-done.79 = bf16[128,1024]{1,0:T(8,128)(2,1)S(1)} collective-permute-done((bf16[128,1024]{1,0:T(8,128)(2,1)S(1)}, bf16[128,1024]{1,0:T(8,128)(2,1)S(1)}, u32[]{:S(2)}, u32[]{:S(2)}) %collective-permute-start.79) | collective-permute-done | bytes 262176 | tf_op jit(solution)/shard_map/ppermute | solution.py:21
  494.6 14.9 %shard_map.408 = (f32[1024,768]{1,0:T(8,128)}, bf16[128,1024]{1,0:T(8,128)(2,1)}, bf16[128,1024]{1,0:T(8,128)(2,1)}, bf16[128,1024]{1,0:T(8,128)(2,1)}, bf16[128,1024]{1,0:T(8,128)(2,1)}) custom-call(s32[4]{0:T(128)} %gather_fusion, bf16[128,1024]{1,0:T(8,128)(2,1)} %multiply_convert_fusion.13.refs_0_, bf16[128,1024]{1,0:T(8,128)(2,1)} %collective-permute-done.44.refs_1_, ...), custom_call_target="tpu_custom_call" | custom-call | flops 1610612736 | bytes 7864320 | tf_op jit(solution)/shard_map/pallas_call | solution.py:40
  522.8 4.8 collective-permute-done.102
  541.2 10.4 %collective-permute-done.105.refs_2_ = bf16[128,1024]{1,0:T(8,128)(2,1)S(1)} collective-permute-done((bf16[128,1024]{1,0:T(8,128)(2,1)S(1)}, bf16[128,1024]{1,0:T(8,128)(2,1)S(1)}, u32[]{:S(2)}, u32[]{:S(2)}) %collective-permute-start.105) | collective-permute-done | bytes 262176 | tf_op jit(solution)/shard_map/ppermute | solution.py:21
  566.5 4.6 multiply_reduce_fusion.5
  591.8 4.8 multiply_reduce_fusion.3
  596.7 4.7 convolution_bitcast_fusion.2
  613.8 4.1 collective-permute-done.114
  618.7 8.1 collective-permute-done.116
  636.4 3.9 convolution_bitcast_fusion.3
  684.4 9.1 %collective-permute-done.119 = bf16[128,1024]{1,0:T(8,128)(2,1)S(1)} collective-permute-done((bf16[128,1024]{1,0:T(8,128)(2,1)S(1)}, bf16[128,1024]{1,0:T(8,128)(2,1)S(1)}, u32[]{:S(2)}, u32[]{:S(2)}) %collective-permute-start.119) | collective-permute-done | bytes 262176 | tf_op jit(solution)/shard_map/ppermute | solution.py:21
  706.6 15.0 %shard_map.412 = (f32[1024,768]{1,0:T(8,128)}, bf16[128,1024]{1,0:T(8,128)(2,1)}, bf16[128,1024]{1,0:T(8,128)(2,1)}, bf16[128,1024]{1,0:T(8,128)(2,1)}, bf16[128,1024]{1,0:T(8,128)(2,1)}) custom-call(s32[4]{0:T(128)} %gather_fusion, bf16[128,1024]{1,0:T(8,128)(2,1)} %fusion.72.refs_0_, bf16[128,1024]{1,0:T(8,128)(2,1)} %collective-permute-done.7.refs_1_, ...), custom_call_target="tpu_custom_call" | custom-call | flops 1610612736 | bytes 7864320 | tf_op jit(solution)/shard_map/pallas_call | solution.py:40
  727.9 3.8 shard_map.415
  735.7 3.9 convert_add_fusion.7
  750.0 3.9 collective-permute-done.130
  759.1 10.2 %collective-permute-done.139 = bf16[256,1024]{1,0:T(8,128)(2,1)S(1)} collective-permute-done((bf16[256,1024]{1,0:T(8,128)(2,1)S(1)}, bf16[256,1024]{1,0:T(8,128)(2,1)S(1)}, u32[]{:S(2)}, u32[]{:S(2)}) %collective-permute-start.139) | collective-permute-done | bytes 524320 | tf_op jit(solution)/shard_map/ppermute | solution.py:21
  773.0 9.7 %collective-permute-done.140 = bf16[128,1024]{1,0:T(8,128)(2,1)S(1)} collective-permute-done((bf16[128,1024]{1,0:T(8,128)(2,1)S(1)}, bf16[128,1024]{1,0:T(8,128)(2,1)S(1)}, u32[]{:S(2)}, u32[]{:S(2)}) %collective-permute-start.140) | collective-permute-done | bytes 262176 | tf_op jit(solution)/shard_map/ppermute | solution.py:21
  786.4 4.6 collective-permute-done.141
  803.2 4.6 collective-permute-done.136.refs_2_
  (835 shorter events, 456.5 us)
Async XLA Ops:
  19.0 21.9 %collective-permute-start.13 = (bf16[128,768]{1,0:T(8,128)(2,1)S(1)}, bf16[128,768]{1,0:T(8,128)(2,1)S(1)}, u32[]{:S(2)}, u32[]{:S(2)}) collective-permute-start(bf16[128,768]{1,0:T(8,128)(2,1)S(1)} %copy.76.refs_0_), channel_id=1, source_target_pairs={{0,16},{4,20},{8,24},{12,28},{16,0},{20,4},{24,8},{28,12},{1,17},{... | collective-permute-start | bytes 589832 | tf_op jit(solution)/shard_map/ppermute | solution.py:21
  19.3 21.5 %collective-permute-start.11 = (bf16[128,768]{1,0:T(8,128)(2,1)S(1)}, bf16[128,768]{1,0:T(8,128)(2,1)S(1)}, u32[]{:S(2)}, u32[]{:S(2)}) collective-permute-start(bf16[128,768]{1,0:T(8,128)(2,1)S(1)} %copy.76.refs_0_), channel_id=1, source_target_pairs={{0,8},{4,12},{8,0},{12,4},{16,24},{20,28},{24,16},{28,20},{1,9},{5... | collective-permute-start | bytes 589832 | tf_op jit(solution)/shard_map/ppermute | solution.py:21
  19.9 22.4 %collective-permute-start.10 = (bf16[128,768]{1,0:T(8,128)(2,1)S(1)}, bf16[128,768]{1,0:T(8,128)(2,1)}, u32[]{:S(2)}, u32[]{:S(2)}) collective-permute-start(bf16[128,768]{1,0:T(8,128)(2,1)S(1)} %copy.76.refs_0_), channel_id=1, source_target_pairs={{0,4},{4,0},{8,12},{12,8},{16,20},{20,16},{24,28},{28,24},{1,5},{5... | collective-permute-start | bytes 589832 | tf_op jit(solution)/shard_map/ppermute | solution.py:21
  19.9 26.2 %collective-permute-start.23 = (bf16[128,1024]{1,0:T(8,128)(2,1)S(1)}, bf16[128,1024]{1,0:T(8,128)(2,1)S(1)}, u32[]{:S(2)}, u32[]{:S(2)}) collective-permute-start(bf16[128,1024]{1,0:T(8,128)(2,1)S(1)} %copy-done.73), channel_id=1, source_target_pairs={{0,16},{4,20},{8,24},{12,28},{16,0},{20,4},{24,8},{28,12},{1,17},{... | collective-permute-start | bytes 786440 | tf_op jit(solution)/shard_map/ppermute | solution.py:21
  24.4 24.8 %collective-permute-start.16 = (bf16[128,768]{1,0:T(8,128)(2,1)S(1)}, bf16[128,768]{1,0:T(8,128)(2,1)S(1)}, u32[]{:S(2)}, u32[]{:S(2)}) collective-permute-start(bf16[128,768]{1,0:T(8,128)(2,1)S(1)} %collective-permute-done.15.refs_6_), channel_id=1, source_target_pairs={{0,4},{4,0},{8,12},{12,8},{16,20},{20,16},{24,28},{28,24},{1,5},{5... | collective-permute-start | bytes 589832 | tf_op jit(solution)/shard_map/ppermute | solution.py:21
  57.5 30.9 %collective-permute-start.20 = (bf16[128,1024]{1,0:T(8,128)(2,1)S(1)}, bf16[128,1024]{1,0:T(8,128)(2,1)S(1)}, u32[]{:S(2)}, u32[]{:S(2)}) collective-permute-start(bf16[128,1024]{1,0:T(8,128)(2,1)S(1)} %copy-done.73), channel_id=1, source_target_pairs={{0,4},{4,0},{8,12},{12,8},{16,20},{20,16},{24,28},{28,24},{1,5},{5... | collective-permute-start | bytes 786440 | tf_op jit(solution)/shard_map/ppermute | solution.py:21
  57.6 30.9 %collective-permute-start.24 = (bf16[128,1024]{1,0:T(8,128)(2,1)S(1)}, bf16[128,1024]{1,0:T(8,128)(2,1)S(1)}, u32[]{:S(2)}, u32[]{:S(2)}) collective-permute-start(bf16[128,1024]{1,0:T(8,128)(2,1)S(1)} %copy-done.76), channel_id=1, source_target_pairs={{0,4},{4,0},{8,12},{12,8},{16,20},{20,16},{24,28},{28,24},{1,5},{5... | collective-permute-start | bytes 786440 | tf_op jit(solution)/shard_map/ppermute | solution.py:21
  59.6 28.8 %collective-permute-start.22 = (bf16[128,1024]{1,0:T(8,128)(2,1)}, bf16[128,1024]{1,0:T(8,128)(2,1)}, u32[]{:S(2)}, u32[]{:S(2)}) collective-permute-start(bf16[128,1024]{1,0:T(8,128)(2,1)} %collective-permute-done.21.refs_2_), channel_id=1, source_target_pairs={{0,4},{4,0},{8,12},{12,8},{16,20},{20,16},{24,28},{28,24},{1,5},{5... | collective-permute-start | bytes 786440 | tf_op jit(solution)/shard_map/ppermute | solution.py:21
  63.5 25.0 %collective-permute-start.26 = (bf16[128,1024]{1,0:T(8,128)(2,1)}, bf16[128,1024]{1,0:T(8,128)(2,1)}, u32[]{:S(2)}, u32[]{:S(2)}) collective-permute-start(bf16[128,1024]{1,0:T(8,128)(2,1)} %collective-permute-done.25.refs_6_), channel_id=1, source_target_pairs={{0,4},{4,0},{8,12},{12,8},{16,20},{20,16},{24,28},{28,24},{1,5},{5... | collective-permute-start | bytes 786440 | tf_op jit(solution)/shard_map/ppermute | solution.py:21
  183.1 31.4 %collective-permute-start.40 = (bf16[512,1024]{1,0:T(8,128)(2,1)}, bf16[512,1024]{1,0:T(8,128)(2,1)}, u32[]{:S(2)}, u32[]{:S(2)}) collective-permute-start(bf16[512,1024]{1,0:T(8,128)(2,1)} %slice.664), channel_id=1, source_target_pairs={{0,4},{4,0},{8,12},{12,8},{16,20},{20,16},{24,28},{28,24},{1,5},{5... | collective-permute-start | bytes 3145736 | tf_op jit(solution)/shard_map/ppermute | solution.py:21
  185.7 28.3 %collective-permute-start.50 = (bf16[128,768]{1,0:T(8,128)(2,1)S(1)}, bf16[128,768]{1,0:T(8,128)(2,1)}, u32[]{:S(2)}, u32[]{:S(2)}) collective-permute-start(bf16[128,768]{1,0:T(8,128)(2,1)S(1)} %copy.84.refs_0_), channel_id=1, source_target_pairs={{0,16},{4,20},{8,24},{12,28},{16,0},{20,4},{24,8},{28,12},{1,17},{... | collective-permute-start | bytes 589832 | tf_op jit(solution)/shard_map/ppermute | solution.py:21
  185.7 28.3 %collective-permute-start.48 = (bf16[128,768]{1,0:T(8,128)(2,1)S(1)}, bf16[128,768]{1,0:T(8,128)(2,1)}, u32[]{:S(2)}, u32[]{:S(2)}) collective-permute-start(bf16[128,768]{1,0:T(8,128)(2,1)S(1)} %copy.84.refs_0_), channel_id=1, source_target_pairs={{0,8},{4,12},{8,0},{12,4},{16,24},{20,28},{24,16},{28,20},{1,9},{5... | collective-permute-start | bytes 589832 | tf_op jit(solution)/shard_map/ppermute | solution.py:21
  187.7 26.2 %collective-permute-start.83 = (bf16[128,1024]{1,0:T(8,128)(2,1)S(1)}, bf16[128,1024]{1,0:T(8,128)(2,1)S(1)}, u32[]{:S(2)}, u32[]{:S(2)}) collective-permute-start(bf16[128,1024]{1,0:T(8,128)(2,1)S(1)} %copy-done.50), channel_id=1, source_target_pairs={{0,24},{4,28},{8,16},{12,20},{16,8},{20,12},{24,0},{28,4},{1,25},{... | collective-permute-start | bytes 786440 | tf_op jit(solution)/shard_map/ppermute | solution.py:21
  193.2 31.5 %collective-permute-start.82 = (bf16[128,1024]{1,0:T(8,128)(2,1)S(1)}, bf16[128,1024]{1,0:T(8,128)(2,1)S(1)}, u32[]{:S(2)}, u32[]{:S(2)}) collective-permute-start(bf16[128,1024]{1,0:T(8,128)(2,1)S(1)} %copy-done.50), channel_id=1, source_target_pairs={{0,16},{4,20},{8,24},{12,28},{16,0},{20,4},{24,8},{28,12},{1,17},{... | collective-permute-start | bytes 786440 | tf_op jit(solution)/shard_map/ppermute | solution.py:21
  229.8 37.6 %collective-permute-start.42 = (bf16[128,1024]{1,0:T(8,128)(2,1)}, bf16[128,1024]{1,0:T(8,128)(2,1)S(1)}, u32[]{:S(2)}, u32[]{:S(2)}) collective-permute-start(bf16[128,1024]{1,0:T(8,128)(2,1)} %get-tuple-element.171), channel_id=1, source_target_pairs={{0,16},{4,20},{8,24},{12,28},{16,0},{20,4},{24,8},{28,12},{1,17},{... | collective-permute-start | bytes 786440 | tf_op jit(solution)/shard_map/ppermute | solution.py:21
  235.5 37.5 %collective-permute-start.60 = (bf16[128,1024]{1,0:T(8,128)(2,1)}, bf16[128,1024]{1,0:T(8,128)(2,1)S(1)}, u32[]{:S(2)}, u32[]{:S(2)}) collective-permute-start(bf16[128,1024]{1,0:T(8,128)(2,1)} %refs_0_.3), channel_id=1, source_target_pairs={{0,16},{4,20},{8,24},{12,28},{16,0},{20,4},{24,8},{28,12},{1,17},{... | collective-permute-start | bytes 786440 | tf_op jit(solution)/shard_map/ppermute | solution.py:21
  235.6 39.7 %collective-permute-start.58 = (bf16[128,1024]{1,0:T(8,128)(2,1)}, bf16[128,1024]{1,0:T(8,128)(2,1)}, u32[]{:S(2)}, u32[]{:S(2)}) collective-permute-start(bf16[128,1024]{1,0:T(8,128)(2,1)} %refs_0_.3), channel_id=1, source_target_pairs={{0,8},{4,12},{8,0},{12,4},{16,24},{20,28},{24,16},{28,20},{1,9},{5... | collective-permute-start | bytes 786440 | tf_op jit(solution)/shard_map/ppermute | solution.py:21
  243.6 31.7 %collective-permute-start.62 = (bf16[128,1024]{1,0:T(8,128)(2,1)}, bf16[128,1024]{1,0:T(8,128)(2,1)}, u32[]{:S(2)}, u32[]{:S(2)}) collective-permute-start(bf16[128,1024]{1,0:T(8,128)(2,1)} %refs_0_.3), channel_id=1, source_target_pairs={{0,24},{4,28},{8,16},{12,20},{16,8},{20,12},{24,0},{28,4},{1,25},{... | collective-permute-start | bytes 786440 | tf_op jit(solution)/shard_map/ppermute | solution.py:21
  275.3 21.3 %collective-permute-start.57 = (bf16[128,1024]{1,0:T(8,128)(2,1)}, bf16[128,1024]{1,0:T(8,128)(2,1)}, u32[]{:S(2)}, u32[]{:S(2)}) collective-permute-start(bf16[128,1024]{1,0:T(8,128)(2,1)} %refs_0_.3), channel_id=1, source_target_pairs={{0,4},{4,0},{8,12},{12,8},{16,20},{20,16},{24,28},{28,24},{1,5},{5... | collective-permute-start | bytes 786440 | tf_op jit(solution)/shard_map/ppermute | solution.py:21
  275.3 22.2 %collective-permute-start.61 = (bf16[128,1024]{1,0:T(8,128)(2,1)}, bf16[128,1024]{1,0:T(8,128)(2,1)}, u32[]{:S(2)}, u32[]{:S(2)}) collective-permute-start(bf16[128,1024]{1,0:T(8,128)(2,1)} %copy-done.77), channel_id=1, source_target_pairs={{0,4},{4,0},{8,12},{12,8},{16,20},{20,16},{24,28},{28,24},{1,5},{5... | collective-permute-start | bytes 786440 | tf_op jit(solution)/shard_map/ppermute | solution.py:21
  313.2 21.8 %collective-permute-start.65 = (bf16[128,1024]{1,0:T(8,128)(2,1)S(1)}, bf16[128,1024]{1,0:T(8,128)(2,1)S(1)}, u32[]{:S(2)}, u32[]{:S(2)}) collective-permute-start(bf16[128,1024]{1,0:T(8,128)(2,1)S(1)} %multiply_convert_fusion.12.refs_0_), channel_id=1, source_target_pairs={{0,16},{4,20},{8,24},{12,28},{16,0},{20,4},{24,8},{28,12},{1,17},{... | collective-permute-start | bytes 786440 | tf_op jit(solution)/shard_map/ppermute | solution.py:21
  313.3 21.7 %collective-permute-start.64 = (bf16[128,1024]{1,0:T(8,128)(2,1)S(1)}, bf16[128,1024]{1,0:T(8,128)(2,1)S(1)}, u32[]{:S(2)}, u32[]{:S(2)}) collective-permute-start(bf16[128,1024]{1,0:T(8,128)(2,1)S(1)} %multiply_convert_fusion.12.refs_0_), channel_id=1, source_target_pairs={{0,8},{4,12},{8,0},{12,4},{16,24},{20,28},{24,16},{28,20},{1,9},{5... | collective-permute-start | bytes 786440 | tf_op jit(solution)/shard_map/ppermute | solution.py:21
  362.3 66.7 %collective-permute-start.160 = (bf16[512,1024]{1,0:T(8,128)(2,1)}, bf16[512,1024]{1,0:T(8,128)(2,1)}, u32[]{:S(2)}, u32[]{:S(2)}) collective-permute-start(bf16[512,1024]{1,0:T(8,128)(2,1)} %get-tuple-element.234), channel_id=1, source_target_pairs={{0,2},{1,3},{2,0},{3,1},{4,6},{5,7},{6,4},{7,5},{8,10},{9,11},{10,... | collective-permute-start | bytes 3145736 | tf_op jit(solution)/shard_map/ppermute | solution.py:21
  362.9 126.9 %collective-permute-start.158 = (bf16[1024,512]{1,0:T(8,128)(2,1)}, bf16[1024,512]{1,0:T(8,128)(2,1)}, u32[]{:S(2)}, u32[]{:S(2)}) collective-permute-start(bf16[1024,512]{1,0:T(8,128)(2,1)} %get-tuple-element.232), channel_id=1, source_target_pairs={{0,1},{1,0},{2,3},{3,2},{4,5},{5,4},{6,7},{7,6},{8,9},{9,8},{10,11... | collective-permute-start | bytes 3145736 | tf_op jit(solution)/shard_map/ppermute | solution.py:21
  376.6 24.4 %collective-permute-start.74 = (bf16[96,1024]{1,0:T(8,128)(2,1)S(1)}, bf16[96,1024]{1,0:T(8,128)(2,1)S(1)}, u32[]{:S(2)}, u32[]{:S(2)}) collective-permute-start(bf16[96,1024]{1,0:T(8,128)(2,1)S(1)} %get-tuple-element.175), channel_id=1, source_target_pairs={{0,1},{1,0},{2,3},{3,2},{4,5},{5,4},{6,7},{7,6},{8,9},{9,8},{10,11... | collective-permute-start | bytes 589832 | tf_op jit(solution)/shard_map/ppermute | solution.py:21
  377.3 26.1 %collective-permute-start.76 = (bf16[96,1024]{1,0:T(8,128)(2,1)}, bf16[96,1024]{1,0:T(8,128)(2,1)}, u32[]{:S(2)}, u32[]{:S(2)}) collective-permute-start(bf16[96,1024]{1,0:T(8,128)(2,1)} %get-tuple-element.176), channel_id=1, source_target_pairs={{0,3},{1,2},{2,1},{3,0},{4,7},{5,6},{6,5},{7,4},{8,11},{9,10},{10,... | collective-permute-start | bytes 589832 | tf_op jit(solution)/shard_map/ppermute | solution.py:21
  378.9 26.2 %collective-permute-start.75 = (bf16[96,1024]{1,0:T(8,128)(2,1)}, bf16[96,1024]{1,0:T(8,128)(2,1)}, u32[]{:S(2)}, u32[]{:S(2)}) collective-permute-start(bf16[96,1024]{1,0:T(8,128)(2,1)} %get-tuple-element.177), channel_id=1, source_target_pairs={{0,2},{1,3},{2,0},{3,1},{4,6},{5,7},{6,4},{7,5},{8,10},{9,11},{10,... | collective-permute-start | bytes 589832 | tf_op jit(solution)/shard_map/ppermute | solution.py:21
  432.0 100.8 %collective-permute-start.161 = (bf16[512,1024]{1,0:T(8,128)(2,1)}, bf16[512,1024]{1,0:T(8,128)(2,1)}, u32[]{:S(2)}, u32[]{:S(2)}) collective-permute-start(bf16[512,1024]{1,0:T(8,128)(2,1)} %fusion.56), channel_id=1, source_target_pairs={{0,1},{1,0},{2,3},{3,2},{4,5},{5,4},{6,7},{7,6},{8,9},{9,8},{10,11... | collective-permute-start | bytes 3145736 | tf_op jit(solution)/shard_map/ppermute | solution.py:21
  436.4 33.2 %collective-permute-start.96 = (bf16[128,1024]{1,0:T(8,128)(2,1)S(1)}, bf16[128,1024]{1,0:T(8,128)(2,1)S(1)}, u32[]{:S(2)}, u32[]{:S(2)}) collective-permute-start(bf16[128,1024]{1,0:T(8,128)(2,1)S(1)} %get-tuple-element.165), channel_id=1, source_target_pairs={{0,16},{4,20},{8,24},{12,28},{16,0},{20,4},{24,8},{28,12},{1,17},{... | collective-permute-start | bytes 786440 | tf_op jit(solution)/shard_map/ppermute | solution.py:21
  442.9 27.1 %collective-permute-start.78 = (bf16[128,1024]{1,0:T(8,128)(2,1)S(1)}, bf16[128,1024]{1,0:T(8,128)(2,1)S(1)}, u32[]{:S(2)}, u32[]{:S(2)}) collective-permute-start(bf16[128,1024]{1,0:T(8,128)(2,1)S(1)} %get-tuple-element.166), channel_id=1, source_target_pairs={{0,8},{4,12},{8,0},{12,4},{16,24},{20,28},{24,16},{28,20},{1,9},{5... | collective-permute-start | bytes 786440 | tf_op jit(solution)/shard_map/ppermute | solution.py:21
  493.0 45.0 %collective-permute-start.159 = (bf16[1024,512]{1,0:T(8,128)(2,1)}, bf16[1024,512]{1,0:T(8,128)(2,1)}, u32[]{:S(2)}, u32[]{:S(2)}) collective-permute-start(bf16[1024,512]{1,0:T(8,128)(2,1)} %fusion.55), channel_id=1, source_target_pairs={{0,2},{1,3},{2,0},{3,1},{4,6},{5,7},{6,4},{7,5},{8,10},{9,11},{10,... | collective-permute-start | bytes 3145736 | tf_op jit(solution)/shard_map/ppermute | solution.py:21
  522.8 57.2 %collective-permute-start.153 = (bf16[512,1024]{1,0:T(8,128)(2,1)}, bf16[512,1024]{1,0:T(8,128)(2,1)}, u32[]{:S(2)}, u32[]{:S(2)}) collective-permute-start(bf16[512,1024]{1,0:T(8,128)(2,1)} %get-tuple-element.91), channel_id=1, source_target_pairs={{0,4},{4,0},{8,12},{12,8},{16,20},{20,16},{24,28},{28,24},{1,5},{5... | collective-permute-start | bytes 3145736 | tf_op jit(solution)/shard_map/ppermute | solution.py:21
  563.0 23.0 %collective-permute-start.113 = (bf16[192,1024]{1,0:T(8,128)(2,1)S(1)}, bf16[192,1024]{1,0:T(8,128)(2,1)S(1)}, u32[]{:S(2)}, u32[]{:S(2)}) collective-permute-start(bf16[192,1024]{1,0:T(8,128)(2,1)S(1)} %bitcast.225), channel_id=1, source_target_pairs={{0,3},{1,2},{2,1},{3,0},{4,7},{5,6},{6,5},{7,4},{8,11},{9,10},{10,... | collective-permute-start | bytes 1179656 | tf_op jit(solution)/shard_map/ppermute | solution.py:21
  564.4 24.0 %collective-permute-start.112 = (bf16[192,1024]{1,0:T(8,128)(2,1)S(1)}, bf16[192,1024]{1,0:T(8,128)(2,1)S(1)}, u32[]{:S(2)}, u32[]{:S(2)}) collective-permute-start(bf16[192,1024]{1,0:T(8,128)(2,1)S(1)} %bitcast.226), channel_id=1, source_target_pairs={{0,2},{1,3},{2,0},{3,1},{4,6},{5,7},{6,4},{7,5},{8,10},{9,11},{10,... | collective-permute-start | bytes 1179656 | tf_op jit(solution)/shard_map/ppermute | solution.py:21
  565.5 23.8 %collective-permute-start.111 = (bf16[192,1024]{1,0:T(8,128)(2,1)S(1)}, bf16[192,1024]{1,0:T(8,128)(2,1)}, u32[]{:S(2)}, u32[]{:S(2)}) collective-permute-start(bf16[192,1024]{1,0:T(8,128)(2,1)S(1)} %bitcast.227), channel_id=1, source_target_pairs={{0,1},{1,0},{2,3},{3,2},{4,5},{5,4},{6,7},{7,6},{8,9},{9,8},{10,11... | collective-permute-start | bytes 1179656 | tf_op jit(solution)/shard_map/ppermute | solution.py:21
  580.0 83.6 %collective-permute-start.143 = (bf16[1024,512]{1,0:T(8,128)(2,1)}, bf16[1024,512]{1,0:T(8,128)(2,1)}, u32[]{:S(2)}, u32[]{:S(2)}) collective-permute-start(bf16[1024,512]{1,0:T(8,128)(2,1)} %get-tuple-element.228), channel_id=1, source_target_pairs={{0,1},{1,0},{2,3},{3,2},{4,5},{5,4},{6,7},{7,6},{8,9},{9,8},{10,11... | collective-permute-start | bytes 3145736 | tf_op jit(solution)/shard_map/ppermute | solution.py:21
  584.8 25.6 %collective-permute-start.154 = (bf16[256,1024]{1,0:T(8,128)(2,1)}, bf16[256,1024]{1,0:T(8,128)(2,1)}, u32[]{:S(2)}, u32[]{:S(2)}) collective-permute-start(bf16[256,1024]{1,0:T(8,128)(2,1)} %slice.665), channel_id=1, source_target_pairs={{0,8},{4,12},{8,0},{12,4},{16,24},{20,28},{24,16},{28,20},{1,9},{5... | collective-permute-start | bytes 1572872 | tf_op jit(solution)/shard_map/ppermute | solution.py:21
  586.0 22.5 %collective-permute-start.149 = (bf16[128,768]{1,0:T(8,128)(2,1)}, bf16[128,768]{1,0:T(8,128)(2,1)}, u32[]{:S(2)}, u32[]{:S(2)}) collective-permute-start(bf16[128,768]{1,0:T(8,128)(2,1)} %slice.671), channel_id=1, source_target_pairs={{0,16},{4,20},{8,24},{12,28},{16,0},{20,4},{24,8},{28,12},{1,17},{... | collective-permute-start | bytes 589832 | tf_op jit(solution)/shard_map/ppermute | solution.py:21
  608.5 21.8 %collective-permute-start.115 = (bf16[192,1024]{1,0:T(8,128)(2,1)S(1)}, bf16[192,1024]{1,0:T(8,128)(2,1)S(1)}, u32[]{:S(2)}, u32[]{:S(2)}) collective-permute-start(bf16[192,1024]{1,0:T(8,128)(2,1)S(1)} %get-tuple-element.156), channel_id=1, source_target_pairs={{0,2},{1,3},{2,0},{3,1},{4,6},{5,7},{6,4},{7,5},{8,10},{9,11},{10,... | collective-permute-start | bytes 1179656 | tf_op jit(solution)/shard_map/ppermute | solution.py:21
  610.4 30.8 %collective-permute-start.152 = (bf16[128,768]{1,0:T(8,128)(2,1)S(1)}, bf16[128,768]{1,0:T(8,128)(2,1)S(1)}, u32[]{:S(2)}, u32[]{:S(2)}) collective-permute-start(bf16[128,768]{1,0:T(8,128)(2,1)S(1)} %fusion.90.refs_0_), channel_id=1, source_target_pairs={{0,3},{1,2},{2,1},{3,0},{4,7},{5,6},{6,5},{7,4},{8,11},{9,10},{10,... | collective-permute-start | bytes 589832 | tf_op jit(solution)/shard_map/ppermute | solution.py:21
  617.9 43.4 %collective-permute-start.155 = (bf16[128,1024]{1,0:T(8,128)(2,1)}, bf16[128,1024]{1,0:T(8,128)(2,1)S(1)}, u32[]{:S(2)}, u32[]{:S(2)}) collective-permute-start(bf16[128,1024]{1,0:T(8,128)(2,1)} %slice.669), channel_id=1, source_target_pairs={{0,16},{4,20},{8,24},{12,28},{16,0},{20,4},{24,8},{28,12},{1,17},{... | collective-permute-start | bytes 786440 | tf_op jit(solution)/shard_map/ppermute | solution.py:21
  635.0 32.8 %collective-permute-start.117 = (bf16[512,1024]{1,0:T(8,128)(2,1)}, bf16[512,1024]{1,0:T(8,128)(2,1)}, u32[]{:S(2)}, u32[]{:S(2)}) collective-permute-start(bf16[512,1024]{1,0:T(8,128)(2,1)} %slice.661), channel_id=1, source_target_pairs={{0,4},{4,0},{8,12},{12,8},{16,20},{20,16},{24,28},{28,24},{1,5},{5... | collective-permute-start | bytes 3145736 | tf_op jit(solution)/shard_map/ppermute | solution.py:21
  646.2 26.2 %collective-permute-start.145 = (bf16[512,1024]{1,0:T(8,128)(2,1)}, bf16[512,1024]{1,0:T(8,128)(2,1)}, u32[]{:S(2)}, u32[]{:S(2)}) collective-permute-start(bf16[512,1024]{1,0:T(8,128)(2,1)} %get-tuple-element.230), channel_id=1, source_target_pairs={{0,2},{1,3},{2,0},{3,1},{4,6},{5,7},{6,4},{7,5},{8,10},{9,11},{10,... | collective-permute-start | bytes 3145736 | tf_op jit(solution)/shard_map/ppermute | solution.py:21
  666.9 68.8 %collective-permute-start.144 = (bf16[1024,512]{1,0:T(8,128)(2,1)}, bf16[1024,512]{1,0:T(8,128)(2,1)}, u32[]{:S(2)}, u32[]{:S(2)}) collective-permute-start(bf16[1024,512]{1,0:T(8,128)(2,1)} %fusion.53), channel_id=1, source_target_pairs={{0,2},{1,3},{2,0},{3,1},{4,6},{5,7},{6,4},{7,5},{8,10},{9,11},{10,... | collective-permute-start | bytes 3145736 | tf_op jit(solution)/shard_map/ppermute | solution.py:21
  676.1 64.7 %collective-permute-start.146 = (bf16[512,1024]{1,0:T(8,128)(2,1)}, bf16[512,1024]{1,0:T(8,128)(2,1)}, u32[]{:S(2)}, u32[]{:S(2)}) collective-permute-start(bf16[512,1024]{1,0:T(8,128)(2,1)} %fusion.54), channel_id=1, source_target_pairs={{0,1},{1,0},{2,3},{3,2},{4,5},{5,4},{6,7},{7,6},{8,9},{9,8},{10,11... | collective-permute-start | bytes 3145736 | tf_op jit(solution)/shard_map/ppermute | solution.py:21
  731.7 22.3 %collective-permute-start.138 = (bf16[512,1024]{1,0:T(8,128)(2,1)}, bf16[512,1024]{1,0:T(8,128)(2,1)}, u32[]{:S(2)}, u32[]{:S(2)}) collective-permute-start(bf16[512,1024]{1,0:T(8,128)(2,1)} %get-tuple-element.86), channel_id=1, source_target_pairs={{0,4},{4,0},{8,12},{12,8},{16,20},{20,16},{24,28},{28,24},{1,5},{5... | collective-permute-start | bytes 3145736 | tf_op jit(solution)/shard_map/ppermute | solution.py:21
  747.5 24.4 %collective-permute-start.132 = (bf16[512,768]{1,0:T(8,128)(2,1)}, bf16[512,768]{1,0:T(8,128)(2,1)S(1)}, u32[]{:S(2)}, u32[]{:S(2)}) collective-permute-start(bf16[512,768]{1,0:T(8,128)(2,1)} %get-tuple-element.84), channel_id=1, source_target_pairs={{0,4},{4,0},{8,12},{12,8},{16,20},{20,16},{24,28},{28,24},{1,5},{5... | collective-permute-start | bytes 2359304 | tf_op jit(solution)/shard_map/ppermute | solution.py:21
  791.9 29.8 %collective-permute-start.142 = (bf16[128,1024]{1,0:T(8,128)(2,1)}, bf16[128,1024]{1,0:T(8,128)(2,1)}, u32[]{:S(2)}, u32[]{:S(2)}) collective-permute-start(bf16[128,1024]{1,0:T(8,128)(2,1)} %fusion.94), channel_id=1, source_target_pairs={{0,2},{1,3},{2,0},{3,1},{4,6},{5,7},{6,4},{7,5},{8,10},{9,11},{10,... | collective-permute-start | bytes 786440 | tf_op jit(solution)/shard_map/ppermute | solution.py:21
  (275 other events, 2690.5 us)

commit v2 on v1

v2 whole, which is shorter than its diff:
```python
import jax
import jax.numpy as jnp
from jax import lax
from jax.experimental import pallas as pl
from jax.experimental.pallas import tpu as pltpu
from jax.sharding import PartitionSpec as P

HEAD_DIM = 64
SLICES_SHALLOW = 4
SLICES_DEEP = 2
F32 = jnp.float32
LOW = jnp.bfloat16
VMEM_LIMIT = 60 * 1024 * 1024


def low(value):
    return value.astype(LOW)


def swap(array, axis, distance):
    return lax.ppermute(array, axis, [(i, i ^ distance) for i in range(lax.axis_size(axis))])


def product(left, right, left_dim, right_dim):
    return lax.dot_general(
        left, right, (((left_dim,), (right_dim,)), ((), ())), preferred_element_type=F32
    )


def vmem():
    return pl.BlockSpec(memory_space=pltpu.VMEM)


def smem():
    return pl.BlockSpec(memory_space=pltpu.SMEM)


def call(kernel, outs, scalars, arrays, scratch=(), flops=0):
    moved = sum(a.size * a.dtype.itemsize for a in list(arrays) + list(outs))
    return pl.pallas_call(
        kernel,
        out_shape=tuple(outs),
        in_specs=[smem()] * len(scalars) + [vmem()] * len(arrays),
        out_specs=tuple(vmem() for _ in outs),
        scratch_shapes=list(scratch),
        compiler_params=pltpu.CompilerParams(vmem_limit_bytes=VMEM_LIMIT),
        cost_estimate=pl.CostEstimate(flops=flops, bytes_accessed=moved, transcendentals=0),
    )(*scalars, *arrays)


def shape(dims, kind):
    return jax.ShapeDtypeStruct(dims, kind)


def join_rows(pieces):
    if len(pieces) == 1:
        return pieces[0]
    count, (rows, columns) = len(pieces), pieces[0].shape

    def kernel(*refs):
        for k in range(count):
            refs[count][k * rows : (k + 1) * rows, :] = refs[k][...]

    return call(kernel, [shape((count * rows, columns), pieces[0].dtype)], [], pieces)[0]


def pack_columns(pieces, base):
    count, (rows, columns) = len(pieces), pieces[0].shape

    def kernel(base_ref, *refs):
        for k in range(count):
            start = pl.multiple_of((base_ref[0] ^ k) * columns, columns)
            refs[count][:, pl.ds(start, columns)] = refs[k][...]

    return call(kernel, [shape((rows, count * columns), pieces[0].dtype)], [base], pieces)[0]


def split_columns(whole, count, base):
    rows, columns = whole.shape[0], whole.shape[1] // count

    def kernel(base_ref, whole_ref, *outs):
        for k in range(count):
            start = pl.multiple_of((base_ref[0] ^ k) * columns, columns)
            outs[k][...] = low(whole_ref[:, pl.ds(start, columns)])

    return call(kernel, [shape((rows, columns), LOW)] * count, [base], [whole])


def own_slab(attention_in, extra, base, below):
    rows, triple = attention_in.shape
    columns = triple // (3 * lax.axis_size("narrow"))
    below_rows = below.shape[0] if below is not None else 0
    wide_extra = extra.shape[1] if extra is not None else 0

    def kernel(base_ref, weight_ref, *refs):
        refs, out = list(refs[:-1]), refs[-1]
        for part in range(3):
            start = pl.multiple_of(part * (triple // 3) + base_ref[0] * columns, columns)
            out[:rows, part * columns : (part + 1) * columns] = weight_ref[:, pl.ds(start, columns)]
        if extra is not None:
            out[:rows, 3 * columns :] = refs.pop(0)[...]
        if below is not None:
            out[rows:, :] = jnp.zeros((below_rows, 3 * columns + wide_extra), LOW)
            out[rows:, : below.shape[1]] = refs.pop(0)[...]

    arrays = [attention_in] + [a for a in (extra, below) if a is not None]
    outs = [shape((rows + below_rows, 3 * columns + wide_extra), LOW)]
    return call(kernel, outs, [base], arrays)[0]


def join_slab(found, rows, parts, at_wide, below=0):
    across, beside = found
    pieces = [p for pair in zip(across, beside) for p in pair]
    count = len(pieces)

    def kernel(base_ref, *refs):
        for k in range(count):
            start = pl.multiple_of((base_ref[0] ^ k) * rows, rows)
            at = 0
            for i, columns in enumerate(parts):
                refs[count + i][pl.ds(start, rows), :] = refs[k][:rows, at : at + columns]
                at += columns
            if below:
                start = pl.multiple_of((base_ref[0] ^ k) * below, below)
                refs[-1][pl.ds(start, below), :] = refs[k][rows:, :rows]

    outs = [shape((count * rows, columns), LOW) for columns in parts]
    if below:
        outs.append(shape((count * below, rows), LOW))
    return call(kernel, outs, [at_wide], pieces)


def spread_columns(pieces, base):
    count, (rows, triple) = len(pieces), pieces[0].shape
    columns = triple // 3

    def kernel(base_ref, *refs):
        for k in range(count):
            for part in range(3):
                start = part * count * columns + (base_ref[0] ^ k) * columns
                refs[count][:, pl.ds(pl.multiple_of(start, columns), columns)] = refs[k][
                    :, part * columns : (part + 1) * columns
                ].astype(F32)

    return call(kernel, [shape((rows, count * triple), F32)], [base], pieces)[0]


def narrow_join(own, at_narrow):
    narrow = lax.axis_size("narrow")
    return spread_columns(
        [own] + [swap(own, "narrow", j) for j in range(1, narrow)], at_narrow
    )


def reorder(whole, slots, at_wide, outward):
    count = whole.shape[0] // slots
    order = list(range(0, count, 2)) + list(range(1, count, 2))

    def kernel(base_ref, whole_ref, out_ref):
        for i, k in enumerate(order):
            start = pl.multiple_of((base_ref[0] ^ k) * slots, slots)
            if outward:
                out_ref[pl.ds(start, slots), :] = whole_ref[i * slots : (i + 1) * slots, :]
            else:
                out_ref[i * slots : (i + 1) * slots, :] = whole_ref[pl.ds(start, slots), :]

    return call(kernel, [shape(whole.shape, whole.dtype)], [at_wide], [whole])[0]


def outer_pair(pieces, grad_packed, context, grad_attended):
    count, (slots, features) = len(pieces), pieces[0].shape
    columns = grad_packed.shape[1]

    def kernel(*refs):
        left = jnp.concatenate([r[...] for r in refs[:count]], axis=0)
        packed_ref, context_ref, attended_ref, out = refs[count:]
        out[:, :columns] = low(product(left, packed_ref[...], 0, 0))
        out[:, columns:] = low(product(context_ref[...], attended_ref[...], 0, 0))

    outs = [shape((features, columns + context.shape[1]), LOW)]
    flops = 2 * slots * features * (count * columns + context.shape[1])
    arrays = list(pieces) + [grad_packed, context, grad_attended]
    return call(kernel, outs, [], arrays, flops=flops)[0]


def join_pair(gathered, columns):
    narrow = lax.axis_size("narrow")
    rows = gathered.shape[0] // narrow
    features = gathered.shape[1] - columns
    third = columns // 3

    def kernel(whole_ref, in_ref, out_ref):
        total = None
        for j in range(narrow):
            block = whole_ref[j * rows : (j + 1) * rows, :]
            for part in range(3):
                at = part * narrow * third + j * third
                in_ref[:, at : at + third] = block[:, part * third : (part + 1) * third].astype(F32)
            found = block[:, columns:].astype(F32)
            total = found if total is None else total + found
        out_ref[...] = total

    outs = [shape((rows, narrow * columns), F32), shape((rows, features), F32)]
    return call(kernel, outs, [], [gathered])


def dense_products(parts):
    return low(up_product(parts)), low(down_product(parts))


def narrow_step(pair, step):
    bits = lax.axis_size("narrow").bit_length() - 1
    return [
        low(value.astype(F32) + swap(value, "narrow", 1 << (step + i) % bits).astype(F32))
        for i, value in enumerate(pair)
    ]


def narrow_last(pair):
    bits = lax.axis_size("narrow").bit_length() - 1
    for step in range(1, bits - 1):
        pair = narrow_step(pair, step)
    return [
        (value, swap(value, "narrow", 1 << (bits - 1 + i) % bits)) for i, value in enumerate(pair)
    ]


def dense_join(parts):
    up, down = parts
    features, units = up.shape
    fold = features // units

    def kernel(up_ref, down_ref, out_ref):
        for i in range(fold):
            out_ref[:units, i * units : (i + 1) * units] = up_ref[i * units : (i + 1) * units, :]
        out_ref[units:, :] = down_ref[...]

    return call(kernel, [shape((2 * units, features), LOW)], [], [up, down])[0]


def narrow_scatter(whole):
    return lax.psum_scatter(whole, "narrow", scatter_dimension=0, tiled=True)


def narrow_gather(own):
    return lax.all_gather(own, "narrow", axis=0, tiled=True)


def dense_outputs(gathered):
    units, features = gathered.shape[0] // 2, gathered.shape[1]
    fold = features // units

    def kernel(whole_ref, up_ref, down_ref):
        for i in range(fold):
            up_ref[i * units : (i + 1) * units, :] = whole_ref[
                :units, i * units : (i + 1) * units
            ].astype(F32)
        down_ref[...] = whole_ref[units:, :].astype(F32)

    return call(kernel, [shape((features, units), F32), shape((units, features), F32)], [], [gathered])


def gather_wide(own):
    return lax.all_gather(own, "wide", axis=0, tiled=True)


def after(value, *others):
    return lax.optimization_barrier((value,) + others)[0]


def reversed_order(count):
    bits = count.bit_length() - 1
    return [sum((i >> b & 1) << (bits - 1 - b) for b in range(bits)) for i in range(count)]


def outer_halves(lefts, right, base):
    count = len(lefts)
    wide = lax.axis_size("wide")
    slots, features = lefts[0].shape
    columns = right.shape[1]
    rows = features // wide
    order = reversed_order(wide)

    def kernel(base_ref, *refs):
        right_ref, keep_ref, send_ref, total_ref = refs[count:]
        left = refs[0][...] if count == 1 else jnp.concatenate([r[...] for r in refs[:count]], axis=0)
        total_ref[...] = product(left, right_ref[...], 0, 0)
        for i, k in enumerate(order):
            start = pl.multiple_of((base_ref[0] ^ k) * rows, rows)
            out, at = (keep_ref, i) if i < wide // 2 else (send_ref, i - wide // 2)
            out[at * rows : (at + 1) * rows, :] = low(total_ref[pl.ds(start, rows), :])

    outs = [shape((features // 2, columns), LOW)] * 2
    scratch = [pltpu.VMEM((features, columns), F32)]
    flops = 2 * count * slots * features * columns
    return call(kernel, outs, [base], list(lefts) + [right], scratch, flops)


def pair_sum(own, received, slots):
    count = own.shape[0] // slots
    features = own.shape[1]

    def kernel(own_ref, received_ref, *outs):
        for k in range(count):
            at = slice(k * slots, (k + 1) * slots)
            total = own_ref[at, :] + received_ref[at, :].astype(F32)
            outs[k][...] = total if k == 0 else low(total)

    outs = [shape((slots, features), F32)] + [shape((slots, features), LOW)] * (count - 1)
    return call(kernel, outs, [], [own, received])


def halving_step(halves, distance):
    keep, send = halves
    total = keep.astype(F32) + swap(send, "wide", distance).astype(F32)
    if 2 * distance == lax.axis_size("wide"):
        return total
    half = total.shape[0] // 2
    return total[:half], low(total[half:])


def halving_rest(halves, distance):
    while distance < lax.axis_size("wide"):
        halves = halving_step(halves, distance)
        distance *= 2
    return halves


def together(value, other):
    return lax.optimization_barrier((value, other))


def narrow_sum(value, first):
    narrow = lax.axis_size("narrow")
    bits = narrow.bit_length() - 1
    for b in range(bits):
        value = value + swap(low(value), "narrow", 1 << (b + first) % bits).astype(F32)
    return value


def narrow_rest(value):
    distance = 2
    while distance < lax.axis_size("narrow"):
        value = value + swap(low(value), "narrow", distance).astype(F32)
        distance *= 2
    return value


def everywhere_sum(value):
    for axis in ("narrow", "wide"):
        distance = 1
        while distance < lax.axis_size(axis):
            value = value + swap(value, axis, distance)
            distance *= 2
    return value


def layer_norm(source, gain):
    centre = source - jnp.mean(source, axis=-1, keepdims=True)
    inverse = lax.rsqrt(jnp.mean(centre * centre, axis=-1, keepdims=True) + 1e-05)
    scaled = centre * inverse
    return scaled * gain, scaled, inverse


def norm_back(upstream, scaled, inverse, gain):
    grad_scaled = upstream * gain
    mean_first = jnp.mean(grad_scaled, axis=-1, keepdims=True)
    mean_second = jnp.mean(grad_scaled * scaled, axis=-1, keepdims=True)
    return (
        inverse * (grad_scaled - mean_first - scaled * mean_second),
        jnp.sum(upstream * scaled, axis=0),
    )


def activate(source):
    return jax.nn.gelu(source)


def activation_back(source, upstream):
    return jax.vjp(activate, source)[1](upstream)[0]


def softened_scores(queries, keys, allowed):
    scores = product(queries, keys, 1, 1) * HEAD_DIM ** (-0.5)
    scores = jnp.where(allowed, scores, -1e30)
    raised = jnp.exp(scores - jnp.max(scores, axis=-1, keepdims=True))
    return raised / jnp.sum(raised, axis=-1, keepdims=True)


def allowed_of(length, slots):
    rows_at = lax.broadcasted_iota(jnp.int32, (slots, slots), 0)
    cols_at = lax.broadcasted_iota(jnp.int32, (slots, slots), 1)
    return (cols_at <= rows_at) & (cols_at < length)


def head_parts(packed, head, columns):
    return [
        packed[:, part * columns + head * HEAD_DIM : part * columns + (head + 1) * HEAD_DIM]
        for part in range(3)
    ]


def attention(pieces, gain, weight, lengths):
    count, (slots, features) = len(pieces), pieces[0].shape
    columns = weight.shape[1] // 3
    raw = gain is not None

    def kernel(lengths_ref, *refs):
        ins, weight_ref, refs = refs[:count], refs[count], refs[count + 1 :]
        if raw:
            gain_ref, refs = refs[0], refs[1:]
        packed_ref, outs = refs[0], refs[1 : count + 1]
        for j in range(count):
            if raw:
                rows = low(layer_norm(ins[j][...].astype(F32), gain_ref[...])[0])
                refs[count + 1 + j][...] = rows
            else:
                rows = ins[j][...]
            packed = low(product(rows, weight_ref[...], 1, 0))
            packed_ref[j] = packed
            allowed = allowed_of(lengths_ref[j], slots)
            found = []
            for head in range(columns // HEAD_DIM):
                queries, keys, values = head_parts(packed, head, columns)
                softened = softened_scores(queries, keys, allowed)
                found.append(product(low(softened), values, 1, 0))
            outs[j][...] = low(jnp.concatenate(found, axis=1))

    outs = [shape((count, slots, 3 * columns), LOW)] + [shape((slots, columns), LOW)] * count
    arrays = list(pieces) + [weight]
    if raw:
        outs += [shape((slots, features), LOW)] * count
        arrays.append(gain[None])
    flops = 2 * count * slots * features * 3 * columns
    packed, *found = call(kernel, outs, [lengths], arrays, flops=flops)
    return packed, found[:count], found[count:] if raw else pieces


def attention_back(packed, grads, lengths):
    count, (slots, columns) = len(grads), grads[0].shape
    scaling = HEAD_DIM ** (-0.5)

    def kernel(lengths_ref, packed_ref, *refs):
        out = refs[count]
        for j in range(count):
            allowed = allowed_of(lengths_ref[j], slots)
            whole = packed_ref[j]
            grad_whole = refs[j][...]
            found = [[], [], []]
            for head in range(columns // HEAD_DIM):
                queries, keys, values = head_parts(whole, head, columns)
                grad_head = grad_whole[:, head * HEAD_DIM : (head + 1) * HEAD_DIM]
                softened = softened_scores(queries, keys, allowed)
                grad_soft = product(grad_head, values, 1, 1)
                inner = jnp.sum(softened * grad_soft, axis=-1, keepdims=True)
                grad_scores = low(softened * (grad_soft - inner))
                found[0].append(scaling * product(grad_scores, keys, 1, 0))
                found[1].append(scaling * product(grad_scores, queries, 0, 0))
                found[2].append(product(low(softened), grad_head, 0, 0))
            out[j * slots : (j + 1) * slots, :] = low(
                jnp.concatenate(found[0] + found[1] + found[2], axis=1)
            )

    outs = [shape((count * slots, 3 * columns), LOW)]
    return call(kernel, outs, [lengths], [packed] + list(grads))[0]


def normed_back(grad_packed, weight, count):
    slots, features = grad_packed.shape[0] // count, weight.shape[0]

    def kernel(grad_ref, weight_ref, *outs):
        whole = low(product(grad_ref[...], weight_ref[...], 1, 1))
        for j in range(count):
            outs[j][...] = whole[j * slots : (j + 1) * slots]

    outs = [shape((slots, features), LOW)] * count
    flops = 2 * count * slots * features * weight.shape[1]
    return call(kernel, outs, [], [grad_packed, weight], flops=flops)


def wide_across(own):
    return [own] + [swap(own, "wide", apart) for apart in range(2, lax.axis_size("wide"), 2)]


def wide_pieces(own):
    across = wide_across(own)
    return across, [swap(piece, "wide", 1) for piece in across]


def wide_join(pieces):
    across, beside = pieces
    return join_rows(list(across) + list(beside))


def wide_sends(own, received, slots):
    parts = pair_sum(own, received, slots)
    return [parts[0]] + [swap(p, "wide", 2 * (i + 1)) for i, p in enumerate(parts[1:])]


def wide_total(parts):
    total = parts[0]
    for part in parts[1:]:
        total = total + part.astype(F32)
    return total


def wide_sums(halves, slots):
    own, other = halves
    return wide_total(wide_sends(own, swap(other, "wide", 1), slots))


def place(labels, experts, capacity):
    blocks, slots = labels.shape
    first = jnp.arange(blocks, dtype=jnp.int32)[:, None] * capacity - 1
    places = jnp.arange(blocks * capacity, dtype=jnp.int32)
    selects = []
    for expert in experts:
        chosen = labels == expert
        at = jnp.where(chosen, first + jnp.cumsum(chosen.astype(jnp.int32), axis=1), -1)
        selects.append(low(places[:, None] == at.reshape(-1)[None, :]))
    return selects


def picked(selects, rows):
    return [low(product(select, rows, 1, 0)) for select in selects]


def exchanged(sent, slices):
    narrow = lax.axis_size("narrow")
    return join_rows(
        [sent[j // slices] if j == 0 else swap(sent[j // slices], "narrow", j) for j in range(narrow)]
    )


def to_experts(selects, rows, slices):
    return exchanged(picked(selects, rows), slices)


def from_experts(selects, outcome, slices):
    narrow = lax.axis_size("narrow")
    parts = outcome.reshape(narrow, -1, outcome.shape[-1])
    found = []
    for r in range(len(selects)):
        total = None
        for j in range(r * slices, (r + 1) * slices):
            part = parts[j] if j == 0 else swap(low(parts[j]), "narrow", j).astype(F32)
            total = part if total is None else total + part
        found.append(low(total))
    return found


def spread_of(selects, found, at):
    total = None
    for select, rows in zip(selects, found):
        part = product(select[:, at], rows, 0, 0)
        total = part if total is None else total + part
    return total


def layer_forward(source, raw, weights, selects, lengths, at_narrow, slices, first_work=None, second_work=None):
    norm_first, attention_in, attention_out, norm_second, mixer, up, down, expert_up, expert_down = weights
    slots, features = source.shape
    wide, narrow = lax.axis_size("wide"), lax.axis_size("narrow")
    normed, scaled_one, inverse_one = layer_norm(source, norm_first)
    own = low(normed)
    pieces = raw
    if raw is None:
        pieces = [own] + [swap(own, "narrow", j) for j in range(1, narrow)]
    if first_work is not None:
        pieces, first_found = together(pieces, first_work(own))
    packed, contexts, pieces = attention(
        pieces, None if raw is None else norm_first, attention_in, lengths
    )
    context = pack_columns(
        [contexts[0]] + [swap(contexts[j], "narrow", j) for j in range(1, narrow)], at_narrow
    )
    middle = source + jnp.dot(context, attention_out, preferred_element_type=F32)
    second, scaled_two, inverse_two = layer_norm(middle, norm_second)
    second = low(second)
    across, beside = wide_pieces(second)
    if second_work is not None:
        across, second_found = together(across, second_work(second, first_found))
    rows = wide_join((across, beside))
    mixing = jax.nn.softmax(jnp.dot(rows, mixer, preferred_element_type=F32), axis=-1)
    pre = jnp.dot(rows, up, preferred_element_type=F32)
    act = low(activate(pre))
    expert_rows, (mixing, pre, act) = together(
        to_experts(selects, rows, slices), (mixing, pre, act)
    )
    expert_pre = jnp.dot(expert_rows, expert_up, preferred_element_type=F32)
    expert_act = low(activate(expert_pre))
    kept = (
        scaled_one, inverse_one, pieces, packed, context, scaled_two, inverse_two,
        (rows, mixing, expert_rows, expert_pre, expert_act, pre, act),
    )
    return (middle, kept) if second_work is None else (middle, kept, second_found)


def experts_found(kept, weights, selects, slices, gate=None):
    act = kept[7][4] if gate is None else after(kept[7][4], gate)
    outcome = jnp.dot(act, weights[8], preferred_element_type=F32)
    return from_experts(selects, outcome, slices)


def merged_halves(kept, weights, selects, found, slots):
    mixing, act = kept[7][1], kept[7][6]

    def merged(at):
        dense = jnp.dot(act[at], weights[6], preferred_element_type=F32)
        return mixing[at, :1] * dense + mixing[at, 1:] * spread_of(selects, found, at)

    half = act.shape[0] // 2
    return merged(slice(0, half)), low(merged(slice(half, 2 * half)))


def dense_back_of(through, kept, weights):
    rows, mixing, _, _, _, pre, act = kept[7]
    dense_dot = jnp.sum(act.astype(F32) * through, axis=1, keepdims=True)
    dense_logit = mixing[:, :1] * mixing[:, 1:] * dense_dot
    grad_pre = low(activation_back(pre, mixing[:, :1] * through))
    return grad_pre, dense_logit


def experts_back(upstream, gathered, kept, weights, selects, slices, beneath, alongside):
    norm_second, mixer, up, down, expert_up, expert_down = weights[3:]
    scaled_two, inverse_two = kept[5:7]
    rows, mixing, expert_rows, expert_pre, expert_act, pre, act = kept[7]
    slots = upstream.shape[0]
    wide = lax.axis_size("wide")
    mixer_gap = (mixer[:, 0].astype(F32) - mixer[:, 1].astype(F32))[None]
    grads, expert_grads, through, (grad_pre, dense_logit) = gathered
    expert_mixing = jax.nn.softmax(
        jnp.dot(expert_rows, mixer, preferred_element_type=F32), axis=-1
    )
    expert_dot = jnp.sum(expert_act.astype(F32) * through, axis=1, keepdims=True)
    expert_logit = -expert_mixing[:, :1] * expert_mixing[:, 1:] * expert_dot
    expert_grad_pre = low(activation_back(expert_pre, expert_mixing[:, 1:] * through))
    expert_back = product(expert_grad_pre, expert_up, 1, 1) + expert_logit * mixer_gap
    dense = (rows, grad_pre, act, mixing[:, :1], grads)
    found = from_experts(selects, expert_back, slices)
    experts = (
        expert_rows, expert_grad_pre,
        expert_act, expert_mixing[:, 1:], expert_grads,
    )
    found, beneath_found = together(found, beneath(expert_back, experts, dense))

    def merged(at):
        dense_back = product(grad_pre[at], up, 1, 1) + dense_logit[at] * mixer_gap
        return dense_back + spread_of(selects, found, at)

    half = grad_pre.shape[0] // 2
    halves = merged(slice(0, half)), low(merged(slice(half, 2 * half)))
    grad_gap = jnp.sum(rows.astype(F32) * dense_logit, axis=0) + jnp.sum(
        expert_rows.astype(F32) * expert_logit, axis=0
    )
    parts = wide_sends(halves[0], swap(halves[1], "wide", 1), slots)
    grad_second, alongside_found = together(
        wide_total(parts), alongside(parts[0], beneath_found, experts, dense)
    )
    grad_norm_part, grad_norm_second = norm_back(grad_second, scaled_two, inverse_two, norm_second)
    return (
        upstream + grad_norm_part, dense, experts, (grad_norm_second, grad_gap),
        beneath_found, alongside_found,
    )


def up_product(parts):
    return product(parts[0], parts[1], 0, 0)


def down_product(parts):
    act, mix, grads = parts[2:]
    return product(act, low(mix * grads.astype(F32)), 0, 0)


def attention_grads(grad_middle, kept, weights, lengths, at_narrow, at_wide, last, hold, aside=None):
    norm_first, attention_in, attention_out = weights[:3]
    scaled_one, inverse_one, pieces, packed, context = kept[:5]
    narrow = lax.axis_size("narrow")
    grad_attended = low(grad_middle)
    grad_contexts = split_columns(product(grad_attended, attention_out, 1, 1), narrow, at_narrow)
    grad_contexts = [grad_contexts[0]] + [
        swap(grad_contexts[j], "narrow", j) for j in range(1, narrow)
    ]
    if last:
        out_halves = outer_halves([context], after(grad_attended, grad_contexts[0]), at_wide)
        grad_contexts, out_halves = together(grad_contexts, halving_step(out_halves, 1))
        out_halves = halving_step(out_halves, 2)
        aside = aside(grad_contexts)
    grad_packed = attention_back(packed, grad_contexts, lengths)
    if last:
        grad_packed, out_halves = together(grad_packed, out_halves)
        in_halves = outer_halves(pieces, grad_packed, at_wide)
        parts = normed_back(after(grad_packed, in_halves), attention_in, narrow)
        in_halves = halving_step(in_halves, 1)
        gate = in_halves
        in_halves = halving_step(in_halves, 2)
        in_sum = low(halving_rest(in_halves, 4))
        out_sum = halving_rest(out_halves, 4)
        out_sum = after(out_sum, in_halves) + swap(
            low(after(out_sum, in_halves)), "narrow", 1
        ).astype(F32)
        out_sum = narrow_rest(after(out_sum, in_sum))
        weight_grads = narrow_join(in_sum, at_narrow), out_sum
        hold = hold, in_sum, aside
    else:
        grad_packed, hold = together(grad_packed, hold)
        parts = normed_back(grad_packed, attention_in, narrow)
        weight_grads = (pieces, after(grad_packed, parts), context, grad_attended)
    parts = [parts[0]] + [swap(parts[j], "narrow", j) for j in range(1, narrow)]
    grad_normed = sum(part.astype(F32) for part in (after(parts, gate) if last else parts))
    grad_norm_part, grad_norm_first = norm_back(grad_normed, scaled_one, inverse_one, norm_first)
    return grad_middle + grad_norm_part, grad_norm_first, weight_grads, hold


def body(
    inputs, cotangent, seq_len, shallow_routes, deep_routes,
    shallow_norm_first, shallow_attention_in, shallow_attention_out, shallow_norm_second,
    shallow_dense_up, shallow_dense_down, shallow_mixer, shallow_expert_up, shallow_expert_down,
    deep_norm_first, deep_attention_in, deep_attention_out, deep_norm_second,
    deep_dense_up, deep_dense_down, deep_mixer, deep_expert_up, deep_expert_down,
):
    wide, narrow = lax.axis_size("wide"), lax.axis_size("narrow")
    wide_at, narrow_at = lax.axis_index("wide"), lax.axis_index("narrow")
    at_wide, at_narrow = wide_at.reshape(1), narrow_at.reshape(1)
    slots, features = inputs.shape
    small = jnp.stack(
        [
            shallow_norm_first, shallow_norm_second, deep_norm_first, deep_norm_second,
            shallow_mixer[:, 0], shallow_mixer[:, 1], deep_mixer[:, 0], deep_mixer[:, 1],
        ]
    )
    narrow_columns = 3 * features // narrow
    rows_own = shallow_attention_in.shape[0]
    input_pieces = [inputs] + [swap(inputs, "narrow", j) for j in range(1, narrow)]
    across = wide_across(own_slab(shallow_attention_in, None, at_narrow, small))
    lengths = seq_len[wide_at * narrow + (narrow_at ^ jnp.arange(narrow))]
    deep_slab = own_slab(deep_attention_in, None, at_narrow, None)
    across, (input_pieces, lengths, deep_slab) = together(
        across, (input_pieces, lengths, deep_slab)
    )
    in_pieces = across, [swap(piece, "wide", 1) for piece in across]
    shallow_in, small = join_slab(
        in_pieces, rows_own, [narrow_columns], at_wide, small.shape[0]
    )
    shallow_out = gather_wide(after(shallow_attention_out, in_pieces[0][-1]))
    small = jnp.transpose(small.reshape(wide, 8, -1), (1, 0, 2)).reshape(8, features)
    gains = small[:4].astype(F32)
    def selects_of(routes, slices):
        table = routes.reshape(wide, narrow, slots)
        own = lax.dynamic_index_in_dim(table, narrow_at, axis=1, keepdims=False)
        capacity = slices * max(1, 3 * slots // (2 * wide * narrow))
        groups = narrow // slices
        experts = [wide_at * groups + ((narrow_at // slices) ^ r) for r in range(groups)]
        order = jnp.array(list(range(0, wide, 2)) + list(range(1, wide, 2)))
        return place(own[wide_at ^ order], experts, capacity)

    shallow_selects = selects_of(shallow_routes, SLICES_SHALLOW)
    deep_selects = selects_of(deep_routes, SLICES_DEEP)
    shallow = (
        gains[0], shallow_in, shallow_out, gains[1], small[4:6].T,
        shallow_dense_up, shallow_dense_down, shallow_expert_up[0], shallow_expert_down[0],
    )
    middle, kept_shallow = layer_forward(
        inputs.astype(F32), input_pieces, shallow, shallow_selects, lengths, at_narrow, SLICES_SHALLOW
    )
    deep_in = gather_wide(after(deep_slab, kept_shallow[7][0]))
    all_grads = gather_wide(after(cotangent, kept_shallow[7][2]))
    found = experts_found(kept_shallow, shallow, shallow_selects, SLICES_SHALLOW)
    halves = merged_halves(kept_shallow, shallow, shallow_selects, found, slots)
    total = wide_sums(halves, slots)
    passed = middle + total
    deep_out = gather_wide(after(deep_attention_out, total))
    deep = (
        gains[2], deep_in, deep_out, gains[3], small[6:8].T,
        deep_dense_up, deep_dense_down, deep_expert_up[0], deep_expert_down[0],
    )
    def first_work(own):
        grads = reorder(after(all_grads, own), slots, at_wide, False)
        return grads, picked(deep_selects, grads)

    def second_work(second, found):
        grads, sent = found
        expert_grads = exchanged(after(sent, second), SLICES_DEEP)
        return (
            grads, expert_grads, product(after(grads, second), deep_dense_down, 1, 1),
            product(expert_grads, deep_expert_down[0], 1, 1),
        )

    middle, kept_deep, gathered = layer_forward(
        passed, None, deep, deep_selects, lengths, at_narrow, SLICES_DEEP, first_work, second_work
    )
    grad_middle, _, deep_experts, deep_rows, whole, (deep_down, token) = experts_back(
        cotangent.astype(F32),
        gathered[:2] + (gathered[3], dense_back_of(gathered[2], kept_deep, deep)), kept_deep,
        deep, deep_selects, SLICES_DEEP,
        lambda token, experts, dense: dense_join(dense_products(dense)),
        lambda token, found, experts, dense: (down_product(after(experts, token)), token),
    )
    found = experts_found(kept_deep, deep, deep_selects, SLICES_DEEP, token)
    grad_passed, deep_first, outer_parts, (whole, found) = attention_grads(
        grad_middle, kept_deep, deep, lengths, at_narrow, at_wide, False,
        (narrow_scatter(whole), found),
    )
    passed_low = low(grad_passed)
    across, beside = wide_pieces(passed_low)
    halves = merged_halves(kept_deep, deep, deep_selects, after(found, passed_low), slots)
    result = reorder(
        jnp.concatenate([low(halves[0]), halves[1]], axis=0), slots, at_wide, True
    )
    deep_up = up_product(after(deep_experts, passed_low))
    across, (result, deep_up, whole) = together(across, (result, deep_up, narrow_gather(whole)))
    grads = wide_join((across, beside))
    pair = outer_pair(*after(outer_parts, grads))
    deep_dense = dense_outputs(after(whole, grads))
    expert_grads, (pair, deep_dense, dense_back) = together(
        to_experts(shallow_selects, grads, SLICES_SHALLOW),
        (
            pair, deep_dense,
            dense_back_of(product(grads, shallow_dense_down, 1, 1), kept_shallow, shallow),
        ),
    )
    pair = lax.psum_scatter(pair, "wide", scatter_dimension=0, tiled=True)

    grad_middle, _, _, shallow_rows, _, (shallow_experts, shallow_dense, pair) = experts_back(
        grad_passed,
        (grads, expert_grads, product(expert_grads, shallow_expert_down[0], 1, 1), dense_back),
        kept_shallow, shallow, shallow_selects, SLICES_SHALLOW,
        lambda token, experts, dense: dense_products(after(dense, token)),
        lambda token, found, experts, dense: (
            [f(after(experts, token)) for f in (up_product, down_product)],
            narrow_step(after(found, token), 0), pair,
        ),
    )
    shallow_up, shallow_down = shallow_experts
    total = lax.psum_scatter(
        after(result, grad_middle), "wide", scatter_dimension=0, tiled=True
    )
    grad_inputs, shallow_first, (grad_shallow_in, grad_shallow_out), total = attention_grads(
        grad_middle, kept_shallow, shallow, lengths, at_narrow, at_wide, True, total,
        lambda token: narrow_last(after(shallow_dense, token)),
    )
    total, vector_gate, shallow_dense = total
    shallow_dense, total, pair = after((shallow_dense, total, narrow_gather(pair)), vector_gate)
    shallow_dense = [own.astype(F32) + other.astype(F32) for own, other in shallow_dense]
    output = middle + total.astype(F32)
    grad_deep_in, grad_deep_out = join_pair(pair, narrow_columns)
    deep_up, deep_down = deep_up[None], deep_down[None]
    shallow_up, shallow_down = shallow_up[None], shallow_down[None]
    grads_shallow = (
        grad_shallow_in, grad_shallow_out, *shallow_dense, shallow_up, shallow_down,
        shallow_first, *shallow_rows,
    )
    grads_deep = (
        grad_deep_in, grad_deep_out, *deep_dense, deep_up, deep_down, deep_first, *deep_rows,
    )
    vectors = everywhere_sum(
        after(jnp.stack(list(grads_shallow[6:]) + list(grads_deep[6:])), vector_gate)
    )
    vectors = lax.dynamic_slice_in_dim(vectors, wide_at * (features // wide), features // wide, axis=1)

    def outputs_of(grads, rows):
        grad_mixer = jnp.stack([rows[2], -rows[2]], axis=1)
        return (
            rows[0], grads[0], grads[1], rows[1], grads[2], grads[3], grad_mixer, grads[4], grads[5],
        )

    return (
        (low(output), grad_inputs)
        + outputs_of(grads_shallow, vectors[:3])
        + outputs_of(grads_deep, vectors[3:])
    )


def solution(mesh):
    both = ("wide", "narrow")
    parameters = (
        P("wide"), P("wide", None), P("wide", None), P("wide"), P(None, "wide"),
        P("wide", None), P("wide", None), P(both, None, None), P(both, None, None),
    )
    return jax.shard_map(
        body,
        mesh=mesh,
        in_specs=(P(both, None), P(both, None), P(), P(), P()) + parameters + parameters,
        out_specs=(P(both, None), P(both, None)) + parameters + parameters,
        check_vma=False,
    )
```

time: 835 us -> 701 us (0.84)
  waiting for transfers between devices: 305 us -> 224 us
  local copies, waits for them, and re-layouts: 78.4 us -> 30.6 us
  starting transfers between devices: 148 us -> 129 us
  other arithmetic: 74.3 us -> 57.2 us
  between operations: 3.09 us -> 16.3 us
  matrix products: 110 us -> 120 us
    ppermute x162 -> x108, waiting for transfers between devices: 305 us -> 222 us  [swap(): lax.ppermute(array, axis, [(i, i ^ distance) for i in range(lax.axis_size...]
    unnamed x326 -> x331, local copies, waits for them, and re-layouts: 38.5 us -> 15.8 us
    ppermute x162 -> x108, starting transfers between devices: 148 us -> 126 us  [swap(): lax.ppermute(array, axis, [(i, i ^ distance) for i in range(lax.axis_size...]
    dot_general x20 -> x38, matrix products: 64.5 us -> 85.9 us  [product(): lax.dot_general(left, right, (((left_dim,), (right_dim,)), ((), ())), pre...]
    convert_element_type x6 -> x0, local copies, waits for them, and re-layouts: 16.3 us -> none  [layer_backward(): grad_in = grad_in.reshape(features // wide, -1).astype(F32)]
    dot_general x18 -> x8, matrix products: 24.7 us -> 12.3 us  [the longest x2 4.72 us: experts_found(): outcome = jnp.dot(act, weights[8], preferred_element_type=F32)]
    add x19 -> x14, other arithmetic: 25.7 us -> 15.7 us  [the longest x2 6.42 us: body(): own.astype(F32) + other.astype(F32)]
    convert_element_type x23 -> x20, other arithmetic: 30.6 us -> 20.9 us  [low(): return value.astype(LOW)]
  transfers between devices with their start and end apart: 162 -> 117, of which waited for: 59 -> 57; matrix products, arithmetic and copies ran while one was open for 25% -> 22% of each run, Pallas kernels for 11% -> 13%
where the time goes in v2:
time: 701 us; the launch traced here: 691 us
  waiting for transfers between devices  224 us (32%)
  starting transfers between devices  129 us (18%)
  matrix products  120 us (17%)
  Pallas kernels  114 us (16%)
  other arithmetic  57.2 us (8%)
  local copies, waits for them, and re-layouts  30.6 us (4%)
  between operations  16.3 us (2%)
    ppermute x108, waiting for transfers between devices, swap(): lax.ppermute(array, axis, [(i, i ^ distance) for i in range(lax.axis_size...  222 us
    ppermute x108, starting transfers between devices, swap(): lax.ppermute(array, axis, [(i, i ^ distance) for i in range(lax.axis_size...  126 us
    pallas_call x32, Pallas kernels, call(): pl.pallas_call(kernel, out_shape=tuple(outs), in_specs=[smem()] * len(sca...  114 us
    dot_general x38, matrix products, product(): lax.dot_general(left, right, (((left_dim,), (right_dim,)), ((), ())), pre...  85.9 us
    convert_element_type x20, other arithmetic, low(): return value.astype(LOW)  20.9 us
    unnamed x331, local copies, waits for them, and re-layouts  15.8 us
  transfers between devices with their start and end apart: 117, of which 57 were waited for; matrix products, arithmetic and copies ran while one was open for 22% of the time, Pallas kernels for 13%

profile of v2, /device:TPU:0, one launch (start us, length us, event | category | flops | bytes accessed | tf_op | source)
XLA Modules:
  0.0 691.4 jit_solution(5996727564134827780)
XLA Ops:
  11.3 5.1 collective-permute-start.2
  22.3 9.0 %collective-permute-start = (bf16[136,768]{1,0:T(8,128)(2,1)}, bf16[136,768]{1,0:T(8,128)(2,1)S(1)}, u32[]{:S(2)}, u32[]{:S(2)}) collective-permute-start(bf16[136,768]{1,0:T(8,128)(2,1)} %shard_map.392.refs_0_), channel_id=1, source_target_pairs={{0,8},{4,12},{8,0},{12,4},{16,24},{20,28},{24,16},{28,20},{1,9},{5... | collective-permute-start | bytes 626696 | tf_op jit(solution)/shard_map/ppermute | solution.py:21
  34.4 4.3 collective-permute-done.refs_2_
  47.6 8.8 %shard_map.395 = (bf16[4,128,768]{2,1,0:T(8,128)(2,1)}, bf16[128,256]{1,0:T(8,128)(2,1)}, bf16[128,256]{1,0:T(8,128)(2,1)}, bf16[128,256]{1,0:T(8,128)(2,1)}, bf...) custom-call(s32[4]{0:T(128)} %gather_fusion, ...), custom_call_target="tpu_custom_call" | custom-call | flops 805306368 | bytes 4722688 | tf_op jit(solution)/shard_map/pallas_call | solution.py:40
  75.9 6.4 collective-permute-done.15.refs_3_
  82.3 15.1 %collective-permute-done.14.refs_2_ = bf16[128,1024]{1,0:T(8,128)(2,1)S(1)} collective-permute-done((bf16[128,1024]{1,0:T(8,128)(2,1)S(1)}, bf16[128,1024]{1,0:T(8,128)(2,1)S(1)}, u32[]{:S(2)}, u32[]{:S(2)}) %collective-permute-start.14) | collective-permute-done | bytes 262176 | tf_op jit(solution)/shard_map/ppermute | solution.py:21
  112.5 5.5 collective-permute-done.22.refs_3_
  117.9 7.5 %collective-permute-done.21.refs_2_ = bf16[192,1024]{1,0:T(8,128)(2,1)S(1)} collective-permute-done((bf16[192,1024]{1,0:T(8,128)(2,1)S(1)}, bf16[192,1024]{1,0:T(8,128)(2,1)S(1)}, u32[]{:S(2)}, u32[]{:S(2)}) %collective-permute-start.21) | collective-permute-done | bytes 393248 | tf_op jit(solution)/shard_map/ppermute | solution.py:21
  129.9 5.5 multiply_convert_fusion.4
  141.6 7.8 %collective-permute-done.23 = bf16[192,1024]{1,0:T(8,128)(2,1)S(1)} collective-permute-done((bf16[192,1024]{1,0:T(8,128)(2,1)S(1)}, bf16[192,1024]{1,0:T(8,128)(2,1)S(1)}, u32[]{:S(2)}, u32[]{:S(2)}) %collective-permute-start.23) | collective-permute-done | bytes 393248 | tf_op jit(solution)/shard_map/ppermute | solution.py:21
  149.3 8.5 %collective-permute-done.25 = bf16[192,1024]{1,0:T(8,128)(2,1)S(1)} collective-permute-done((bf16[192,1024]{1,0:T(8,128)(2,1)S(1)}, bf16[192,1024]{1,0:T(8,128)(2,1)S(1)}, u32[]{:S(2)}, u32[]{:S(2)}) %collective-permute-start.25) | collective-permute-done | bytes 393248 | tf_op jit(solution)/shard_map/ppermute | solution.py:21
  170.2 20.9 %collective-permute-done.27 = bf16[128,1024]{1,0:T(8,128)(2,1)S(1)} collective-permute-done((bf16[128,1024]{1,0:T(8,128)(2,1)}, bf16[128,1024]{1,0:T(8,128)(2,1)S(1)}, u32[]{:S(2)}, u32[]{:S(2)}) %collective-permute-start.27) | collective-permute-done | bytes 262176 | tf_op jit(solution)/shard_map/ppermute | solution.py:21
  191.1 7.3 %collective-permute-done.28 = bf16[128,1024]{1,0:T(8,128)(2,1)S(1)} collective-permute-done((bf16[128,1024]{1,0:T(8,128)(2,1)}, bf16[128,1024]{1,0:T(8,128)(2,1)S(1)}, u32[]{:S(2)}, u32[]{:S(2)}) %collective-permute-start.28) | collective-permute-done | bytes 262176 | tf_op jit(solution)/shard_map/ppermute | solution.py:21
  213.5 4.4 collective-permute-done.31.refs_2_
  217.9 8.0 %shard_map.401 = (bf16[4,128,768]{2,1,0:T(8,128)(2,1)}, bf16[128,256]{1,0:T(8,128)(2,1)}, bf16[128,256]{1,0:T(8,128)(2,1)}, bf16[128,256]{1,0:T(8,128)(2,1)}, bf16[128,256]{1,0:T(8,128)(2,1)}) custom-call(s32[4]{0:T(128)} %gather_fusion, bf16[128,1024]{1,0:T(8,128)(2,1)} %copy-done.59, bf16[128,1024]{1,0:T(8,128)(2,1)} %collective-permute-done.30.refs_1_, ...), custom_call_target="tpu_custom_call" | custom-call | flops 805306368 | bytes 3670016 | tf_op jit(solution)/shard_map/pallas_call | solution.py:40
  244.7 6.2 collective-permute-start.37
  258.8 9.0 %collective-permute-done.37.refs_2_ = bf16[128,1024]{1,0:T(8,128)(2,1)} collective-permute-done((bf16[128,1024]{1,0:T(8,128)(2,1)S(1)}, bf16[128,1024]{1,0:T(8,128)(2,1)}, u32[]{:S(2)}, u32[]{:S(2)}) %collective-permute-start.37) | collective-permute-done | bytes 262176 | tf_op jit(solution)/shard_map/ppermute | solution.py:21
  268.4 5.9 fusion.6
  285.6 3.4 fusion.51
  289.1 4.3 collective-permute-done.46.refs_1_
  299.1 4.4 fusion.69.down_ref
  352.0 7.5 %fusion.72 = f32[2048,1024]{1,0:T(8,128)} fusion(bf16[384,2048]{1,0:T(8,128)(2,1)} %copy-done.45, bf16[384,1024]{1,0:T(8,128)(2,1)} %shard_map.403, f32[384]{0:T(512)S(1)} %reduce.2), kind=kOutput, calls=%fused_computation.124 | convolution fusion | flops 1611792384 | bytes 10749440 | tf_op jit(solution)/shard_map/dot_general | solution.py:25
  361.6 7.6 %collective-permute-done.54 = bf16[128,1024]{1,0:T(8,128)(2,1)} collective-permute-done((bf16[128,1024]{1,0:T(8,128)(2,1)}, bf16[128,1024]{1,0:T(8,128)(2,1)}, u32[]{:S(2)}, u32[]{:S(2)}) %collective-permute-start.54) | collective-permute-done | bytes 262176 | tf_op jit(solution)/shard_map/ppermute | solution.py:21
  384.5 9.7 %shard_map.409.grad_ref.refs_4_ = bf16[512,768]{1,0:T(8,128)(2,1)} custom-call(s32[4]{0:T(128)} %gather_fusion, bf16[4,128,768]{2,1,0:T(8,128)(2,1)} %get-tuple-element.263.packed_ref, bf16[128,256]{1,0:T(8,128)(2,1)} %get-tuple-element.264.refs_0_, bf16[128,256]{1,0:T(8,128)(2,1)} %copy-done.118, bf16[128,256]{1,0:T(8,128)(2,1)} %copy-done.119, ...), custom_call_target="tpu_custom_call" | custom-call | bytes 1835008 | tf_op jit(solution)/shard_map/pallas_call | solution.py:40
  394.2 3.5 shard_map.410
  407.0 3.8 collective-permute-done.63
  416.2 5.4 collective-permute-start.66
  430.6 11.3 %collective-permute-done.66.refs_2_ = bf16[128,1024]{1,0:T(8,128)(2,1)} collective-permute-done((bf16[128,1024]{1,0:T(8,128)(2,1)}, bf16[128,1024]{1,0:T(8,128)(2,1)}, u32[]{:S(2)}, u32[]{:S(2)}) %collective-permute-start.66) | collective-permute-done | bytes 262176 | tf_op jit(solution)/shard_map/ppermute | solution.py:21
  442.4 7.2 %fusion.189 = f32[1024,2048]{1,0:T(8,128)} fusion(bf16[384,1024]{1,0:T(8,128)(2,1)S(1)} %copy-done.14, bf16[384,2048]{1,0:T(8,128)(2,1)} %copy-done.22), kind=kOutput, calls=%fused_computation.355 | convolution fusion | flops 1610612736 | bytes 10747904 | tf_op jit(solution)/shard_map/dot_general | solution.py:25
  458.5 5.8 multiply_reduce_fusion.5
  464.4 3.7 shard_map.415
  468.1 5.0 shard_map.414
  478.9 4.6 multiply_reduce_fusion.3
  496.3 3.9 collective-permute-done.75
  500.2 7.8 %collective-permute-done.77 = bf16[192,1024]{1,0:T(8,128)(2,1)S(1)} collective-permute-done((bf16[192,1024]{1,0:T(8,128)(2,1)S(1)}, bf16[192,1024]{1,0:T(8,128)(2,1)S(1)}, u32[]{:S(2)}, u32[]{:S(2)}) %collective-permute-start.77) | collective-permute-done | bytes 393248 | tf_op jit(solution)/shard_map/ppermute | solution.py:21
  524.2 5.8 fusion.66
  530.1 3.9 fusion.190
  533.9 5.6 collective-permute-done.80
  540.5 6.5 collective-permute-done.82
  568.9 9.8 %shard_map.419.refs_4_.grad_ref = bf16[512,768]{1,0:T(8,128)(2,1)} custom-call(s32[4]{0:T(128)} %gather_fusion, bf16[4,128,768]{2,1,0:T(8,128)(2,1)} %get-tuple-element.344.packed_ref, bf16[128,256]{1,0:T(8,128)(2,1)} %get-tuple-element.331.refs_0_, bf16[128,256]{1,0:T(8,128)(2,1)} %copy-done.115, bf16[128,256]{1,0:T(8,128)(2,1)} %copy-done.116, ...), custom_call_target="tpu_custom_call" | custom-call | bytes 1835008 | tf_op jit(solution)/shard_map/pallas_call | solution.py:40
  583.7 3.9 shard_map.420
  590.4 3.5 shard_map.421
  604.5 5.3 collective-permute-done.95
  611.1 15.0 %collective-permute-done.92 = bf16[256,768]{1,0:T(8,128)(2,1)S(1)} collective-permute-done((bf16[256,768]{1,0:T(8,128)(2,1)S(1)}, bf16[256,768]{1,0:T(8,128)(2,1)S(1)}, u32[]{:S(2)}, u32[]{:S(2)}) %collective-permute-start.92) | collective-permute-done | bytes 393248 | tf_op jit(solution)/shard_map/ppermute | solution.py:21
  630.6 8.7 %collective-permute-done.93 = bf16[128,768]{1,0:T(8,128)(2,1)} collective-permute-done((bf16[128,768]{1,0:T(8,128)(2,1)}, bf16[128,768]{1,0:T(8,128)(2,1)}, u32[]{:S(2)}, u32[]{:S(2)}) %collective-permute-start.93) | collective-permute-done | bytes 196640 | tf_op jit(solution)/shard_map/ppermute | solution.py:21
  657.7 4.7 collective-permute-done.101
  666.6 3.5 collective-permute-done.102.refs_1_
  681.3 3.2 convert_add_fusion
  (746 shorter events, 351.5 us)
Async XLA Ops:
  7.2 60.8 %all-gather.7.cloned.1.call-start = ((), (), s32[]{:S(2)}) async-start(), calls=%async_computation.3 | async-start | bytes 2359296 | tf_op jit(solution)/shard_map/all_gather | solution.py:264
  16.3 22.4 %collective-permute-start.4 = (bf16[128,1024]{1,0:T(8,128)(2,1)}, bf16[128,1024]{1,0:T(8,128)(2,1)S(1)}, u32[]{:S(2)}, u32[]{:S(2)}) collective-permute-start(bf16[128,1024]{1,0:T(8,128)(2,1)} %refs_0_), channel_id=1, source_target_pairs={{0,2},{1,3},{2,0},{3,1},{4,6},{5,7},{6,4},{7,5},{8,10},{9,11},{10,... | collective-permute-start | bytes 786440 | tf_op jit(solution)/shard_map/ppermute | solution.py:21
  17.9 20.9 %collective-permute-start.3 = (bf16[128,1024]{1,0:T(8,128)(2,1)}, bf16[128,1024]{1,0:T(8,128)(2,1)S(1)}, u32[]{:S(2)}, u32[]{:S(2)}) collective-permute-start(bf16[128,1024]{1,0:T(8,128)(2,1)} %refs_0_), channel_id=1, source_target_pairs={{0,1},{1,0},{2,3},{3,2},{4,5},{5,4},{6,7},{7,6},{8,9},{9,8},{10,11... | collective-permute-start | bytes 786440 | tf_op jit(solution)/shard_map/ppermute | solution.py:21
  19.4 19.4 %collective-permute-start.5 = (bf16[128,1024]{1,0:T(8,128)(2,1)}, bf16[128,1024]{1,0:T(8,128)(2,1)}, u32[]{:S(2)}, u32[]{:S(2)}) collective-permute-start(bf16[128,1024]{1,0:T(8,128)(2,1)} %refs_0_), channel_id=1, source_target_pairs={{0,3},{1,2},{2,1},{3,0},{4,7},{5,6},{6,5},{7,4},{8,11},{9,10},{10,... | collective-permute-start | bytes 786440 | tf_op jit(solution)/shard_map/ppermute | solution.py:21
  22.3 16.4 %collective-permute-start = (bf16[136,768]{1,0:T(8,128)(2,1)}, bf16[136,768]{1,0:T(8,128)(2,1)S(1)}, u32[]{:S(2)}, u32[]{:S(2)}) collective-permute-start(bf16[136,768]{1,0:T(8,128)(2,1)} %shard_map.392.refs_0_), channel_id=1, source_target_pairs={{0,8},{4,12},{8,0},{12,4},{16,24},{20,28},{24,16},{28,20},{1,9},{5... | collective-permute-start | bytes 626696 | tf_op jit(solution)/shard_map/ppermute | solution.py:21
  38.8 168.0 %all-gather.9.cloned.1.call-start = ((), (), s32[]{:S(2)}) async-start(), calls=%async_computation.4 | async-start | bytes 2359296 | tf_op jit(solution)/shard_map/all_gather | solution.py:264
  73.0 24.4 %collective-permute-start.14 = (bf16[128,1024]{1,0:T(8,128)(2,1)S(1)}, bf16[128,1024]{1,0:T(8,128)(2,1)S(1)}, u32[]{:S(2)}, u32[]{:S(2)}) collective-permute-start(bf16[128,1024]{1,0:T(8,128)(2,1)S(1)} %multiply_convert_fusion.16.refs_0_), channel_id=1, source_target_pairs={{0,16},{4,20},{8,24},{12,28},{16,0},{20,4},{24,8},{28,12},{1,17},{... | collective-permute-start | bytes 786440 | tf_op jit(solution)/shard_map/ppermute | solution.py:21
  74.1 23.3 %collective-permute-start.13 = (bf16[128,1024]{1,0:T(8,128)(2,1)S(1)}, bf16[128,1024]{1,0:T(8,128)(2,1)}, u32[]{:S(2)}, u32[]{:S(2)}) collective-permute-start(bf16[128,1024]{1,0:T(8,128)(2,1)S(1)} %multiply_convert_fusion.16.refs_0_), channel_id=1, source_target_pairs={{0,8},{4,12},{8,0},{12,4},{16,24},{20,28},{24,16},{28,20},{1,9},{5... | collective-permute-start | bytes 786440 | tf_op jit(solution)/shard_map/ppermute | solution.py:21
  75.8 22.1 %collective-permute-start.16 = (bf16[128,1024]{1,0:T(8,128)(2,1)S(1)}, bf16[128,1024]{1,0:T(8,128)(2,1)S(1)}, u32[]{:S(2)}, u32[]{:S(2)}) collective-permute-start(bf16[128,1024]{1,0:T(8,128)(2,1)S(1)} %multiply_convert_fusion.16.refs_0_), channel_id=1, source_target_pairs={{0,4},{4,0},{8,12},{12,8},{16,20},{20,16},{24,28},{28,24},{1,5},{5... | collective-permute-start | bytes 786440 | tf_op jit(solution)/shard_map/ppermute | solution.py:21
  107.4 18.1 %collective-permute-start.21 = (bf16[192,1024]{1,0:T(8,128)(2,1)S(1)}, bf16[192,1024]{1,0:T(8,128)(2,1)S(1)}, u32[]{:S(2)}, u32[]{:S(2)}) collective-permute-start(bf16[192,1024]{1,0:T(8,128)(2,1)S(1)} %convolution_convert_fusion.3.refs_0_), channel_id=1, source_target_pairs={{0,2},{1,3},{2,0},{3,1},{4,6},{5,7},{6,4},{7,5},{8,10},{9,11},{10,... | collective-permute-start | bytes 1179656 | tf_op jit(solution)/shard_map/ppermute | solution.py:21
  107.9 17.7 %collective-permute-start.20 = (bf16[192,1024]{1,0:T(8,128)(2,1)S(1)}, bf16[192,1024]{1,0:T(8,128)(2,1)}, u32[]{:S(2)}, u32[]{:S(2)}) collective-permute-start(bf16[192,1024]{1,0:T(8,128)(2,1)S(1)} %convolution_convert_fusion.3.refs_0_), channel_id=1, source_target_pairs={{0,1},{1,0},{2,3},{3,2},{4,5},{5,4},{6,7},{7,6},{8,9},{9,8},{10,11... | collective-permute-start | bytes 1179656 | tf_op jit(solution)/shard_map/ppermute | solution.py:21
  128.9 89.0 %all-gather.11.cloned.1.call-start = ((), (), s32[]{:S(2)}) async-start(), calls=%async_computation.5 | async-start | bytes 1769472 | tf_op jit(solution)/shard_map/all_gather | solution.py:264
  129.6 106.2 %all-gather.13.cloned.1.call-start = ((), (), s32[]{:S(2)}) async-start(), calls=%async_computation.6 | async-start | bytes 2359296 | tf_op jit(solution)/shard_map/all_gather | solution.py:264
  138.8 19.0 %collective-permute-start.25 = (bf16[192,1024]{1,0:T(8,128)(2,1)S(1)}, bf16[192,1024]{1,0:T(8,128)(2,1)S(1)}, u32[]{:S(2)}, u32[]{:S(2)}) collective-permute-start(bf16[192,1024]{1,0:T(8,128)(2,1)S(1)} %get-tuple-element.421), channel_id=1, source_target_pairs={{0,3},{1,2},{2,1},{3,0},{4,7},{5,6},{6,5},{7,4},{8,11},{9,10},{10,... | collective-permute-start | bytes 1179656 | tf_op jit(solution)/shard_map/ppermute | solution.py:21
  140.3 18.9 %collective-permute-start.24 = (bf16[192,1024]{1,0:T(8,128)(2,1)S(1)}, bf16[192,1024]{1,0:T(8,128)(2,1)S(1)}, u32[]{:S(2)}, u32[]{:S(2)}) collective-permute-start(bf16[192,1024]{1,0:T(8,128)(2,1)S(1)} %get-tuple-element.422), channel_id=1, source_target_pairs={{0,2},{1,3},{2,0},{3,1},{4,6},{5,7},{6,4},{7,5},{8,10},{9,11},{10,... | collective-permute-start | bytes 1179656 | tf_op jit(solution)/shard_map/ppermute | solution.py:21
  165.8 25.3 %collective-permute-start.27 = (bf16[128,1024]{1,0:T(8,128)(2,1)}, bf16[128,1024]{1,0:T(8,128)(2,1)S(1)}, u32[]{:S(2)}, u32[]{:S(2)}) collective-permute-start(bf16[128,1024]{1,0:T(8,128)(2,1)} %get-tuple-element.219), channel_id=1, source_target_pairs={{0,8},{4,12},{8,0},{12,4},{16,24},{20,28},{24,16},{28,20},{1,9},{5... | collective-permute-start | bytes 786440 | tf_op jit(solution)/shard_map/ppermute | solution.py:21
  165.8 32.7 %collective-permute-start.28 = (bf16[128,1024]{1,0:T(8,128)(2,1)}, bf16[128,1024]{1,0:T(8,128)(2,1)S(1)}, u32[]{:S(2)}, u32[]{:S(2)}) collective-permute-start(bf16[128,1024]{1,0:T(8,128)(2,1)} %get-tuple-element.220), channel_id=1, source_target_pairs={{0,16},{4,20},{8,24},{12,28},{16,0},{20,4},{24,8},{28,12},{1,17},{... | collective-permute-start | bytes 786440 | tf_op jit(solution)/shard_map/ppermute | solution.py:21
  168.2 30.3 %collective-permute-start.29 = (bf16[128,1024]{1,0:T(8,128)(2,1)}, bf16[128,1024]{1,0:T(8,128)(2,1)S(1)}, u32[]{:S(2)}, u32[]{:S(2)}) collective-permute-start(bf16[128,1024]{1,0:T(8,128)(2,1)} %get-tuple-element.221), channel_id=1, source_target_pairs={{0,24},{4,28},{8,16},{12,20},{16,8},{20,12},{24,0},{28,4},{1,25},{... | collective-permute-start | bytes 786440 | tf_op jit(solution)/shard_map/ppermute | solution.py:21
  199.8 194.4 %reduce-scatter.4.cloned.1.call-start = ((), (), s32[]{:S(2)}) async-start(), calls=%async_computation.7 | async-start | bytes 2621440 | tf_op jit(solution)/shard_map/reduce_scatter | solution.py:242
  244.7 23.1 %collective-permute-start.37 = (bf16[128,1024]{1,0:T(8,128)(2,1)S(1)}, bf16[128,1024]{1,0:T(8,128)(2,1)}, u32[]{:S(2)}, u32[]{:S(2)}) collective-permute-start(bf16[128,1024]{1,0:T(8,128)(2,1)S(1)} %multiply_convert_fusion.14.refs_0_), channel_id=1, source_target_pairs={{0,16},{4,20},{8,24},{12,28},{16,0},{20,4},{24,8},{28,12},{1,17},{... | collective-permute-start | bytes 786440 | tf_op jit(solution)/shard_map/ppermute | solution.py:21
  251.6 16.2 %collective-permute-start.36 = (bf16[128,1024]{1,0:T(8,128)(2,1)S(1)}, bf16[128,1024]{1,0:T(8,128)(2,1)S(1)}, u32[]{:S(2)}, u32[]{:S(2)}) collective-permute-start(bf16[128,1024]{1,0:T(8,128)(2,1)S(1)} %multiply_convert_fusion.14.refs_0_), channel_id=1, source_target_pairs={{0,8},{4,12},{8,0},{12,4},{16,24},{20,28},{24,16},{28,20},{1,9},{5... | collective-permute-start | bytes 786440 | tf_op jit(solution)/shard_map/ppermute | solution.py:21
  256.0 18.3 %collective-permute-start.42 = (bf16[128,1024]{1,0:T(8,128)(2,1)S(1)}, bf16[128,1024]{1,0:T(8,128)(2,1)}, u32[]{:S(2)}, u32[]{:S(2)}) collective-permute-start(bf16[128,1024]{1,0:T(8,128)(2,1)S(1)} %multiply_convert_fusion.14.refs_0_), channel_id=1, source_target_pairs={{0,4},{4,0},{8,12},{12,8},{16,20},{20,16},{24,28},{28,24},{1,5},{5... | collective-permute-start | bytes 786440 | tf_op jit(solution)/shard_map/ppermute | solution.py:21
  327.0 52.9 %collective-permute-start.60 = (bf16[96,1024]{1,0:T(8,128)(2,1)}, bf16[96,1024]{1,0:T(8,128)(2,1)}, u32[]{:S(2)}, u32[]{:S(2)}) collective-permute-start(bf16[96,1024]{1,0:T(8,128)(2,1)} %get-tuple-element.423), channel_id=1, source_target_pairs={{0,2},{1,3},{2,0},{3,1},{4,6},{5,7},{6,4},{7,5},{8,10},{9,11},{10,... | collective-permute-start | bytes 589832 | tf_op jit(solution)/shard_map/ppermute | solution.py:21
  328.4 51.5 %collective-permute-start.61 = (bf16[96,1024]{1,0:T(8,128)(2,1)}, bf16[96,1024]{1,0:T(8,128)(2,1)}, u32[]{:S(2)}, u32[]{:S(2)}) collective-permute-start(bf16[96,1024]{1,0:T(8,128)(2,1)} %get-tuple-element.424), channel_id=1, source_target_pairs={{0,3},{1,2},{2,1},{3,0},{4,7},{5,6},{6,5},{7,4},{8,11},{9,10},{10,... | collective-permute-start | bytes 589832 | tf_op jit(solution)/shard_map/ppermute | solution.py:21
  337.0 112.6 %all-gather.15.cloned.1.call-start = ((), (), s32[]{:S(2)}) async-start(), calls=%async_computation.8 | async-start | bytes 2621440 | tf_op jit(solution)/shard_map/all_gather | solution.py:246
  347.5 21.7 %collective-permute-start.54 = (bf16[128,1024]{1,0:T(8,128)(2,1)}, bf16[128,1024]{1,0:T(8,128)(2,1)}, u32[]{:S(2)}, u32[]{:S(2)}) collective-permute-start(bf16[128,1024]{1,0:T(8,128)(2,1)} %get-tuple-element.256), channel_id=1, source_target_pairs={{0,16},{4,20},{8,24},{12,28},{16,0},{20,4},{24,8},{28,12},{1,17},{... | collective-permute-start | bytes 786440 | tf_op jit(solution)/shard_map/ppermute | solution.py:21
  350.1 19.1 %collective-permute-start.55 = (bf16[128,1024]{1,0:T(8,128)(2,1)}, bf16[128,1024]{1,0:T(8,128)(2,1)}, u32[]{:S(2)}, u32[]{:S(2)}) collective-permute-start(bf16[128,1024]{1,0:T(8,128)(2,1)} %get-tuple-element.257), channel_id=1, source_target_pairs={{0,24},{4,28},{8,16},{12,20},{16,8},{20,12},{24,0},{28,4},{1,25},{... | collective-permute-start | bytes 786440 | tf_op jit(solution)/shard_map/ppermute | solution.py:21
  405.5 144.2 %reduce-scatter.6.cloned.1.call-start = ((), (), s32[]{:S(2)}) async-start(), calls=%async_computation.9 | async-start | bytes 4128768 | tf_op jit(solution)/shard_map/reduce_scatter | solution.py:823
  414.2 35.4 %collective-permute-start.68 = (bf16[128,1024]{1,0:T(8,128)(2,1)}, bf16[128,1024]{1,0:T(8,128)(2,1)}, u32[]{:S(2)}, u32[]{:S(2)}) collective-permute-start(bf16[128,1024]{1,0:T(8,128)(2,1)} %get-tuple-element.281.refs_0_), channel_id=1, source_target_pairs={{0,4},{4,0},{8,12},{12,8},{16,20},{20,16},{24,28},{28,24},{1,5},{5... | collective-permute-start | bytes 786440 | tf_op jit(solution)/shard_map/ppermute | solution.py:21
  414.2 16.4 %collective-permute-start.67 = (bf16[128,1024]{1,0:T(8,128)(2,1)}, bf16[128,1024]{1,0:T(8,128)(2,1)}, u32[]{:S(2)}, u32[]{:S(2)}) collective-permute-start(bf16[128,1024]{1,0:T(8,128)(2,1)} %get-tuple-element.281.refs_0_), channel_id=1, source_target_pairs={{0,24},{4,28},{8,16},{12,20},{16,8},{20,12},{24,0},{28,4},{1,25},{... | collective-permute-start | bytes 786440 | tf_op jit(solution)/shard_map/ppermute | solution.py:21
  416.2 25.6 %collective-permute-start.66 = (bf16[128,1024]{1,0:T(8,128)(2,1)}, bf16[128,1024]{1,0:T(8,128)(2,1)}, u32[]{:S(2)}, u32[]{:S(2)}) collective-permute-start(bf16[128,1024]{1,0:T(8,128)(2,1)} %get-tuple-element.281.refs_0_), channel_id=1, source_target_pairs={{0,16},{4,20},{8,24},{12,28},{16,0},{20,4},{24,8},{28,12},{1,17},{... | collective-permute-start | bytes 786440 | tf_op jit(solution)/shard_map/ppermute | solution.py:21
  421.7 20.3 %collective-permute-start.65 = (bf16[128,1024]{1,0:T(8,128)(2,1)}, bf16[128,1024]{1,0:T(8,128)(2,1)}, u32[]{:S(2)}, u32[]{:S(2)}) collective-permute-start(bf16[128,1024]{1,0:T(8,128)(2,1)} %get-tuple-element.281.refs_0_), channel_id=1, source_target_pairs={{0,8},{4,12},{8,0},{12,4},{16,24},{20,28},{24,16},{28,20},{1,9},{5... | collective-permute-start | bytes 786440 | tf_op jit(solution)/shard_map/ppermute | solution.py:21
  430.6 19.0 %collective-permute-start.71 = (bf16[128,1024]{1,0:T(8,128)(2,1)}, bf16[128,1024]{1,0:T(8,128)(2,1)}, u32[]{:S(2)}, u32[]{:S(2)}) collective-permute-start(bf16[128,1024]{1,0:T(8,128)(2,1)} %collective-permute-done.67.refs_3_), channel_id=1, source_target_pairs={{0,4},{4,0},{8,12},{12,8},{16,20},{20,16},{24,28},{28,24},{1,5},{5... | collective-permute-start | bytes 786440 | tf_op jit(solution)/shard_map/ppermute | solution.py:21
  454.9 18.2 %collective-permute-start.74 = (bf16[192,1024]{1,0:T(8,128)(2,1)S(1)}, bf16[192,1024]{1,0:T(8,128)(2,1)S(1)}, u32[]{:S(2)}, u32[]{:S(2)}) collective-permute-start(bf16[192,1024]{1,0:T(8,128)(2,1)S(1)} %convolution_convert_fusion.2.refs_0_), channel_id=1, source_target_pairs={{0,3},{1,2},{2,1},{3,0},{4,7},{5,6},{6,5},{7,4},{8,11},{9,10},{10,... | collective-permute-start | bytes 1179656 | tf_op jit(solution)/shard_map/ppermute | solution.py:21
  456.4 19.1 %collective-permute-start.73 = (bf16[192,1024]{1,0:T(8,128)(2,1)S(1)}, bf16[192,1024]{1,0:T(8,128)(2,1)}, u32[]{:S(2)}, u32[]{:S(2)}) collective-permute-start(bf16[192,1024]{1,0:T(8,128)(2,1)S(1)} %convolution_convert_fusion.2.refs_0_), channel_id=1, source_target_pairs={{0,2},{1,3},{2,0},{3,1},{4,6},{5,7},{6,4},{7,5},{8,10},{9,11},{10,... | collective-permute-start | bytes 1179656 | tf_op jit(solution)/shard_map/ppermute | solution.py:21
  457.3 18.2 %collective-permute-start.72 = (bf16[192,1024]{1,0:T(8,128)(2,1)S(1)}, bf16[192,1024]{1,0:T(8,128)(2,1)}, u32[]{:S(2)}, u32[]{:S(2)}) collective-permute-start(bf16[192,1024]{1,0:T(8,128)(2,1)S(1)} %convolution_convert_fusion.2.refs_0_), channel_id=1, source_target_pairs={{0,1},{1,0},{2,3},{3,2},{4,5},{5,4},{6,7},{7,6},{8,9},{9,8},{10,11... | collective-permute-start | bytes 1179656 | tf_op jit(solution)/shard_map/ppermute | solution.py:21
  478.2 195.2 %all-gather.17.cloned.1.call-start = ((), (), s32[]{:S(2)}) async-start(), calls=%async_computation.11 | async-start | bytes 2293760 | tf_op jit(solution)/shard_map/all_gather | solution.py:246
  489.1 19.0 %collective-permute-start.77 = (bf16[192,1024]{1,0:T(8,128)(2,1)S(1)}, bf16[192,1024]{1,0:T(8,128)(2,1)S(1)}, u32[]{:S(2)}, u32[]{:S(2)}) collective-permute-start(bf16[192,1024]{1,0:T(8,128)(2,1)S(1)} %get-tuple-element.418), channel_id=1, source_target_pairs={{0,3},{1,2},{2,1},{3,0},{4,7},{5,6},{6,5},{7,4},{8,11},{9,10},{10,... | collective-permute-start | bytes 1179656 | tf_op jit(solution)/shard_map/ppermute | solution.py:21
  490.5 18.9 %collective-permute-start.76 = (bf16[192,1024]{1,0:T(8,128)(2,1)S(1)}, bf16[192,1024]{1,0:T(8,128)(2,1)S(1)}, u32[]{:S(2)}, u32[]{:S(2)}) collective-permute-start(bf16[192,1024]{1,0:T(8,128)(2,1)S(1)} %get-tuple-element.419), channel_id=1, source_target_pairs={{0,2},{1,3},{2,0},{3,1},{4,6},{5,7},{6,4},{7,5},{8,10},{9,11},{10,... | collective-permute-start | bytes 1179656 | tf_op jit(solution)/shard_map/ppermute | solution.py:21
  517.9 21.6 %collective-permute-start.80 = (bf16[128,1024]{1,0:T(8,128)(2,1)}, bf16[128,1024]{1,0:T(8,128)(2,1)S(1)}, u32[]{:S(2)}, u32[]{:S(2)}) collective-permute-start(bf16[128,1024]{1,0:T(8,128)(2,1)} %get-tuple-element.309), channel_id=1, source_target_pairs={{0,16},{4,20},{8,24},{12,28},{16,0},{20,4},{24,8},{28,12},{1,17},{... | collective-permute-start | bytes 786440 | tf_op jit(solution)/shard_map/ppermute | solution.py:21
  520.2 19.3 %collective-permute-start.81 = (bf16[128,1024]{1,0:T(8,128)(2,1)}, bf16[128,1024]{1,0:T(8,128)(2,1)S(1)}, u32[]{:S(2)}, u32[]{:S(2)}) collective-permute-start(bf16[128,1024]{1,0:T(8,128)(2,1)} %get-tuple-element.310), channel_id=1, source_target_pairs={{0,24},{4,28},{8,16},{12,20},{16,8},{20,12},{24,0},{28,4},{1,25},{... | collective-permute-start | bytes 786440 | tf_op jit(solution)/shard_map/ppermute | solution.py:21
  522.3 24.7 %collective-permute-start.82 = (bf16[1024,512]{1,0:T(8,128)(2,1)}, bf16[1024,512]{1,0:T(8,128)(2,1)S(1)}, u32[]{:S(2)}, u32[]{:S(2)}) collective-permute-start(bf16[1024,512]{1,0:T(8,128)(2,1)} %convolution_convert_fusion), channel_id=1, source_target_pairs={{0,1},{1,0},{2,3},{3,2},{4,5},{5,4},{6,7},{7,6},{8,9},{9,8},{10,11... | collective-permute-start | bytes 3145736 | tf_op jit(solution)/shard_map/ppermute | solution.py:21
  523.3 24.9 %collective-permute-start.83 = (bf16[512,1024]{1,0:T(8,128)(2,1)}, bf16[512,1024]{1,0:T(8,128)(2,1)S(1)}, u32[]{:S(2)}, u32[]{:S(2)}) collective-permute-start(bf16[512,1024]{1,0:T(8,128)(2,1)} %fusion.68), channel_id=1, source_target_pairs={{0,2},{1,3},{2,0},{3,1},{4,6},{5,7},{6,4},{7,5},{8,10},{9,11},{10,... | collective-permute-start | bytes 3145736 | tf_op jit(solution)/shard_map/ppermute | solution.py:21
  549.7 123.7 %reduce-scatter.8.cloned.1.call-start = ((), (), s32[]{:S(2)}) async-start(), calls=%async_computation.10 | async-start | bytes 2359296 | tf_op jit(solution)/shard_map/reduce_scatter | solution.py:836
  598.8 27.3 %collective-permute-start.92 = (bf16[256,768]{1,0:T(8,128)(2,1)S(1)}, bf16[256,768]{1,0:T(8,128)(2,1)S(1)}, u32[]{:S(2)}, u32[]{:S(2)}) collective-permute-start(bf16[256,768]{1,0:T(8,128)(2,1)S(1)} %slice.565), channel_id=1, source_target_pairs={{0,8},{4,12},{8,0},{12,4},{16,24},{20,28},{24,16},{28,20},{1,9},{5... | collective-permute-start | bytes 1179656 | tf_op jit(solution)/shard_map/ppermute | solution.py:21
  601.2 72.2 %collective-permute-start.88 = (bf16[1024,512]{1,0:T(8,128)(2,1)}, bf16[1024,512]{1,0:T(8,128)(2,1)}, u32[]{:S(2)}, u32[]{:S(2)}) collective-permute-start(bf16[1024,512]{1,0:T(8,128)(2,1)} %add_convert_fusion.1), channel_id=1, source_target_pairs={{0,2},{1,3},{2,0},{3,1},{4,6},{5,7},{6,4},{7,5},{8,10},{9,11},{10,... | collective-permute-start | bytes 3145736 | tf_op jit(solution)/shard_map/ppermute | solution.py:21
  603.3 70.1 %collective-permute-start.89 = (bf16[512,1024]{1,0:T(8,128)(2,1)}, bf16[512,1024]{1,0:T(8,128)(2,1)}, u32[]{:S(2)}, u32[]{:S(2)}) collective-permute-start(bf16[512,1024]{1,0:T(8,128)(2,1)} %add_convert_fusion), channel_id=1, source_target_pairs={{0,1},{1,0},{2,3},{3,2},{4,5},{5,4},{6,7},{7,6},{8,9},{9,8},{10,11... | collective-permute-start | bytes 3145736 | tf_op jit(solution)/shard_map/ppermute | solution.py:21
  609.8 32.3 %collective-permute-start.105 = (bf16[128,1024]{1,0:T(8,128)(2,1)}, bf16[128,1024]{1,0:T(8,128)(2,1)}, u32[]{:S(2)}, u32[]{:S(2)}) collective-permute-start(bf16[128,1024]{1,0:T(8,128)(2,1)} %slice.566), channel_id=1, source_target_pairs={{0,16},{4,20},{8,24},{12,28},{16,0},{20,4},{24,8},{28,12},{1,17},{... | collective-permute-start | bytes 786440 | tf_op jit(solution)/shard_map/ppermute | solution.py:21
  (234 other events, 2689.3 us)
Sparse Core Ops, SparseCore 0:
  38.9 29.0 all-gather.6
  129.0 27.8 all-gather.8
  159.1 42.7 all-gather.10
  203.3 29.8 all-gather.12
  337.1 33.8 reduce-scatter.3
  405.6 38.0 all-gather.14
  478.3 43.6 reduce-scatter.5
  549.8 33.5 all-gather.16
  588.0 43.6 reduce-scatter.7

commit v3 on v2

--- a/solution.py
+++ b/solution.py
@@ -64,26 +64,43 @@
     return call(kernel, [shape((count * rows, columns), pieces[0].dtype)], [], pieces)[0]
 
 
-def pack_columns(pieces, base):
-    count, (rows, columns) = len(pieces), pieces[0].shape
-
-    def kernel(base_ref, *refs):
+def context_back(grads, weight, count, base):
+    slots, features = grads.shape
+    columns = features // count
+
+    def kernel(base_ref, grads_ref, weight_ref, *outs):
         for k in range(count):
             start = pl.multiple_of((base_ref[0] ^ k) * columns, columns)
-            refs[count][:, pl.ds(start, columns)] = refs[k][...]
-
-    return call(kernel, [shape((rows, count * columns), pieces[0].dtype)], [base], pieces)[0]
-
-
-def split_columns(whole, count, base):
-    rows, columns = whole.shape[0], whole.shape[1] // count
-
-    def kernel(base_ref, whole_ref, *outs):
+            outs[k][...] = low(product(grads_ref[...], weight_ref[pl.ds(start, columns), :], 1, 1))
+
+    outs = [shape((slots, columns), LOW)] * count
+    flops = 2 * slots * features * features
+    return call(kernel, outs, [base], [grads, weight], flops=flops)
+
+
+def attended(pieces, weight, source, gain, base):
+    count, (slots, columns) = len(pieces), pieces[0].shape
+    features = source.shape[1]
+
+    def kernel(base_ref, weight_ref, source_ref, gain_ref, *refs):
+        context_ref, middle_ref, second_ref, scaled_ref, inverse_ref = refs[count:]
+        total = source_ref[...]
         for k in range(count):
             start = pl.multiple_of((base_ref[0] ^ k) * columns, columns)
-            outs[k][...] = low(whole_ref[:, pl.ds(start, columns)])
-
-    return call(kernel, [shape((rows, columns), LOW)] * count, [base], [whole])
+            context_ref[:, pl.ds(start, columns)] = refs[k][...]
+            total = total + product(refs[k][...], weight_ref[pl.ds(start, columns), :], 1, 0)
+        middle_ref[...] = total
+        second, scaled, inverse = layer_norm(total, gain_ref[...])
+        second_ref[...] = low(second)
+        scaled_ref[...] = scaled
+        inverse_ref[...] = inverse
+
+    outs = [
+        shape((slots, features), LOW), shape((slots, features), F32), shape((slots, features), LOW),
+        shape((slots, features), F32), shape((slots, 1), F32),
+    ]
+    flops = 2 * slots * features * features
+    return call(kernel, outs, [base], [weight, source, gain[None]] + list(pieces), flops=flops)
 
 
 def own_slab(attention_in, extra, base, below):
@@ -145,13 +162,6 @@
     return call(kernel, [shape((rows, count * triple), F32)], [base], pieces)[0]
 
 
-def narrow_join(own, at_narrow):
-    narrow = lax.axis_size("narrow")
-    return spread_columns(
-        [own] + [swap(own, "narrow", j) for j in range(1, narrow)], at_narrow
-    )
-
-
 def reorder(whole, slots, at_wide, outward):
     count = whole.shape[0] // slots
     order = list(range(0, count, 2)) + list(range(1, count, 2))
@@ -183,46 +193,59 @@
     return call(kernel, outs, [], arrays, flops=flops)[0]
 
 
-def join_pair(gathered, columns):
+def stack_own(dense, pair, columns):
+    units, features = dense.shape
+    rows = pair.shape[0]
+
+    def kernel(dense_ref, pair_ref, out_ref):
+        out_ref[:units, :] = dense_ref[...]
+        out_ref[units : units + rows, :] = pair_ref[:, columns:]
+        out_ref[units + rows :, columns:] = jnp.zeros((rows, features - columns), LOW)
+        out_ref[units + rows :, :columns] = pair_ref[:, :columns]
+
+    return call(kernel, [shape((units + 2 * rows, features), LOW)], [], [dense, pair])[0]
+
+
+def split_gathered(gathered, rows, columns):
     narrow = lax.axis_size("narrow")
-    rows = gathered.shape[0] // narrow
-    features = gathered.shape[1] - columns
+    features = gathered.shape[1]
+    block = gathered.shape[0] // narrow
+    units = block - 2 * rows
+    half = units * narrow // 2
+    fold = features // half
     third = columns // 3
 
-    def kernel(whole_ref, in_ref, out_ref):
+    def kernel(whole_ref, up_ref, down_ref, in_ref, out_ref):
         total = None
         for j in range(narrow):
-            block = whole_ref[j * rows : (j + 1) * rows, :]
+            own = whole_ref[j * block : j * block + units, :].astype(F32)
+            if j < narrow // 2:
+                for i in range(fold):
+                    at = i * half + j * units
+                    up_ref[at : at + units, :] = own[:, i * half : (i + 1) * half]
+            else:
+                at = (j - narrow // 2) * units
+                down_ref[at : at + units, :] = own
+            at = j * block + units
+            found = whole_ref[at : at + rows, :].astype(F32)
+            total = found if total is None else total + found
+            at += rows
             for part in range(3):
-                at = part * narrow * third + j * third
-                in_ref[:, at : at + third] = block[:, part * third : (part + 1) * third].astype(F32)
-            found = block[:, columns:].astype(F32)
-            total = found if total is None else total + found
+                start = part * narrow * third + j * third
+                in_ref[:, start : start + third] = whole_ref[
+                    at : at + rows, part * third : (part + 1) * third
+                ].astype(F32)
         out_ref[...] = total
 
-    outs = [shape((rows, narrow * columns), F32), shape((rows, features), F32)]
+    outs = [
+        shape((features, half), F32), shape((half, features), F32),
+        shape((rows, narrow * columns), F32), shape((rows, features), F32),
+    ]
     return call(kernel, outs, [], [gathered])
 
 
 def dense_products(parts):
     return low(up_product(parts)), low(down_product(parts))
-
-
-def narrow_step(pair, step):
-    bits = lax.axis_size("narrow").bit_length() - 1
-    return [
-        low(value.astype(F32) + swap(value, "narrow", 1 << (step + i) % bits).astype(F32))
-        for i, value in enumerate(pair)
-    ]
-
-
-def narrow_last(pair):
-    bits = lax.axis_size("narrow").bit_length() - 1
-    for step in range(1, bits - 1):
-        pair = narrow_step(pair, step)
-    return [
-        (value, swap(value, "narrow", 1 << (bits - 1 + i) % bits)) for i, value in enumerate(pair)
-    ]
 
 
 def dense_join(parts):
@@ -346,12 +369,10 @@
     return value
 
 
-def everywhere_sum(value):
-    for axis in ("narrow", "wide"):
-        distance = 1
-        while distance < lax.axis_size(axis):
-            value = value + swap(value, axis, distance)
-            distance *= 2
+def axis_sum(value, axis, distance=1):
+    while distance < lax.axis_size(axis):
+        value = value + swap(value, axis, distance)
+        distance *= 2
     return value
 
 
@@ -380,11 +401,9 @@
     return jax.vjp(activate, source)[1](upstream)[0]
 
 
-def softened_scores(queries, keys, allowed):
+def masked_scores(queries, keys, allowed):
     scores = product(queries, keys, 1, 1) * HEAD_DIM ** (-0.5)
-    scores = jnp.where(allowed, scores, -1e30)
-    raised = jnp.exp(scores - jnp.max(scores, axis=-1, keepdims=True))
-    return raised / jnp.sum(raised, axis=-1, keepdims=True)
+    return jnp.where(allowed, scores, -1e30)
 
 
 def allowed_of(length, slots):
@@ -409,11 +428,12 @@
         ins, weight_ref, refs = refs[:count], refs[count], refs[count + 1 :]
         if raw:
             gain_ref, refs = refs[0], refs[1:]
-        packed_ref, outs = refs[0], refs[1 : count + 1]
+        packed_ref, level_ref, outs = refs[0], refs[1], refs[2 : count + 2]
+        levels = []
         for j in range(count):
             if raw:
                 rows = low(layer_norm(ins[j][...].astype(F32), gain_ref[...])[0])
-                refs[count + 1 + j][...] = rows
+                refs[count + 2 + j][...] = rows
             else:
                 rows = ins[j][...]
             packed = low(product(rows, weight_ref[...], 1, 0))
@@ -422,25 +442,33 @@
             found = []
             for head in range(columns // HEAD_DIM):
                 queries, keys, values = head_parts(packed, head, columns)
-                softened = softened_scores(queries, keys, allowed)
-                found.append(product(low(softened), values, 1, 0))
+                scores = masked_scores(queries, keys, allowed)
+                top = jnp.max(scores, axis=-1, keepdims=True)
+                raised = jnp.exp(scores - top)
+                weight_sum = jnp.sum(raised, axis=-1, keepdims=True)
+                levels.append(top + jnp.log(weight_sum))
+                found.append(product(low(raised / weight_sum), values, 1, 0))
             outs[j][...] = low(jnp.concatenate(found, axis=1))
-
-    outs = [shape((count, slots, 3 * columns), LOW)] + [shape((slots, columns), LOW)] * count
+        level_ref[...] = jnp.concatenate(levels, axis=1)
+
+    outs = [shape((count, slots, 3 * columns), LOW)]
+    outs += [shape((slots, count * columns // HEAD_DIM), F32)]
+    outs += [shape((slots, columns), LOW)] * count
     arrays = list(pieces) + [weight]
     if raw:
         outs += [shape((slots, features), LOW)] * count
         arrays.append(gain[None])
     flops = 2 * count * slots * features * 3 * columns
-    packed, *found = call(kernel, outs, [lengths], arrays, flops=flops)
-    return packed, found[:count], found[count:] if raw else pieces
+    packed, levels, *found = call(kernel, outs, [lengths], arrays, flops=flops)
+    return (packed, levels), found[:count], found[count:] if raw else pieces
 
 
 def attention_back(packed, grads, lengths):
+    packed, levels = packed
     count, (slots, columns) = len(grads), grads[0].shape
     scaling = HEAD_DIM ** (-0.5)
 
-    def kernel(lengths_ref, packed_ref, *refs):
+    def kernel(lengths_ref, packed_ref, level_ref, *refs):
         out = refs[count]
         for j in range(count):
             allowed = allowed_of(lengths_ref[j], slots)
@@ -450,7 +478,9 @@
             for head in range(columns // HEAD_DIM):
                 queries, keys, values = head_parts(whole, head, columns)
                 grad_head = grad_whole[:, head * HEAD_DIM : (head + 1) * HEAD_DIM]
-                softened = softened_scores(queries, keys, allowed)
+                at = j * (columns // HEAD_DIM) + head
+                scores = masked_scores(queries, keys, allowed)
+                softened = jnp.exp(scores - level_ref[:, at : at + 1])
                 grad_soft = product(grad_head, values, 1, 1)
                 inner = jnp.sum(softened * grad_soft, axis=-1, keepdims=True)
                 grad_scores = low(softened * (grad_soft - inner))
@@ -462,7 +492,7 @@
             )
 
     outs = [shape((count * slots, 3 * columns), LOW)]
-    return call(kernel, outs, [lengths], [packed] + list(grads))[0]
+    return call(kernel, outs, [lengths], [packed, levels] + list(grads))[0]
 
 
 def normed_back(grad_packed, weight, count):
@@ -557,7 +587,7 @@
     return total
 
 
-def layer_forward(source, raw, weights, selects, lengths, at_narrow, slices, first_work=None, second_work=None):
+def layer_forward(source, raw, weights, selects, lengths, at_narrow, slices, second_work=None, third_work=None):
     norm_first, attention_in, attention_out, norm_second, mixer, up, down, expert_up, expert_down = weights
     slots, features = source.shape
     wide, narrow = lax.axis_size("wide"), lax.axis_size("narrow")
@@ -566,26 +596,23 @@
     pieces = raw
     if raw is None:
         pieces = [own] + [swap(own, "narrow", j) for j in range(1, narrow)]
-    if first_work is not None:
-        pieces, first_found = together(pieces, first_work(own))
     packed, contexts, pieces = attention(
         pieces, None if raw is None else norm_first, attention_in, lengths
     )
-    context = pack_columns(
-        [contexts[0]] + [swap(contexts[j], "narrow", j) for j in range(1, narrow)], at_narrow
-    )
-    middle = source + jnp.dot(context, attention_out, preferred_element_type=F32)
-    second, scaled_two, inverse_two = layer_norm(middle, norm_second)
-    second = low(second)
+    context, middle, second, scaled_two, inverse_two = attended(
+        [contexts[0]] + [swap(contexts[j], "narrow", j) for j in range(1, narrow)],
+        attention_out, source, norm_second, at_narrow,
+    )
     across, beside = wide_pieces(second)
     if second_work is not None:
-        across, second_found = together(across, second_work(second, first_found))
+        across, second_found = together(across, second_work(second))
     rows = wide_join((across, beside))
     mixing = jax.nn.softmax(jnp.dot(rows, mixer, preferred_element_type=F32), axis=-1)
     pre = jnp.dot(rows, up, preferred_element_type=F32)
     act = low(activate(pre))
-    expert_rows, (mixing, pre, act) = together(
-        to_experts(selects, rows, slices), (mixing, pre, act)
+    third_found = None if third_work is None else third_work(rows, second_found)
+    expert_rows, (mixing, pre, act, third_found) = together(
+        to_experts(selects, rows, slices), (mixing, pre, act, third_found)
     )
     expert_pre = jnp.dot(expert_rows, expert_up, preferred_element_type=F32)
     expert_act = low(activate(expert_pre))
@@ -593,7 +620,7 @@
         scaled_one, inverse_one, pieces, packed, context, scaled_two, inverse_two,
         (rows, mixing, expert_rows, expert_pre, expert_act, pre, act),
     )
-    return (middle, kept) if second_work is None else (middle, kept, second_found)
+    return (middle, kept) if second_work is None else (middle, kept, third_found)
 
 
 def experts_found(kept, weights, selects, slices, gate=None):
@@ -628,7 +655,7 @@
     slots = upstream.shape[0]
     wide = lax.axis_size("wide")
     mixer_gap = (mixer[:, 0].astype(F32) - mixer[:, 1].astype(F32))[None]
-    grads, expert_grads, through, (grad_pre, dense_logit) = gathered
+    grads, expert_grads, through, dense_back = gathered
     expert_mixing = jax.nn.softmax(
         jnp.dot(expert_rows, mixer, preferred_element_type=F32), axis=-1
     )
@@ -636,6 +663,9 @@
     expert_logit = -expert_mixing[:, :1] * expert_mixing[:, 1:] * expert_dot
     expert_grad_pre = low(activation_back(expert_pre, expert_mixing[:, 1:] * through))
     expert_back = product(expert_grad_pre, expert_up, 1, 1) + expert_logit * mixer_gap
+    if callable(dense_back):
+        dense_back = dense_back(expert_back)
+    grad_pre, dense_logit = dense_back
     dense = (rows, grad_pre, act, mixing[:, :1], grads)
     found = from_experts(selects, expert_back, slices)
     experts = (
@@ -650,12 +680,15 @@
 
     half = grad_pre.shape[0] // 2
     halves = merged(slice(0, half)), low(merged(slice(half, 2 * half)))
+    parts = wide_sends(halves[0], swap(halves[1], "wide", 1), slots)
+    rows, dense_logit, expert_rows, expert_logit = after(
+        (rows, dense_logit, expert_rows, expert_logit), parts[0]
+    )
     grad_gap = jnp.sum(rows.astype(F32) * dense_logit, axis=0) + jnp.sum(
         expert_rows.astype(F32) * expert_logit, axis=0
     )
-    parts = wide_sends(halves[0], swap(halves[1], "wide", 1), slots)
-    grad_second, alongside_found = together(
-        wide_total(parts), alongside(parts[0], beneath_found, experts, dense)
+    grad_second, (grad_gap, alongside_found) = together(
+        wide_total(parts), (grad_gap, alongside(parts[0], halves[1], beneath_found, experts, dense))
     )
     grad_norm_part, grad_norm_second = norm_back(grad_second, scaled_two, inverse_two, norm_second)
     return (
@@ -673,44 +706,71 @@
     return product(act, low(mix * grads.astype(F32)), 0, 0)
 
 
-def attention_grads(grad_middle, kept, weights, lengths, at_narrow, at_wide, last, hold, aside=None):
+def attention_grads(grad_middle, kept, weights, lengths, at_narrow, hold, filler):
     norm_first, attention_in, attention_out = weights[:3]
     scaled_one, inverse_one, pieces, packed, context = kept[:5]
     narrow = lax.axis_size("narrow")
     grad_attended = low(grad_middle)
-    grad_contexts = split_columns(product(grad_attended, attention_out, 1, 1), narrow, at_narrow)
+    grad_contexts = context_back(grad_attended, attention_out, narrow, at_narrow)
     grad_contexts = [grad_contexts[0]] + [
         swap(grad_contexts[j], "narrow", j) for j in range(1, narrow)
     ]
-    if last:
-        out_halves = outer_halves([context], after(grad_attended, grad_contexts[0]), at_wide)
-        grad_contexts, out_halves = together(grad_contexts, halving_step(out_halves, 1))
-        out_halves = halving_step(out_halves, 2)
-        aside = aside(grad_contexts)
     grad_packed = attention_back(packed, grad_contexts, lengths)
-    if last:
-        grad_packed, out_halves = together(grad_packed, out_halves)
-        in_halves = outer_halves(pieces, grad_packed, at_wide)
-        parts = normed_back(after(grad_packed, in_halves), attention_in, narrow)
-        in_halves = halving_step(in_halves, 1)
-        gate = in_halves
-        in_halves = halving_step(in_halves, 2)
-        in_sum = low(halving_rest(in_halves, 4))
-        out_sum = halving_rest(out_halves, 4)
-        out_sum = after(out_sum, in_halves) + swap(
-            low(after(out_sum, in_halves)), "narrow", 1
-        ).astype(F32)
-        out_sum = narrow_rest(after(out_sum, in_sum))
-        weight_grads = narrow_join(in_sum, at_narrow), out_sum
-        hold = hold, in_sum, aside
-    else:
-        grad_packed, hold = together(grad_packed, hold)
-        parts = normed_back(grad_packed, attention_in, narrow)
-        weight_grads = (pieces, after(grad_packed, parts), context, grad_attended)
+    grad_packed, hold = together(grad_packed, hold)
+    parts = normed_back(grad_packed, attention_in, narrow)
+    weight_grads = (pieces, after(grad_packed, parts), context, grad_attended)
+    filled = filler(parts[0])
     parts = [parts[0]] + [swap(parts[j], "narrow", j) for j in range(1, narrow)]
-    grad_normed = sum(part.astype(F32) for part in (after(parts, gate) if last else parts))
+    parts, filled = together(parts, filled)
+    grad_normed = sum(part.astype(F32) for part in parts)
     grad_norm_part, grad_norm_first = norm_back(grad_normed, scaled_one, inverse_one, norm_first)
-    return grad_middle + grad_norm_part, grad_norm_first, weight_grads, hold
+    return grad_middle + grad_norm_part, grad_norm_first, weight_grads, hold, filled
+
+
+def last_grads(
+    grad_middle, kept, weights, lengths, at_narrow, at_wide, dense, pair, narrow_columns, early
+):
+    norm_first, attention_in, attention_out = weights[:3]
+    scaled_one, inverse_one, pieces, packed, context = kept[:5]
+    narrow = lax.axis_size("narrow")
+    grad_attended = low(grad_middle)
+    grad_contexts = context_back(grad_attended, attention_out, narrow, at_narrow)
+    grad_contexts = [grad_contexts[0]] + [
+        swap(grad_contexts[j], "narrow", j) for j in range(1, narrow)
+    ]
+    out_halves = outer_halves([context], after(grad_attended, grad_contexts[-1]), at_wide)
+    grad_contexts, out_halves = together(grad_contexts, halving_step(out_halves, 1))
+    rows = pair.shape[0]
+    gathered = narrow_gather(stack_own(dense, after(pair, grad_contexts), narrow_columns))
+    out_halves = halving_step(out_halves, 2)
+    early = after(early, grad_contexts)
+    early = early + swap(early, "narrow", 1)
+    grad_packed = attention_back(packed, grad_contexts, lengths)
+    grad_packed, (out_halves, early) = together(grad_packed, (out_halves, early))
+    in_halves = outer_halves(pieces, grad_packed, at_wide)
+    in_halves, early = together(in_halves, axis_sum(early, "narrow", 2))
+    parts = normed_back(after(grad_packed, in_halves), attention_in, narrow)
+    in_halves = halving_step(halving_step(in_halves, 1), 2)
+    parts = [parts[0]] + [swap(parts[j], "narrow", j) for j in range(1, narrow)]
+    parts = after(parts, in_halves)
+    grad_normed = sum(part.astype(F32) for part in parts)
+    grad_norm_part, grad_norm_first = norm_back(grad_normed, scaled_one, inverse_one, norm_first)
+    grad_inputs = grad_middle + grad_norm_part
+    out_sum = halving_rest(out_halves, 4)
+    in_sum, (first, grad_inputs) = together(
+        low(halving_rest(in_halves, 4)), (grad_norm_first[None], grad_inputs)
+    )
+    out_sum = after(out_sum, in_halves)
+    out_sum = out_sum + swap(low(out_sum), "narrow", 1).astype(F32)
+    in_pieces = [in_sum] + [swap(in_sum, "narrow", j) for j in range(1, narrow)]
+    in_pieces, gathered = together(
+        in_pieces, split_gathered(after(gathered, in_sum), rows, narrow_columns)
+    )
+    vectors = axis_sum(jnp.concatenate([axis_sum(first, "narrow"), early], axis=0), "wide")
+    out_sum = narrow_rest(after(out_sum, in_sum))
+    return (
+        grad_inputs, (spread_columns(in_pieces, at_narrow), out_sum), vectors, gathered
+    )
 
 
 def body(
@@ -765,97 +825,94 @@
         inputs.astype(F32), input_pieces, shallow, shallow_selects, lengths, at_narrow, SLICES_SHALLOW
     )
     deep_in = gather_wide(after(deep_slab, kept_shallow[7][0]))
-    all_grads = gather_wide(after(cotangent, kept_shallow[7][2]))
+    deep_out = gather_wide(after(deep_attention_out, kept_shallow[7][2]))
     found = experts_found(kept_shallow, shallow, shallow_selects, SLICES_SHALLOW)
     halves = merged_halves(kept_shallow, shallow, shallow_selects, found, slots)
     total = wide_sums(halves, slots)
     passed = middle + total
-    deep_out = gather_wide(after(deep_attention_out, total))
+    all_grads = gather_wide(after(cotangent, total))
     deep = (
         gains[2], deep_in, deep_out, gains[3], small[6:8].T,
         deep_dense_up, deep_dense_down, deep_expert_up[0], deep_expert_down[0],
     )
-    def first_work(own):
-        grads = reorder(after(all_grads, own), slots, at_wide, False)
-        return grads, picked(deep_selects, grads)
-
-    def second_work(second, found):
-        grads, sent = found
-        expert_grads = exchanged(after(sent, second), SLICES_DEEP)
-        return (
-            grads, expert_grads, product(after(grads, second), deep_dense_down, 1, 1),
-            product(expert_grads, deep_expert_down[0], 1, 1),
+    def second_work(second):
+        grads = reorder(after(all_grads, second), slots, at_wide, False)
+        expert_grads = to_experts(deep_selects, grads, SLICES_DEEP)
+        return grads, expert_grads, product(grads, deep_dense_down, 1, 1)
+
+    def third_work(rows, found):
+        grads, expert_grads, through = found
+        return grads, expert_grads, through, product(after(expert_grads, rows), deep_expert_down[0], 1, 1)
+
+    middle, kept_deep, gathered = layer_forward(
+        passed, None, deep, deep_selects, lengths, at_narrow, SLICES_DEEP, second_work, third_work
+    )
+    def deep_result(found):
+        halves = merged_halves(kept_deep, deep, deep_selects, found, slots)
+        return reorder(
+            jnp.concatenate([low(halves[0]), halves[1]], axis=0), slots, at_wide, True
         )
 
-    middle, kept_deep, gathered = layer_forward(
-        passed, None, deep, deep_selects, lengths, at_narrow, SLICES_DEEP, first_work, second_work
-    )
-    grad_middle, _, deep_experts, deep_rows, whole, (deep_down, token) = experts_back(
+    grad_middle, _, deep_experts, deep_rows, (whole, found), result = experts_back(
         cotangent.astype(F32),
-        gathered[:2] + (gathered[3], dense_back_of(gathered[2], kept_deep, deep)), kept_deep,
+        gathered[:2] + (
+            gathered[3],
+            lambda token: dense_back_of(after(gathered[2], token), kept_deep, deep),
+        ), kept_deep,
         deep, deep_selects, SLICES_DEEP,
-        lambda token, experts, dense: dense_join(dense_products(dense)),
-        lambda token, found, experts, dense: (down_product(after(experts, token)), token),
-    )
-    found = experts_found(kept_deep, deep, deep_selects, SLICES_DEEP, token)
-    grad_passed, deep_first, outer_parts, (whole, found) = attention_grads(
-        grad_middle, kept_deep, deep, lengths, at_narrow, at_wide, False,
-        (narrow_scatter(whole), found),
+        lambda token, experts, dense: (
+            dense_join(dense_products(after(dense, token))),
+            experts_found(kept_deep, deep, deep_selects, SLICES_DEEP, token),
+        ),
+        lambda token, other, found, experts, dense: deep_result(after(found[1], token)),
+    )
+    total = lax.psum_scatter(result, "wide", scatter_dimension=0, tiled=True)
+    grad_passed, deep_first, outer_parts, whole, deep_down = attention_grads(
+        grad_middle, kept_deep, deep, lengths, at_narrow, narrow_scatter(whole),
+        lambda token: down_product(after(deep_experts, token)),
     )
     passed_low = low(grad_passed)
     across, beside = wide_pieces(passed_low)
-    halves = merged_halves(kept_deep, deep, deep_selects, after(found, passed_low), slots)
-    result = reorder(
-        jnp.concatenate([low(halves[0]), halves[1]], axis=0), slots, at_wide, True
-    )
-    deep_up = up_product(after(deep_experts, passed_low))
-    across, (result, deep_up, whole) = together(across, (result, deep_up, narrow_gather(whole)))
+    across, total = together(across, total)
     grads = wide_join((across, beside))
     pair = outer_pair(*after(outer_parts, grads))
-    deep_dense = dense_outputs(after(whole, grads))
-    expert_grads, (pair, deep_dense, dense_back) = together(
+    expert_grads, (pair, dense_back) = together(
         to_experts(shallow_selects, grads, SLICES_SHALLOW),
         (
-            pair, deep_dense,
+            pair,
             dense_back_of(product(grads, shallow_dense_down, 1, 1), kept_shallow, shallow),
         ),
     )
     pair = lax.psum_scatter(pair, "wide", scatter_dimension=0, tiled=True)
-
-    grad_middle, _, _, shallow_rows, _, (shallow_experts, shallow_dense, pair) = experts_back(
+    whole = narrow_gather(after(whole, passed_low))
+    grad_middle, _, _, shallow_rows, (joined, deep_up), (shallow_experts, pair, deep_dense) = experts_back(
         grad_passed,
         (grads, expert_grads, product(expert_grads, shallow_expert_down[0], 1, 1), dense_back),
         kept_shallow, shallow, shallow_selects, SLICES_SHALLOW,
-        lambda token, experts, dense: dense_products(after(dense, token)),
-        lambda token, found, experts, dense: (
-            [f(after(experts, token)) for f in (up_product, down_product)],
-            narrow_step(after(found, token), 0), pair,
+        lambda token, experts, dense: (
+            dense_join(dense_products(after(dense, token))),
+            up_product(after(deep_experts, token)),
         ),
+        lambda token, other, found, experts, dense: (
+            [f(after(experts, token)) for f in (up_product, down_product)], pair,
+            dense_outputs(after(whole, token)),
+        ),
     )
     shallow_up, shallow_down = shallow_experts
-    total = lax.psum_scatter(
-        after(result, grad_middle), "wide", scatter_dimension=0, tiled=True
-    )
-    grad_inputs, shallow_first, (grad_shallow_in, grad_shallow_out), total = attention_grads(
-        grad_middle, kept_shallow, shallow, lengths, at_narrow, at_wide, True, total,
-        lambda token: narrow_last(after(shallow_dense, token)),
-    )
-    total, vector_gate, shallow_dense = total
-    shallow_dense, total, pair = after((shallow_dense, total, narrow_gather(pair)), vector_gate)
-    shallow_dense = [own.astype(F32) + other.astype(F32) for own, other in shallow_dense]
+    early = jnp.stack(list(shallow_rows) + [deep_first] + list(deep_rows))
+    grad_inputs, (grad_shallow_in, grad_shallow_out), vectors, gathered = last_grads(
+        grad_middle, kept_shallow, shallow, lengths, at_narrow, at_wide,
+        narrow_scatter(joined), pair, narrow_columns, early,
+    )
+    *shallow_dense, grad_deep_in, grad_deep_out = gathered
     output = middle + total.astype(F32)
-    grad_deep_in, grad_deep_out = join_pair(pair, narrow_columns)
     deep_up, deep_down = deep_up[None], deep_down[None]
     shallow_up, shallow_down = shallow_up[None], shallow_down[None]
     grads_shallow = (
         grad_shallow_in, grad_shallow_out, *shallow_dense, shallow_up, shallow_down,
-        shallow_first, *shallow_rows,
     )
     grads_deep = (
-        grad_deep_in, grad_deep_out, *deep_dense, deep_up, deep_down, deep_first, *deep_rows,
-    )
-    vectors = everywhere_sum(
-        after(jnp.stack(list(grads_shallow[6:]) + list(grads_deep[6:])), vector_gate)
+        grad_deep_in, grad_deep_out, *deep_dense, deep_up, deep_down,
     )
     vectors = lax.dynamic_slice_in_dim(vectors, wide_at * (features // wide), features // wide, axis=1)
 

time: 701 us -> 670 us (0.956)
  starting transfers between devices: 129 us -> 112 us
  Pallas kernels: 114 us -> 124 us
  matrix products: 120 us -> 111 us
  other arithmetic: 57.2 us -> 49.6 us
    ppermute x108 -> x106, starting transfers between devices: 126 us -> 109 us  [swap(): lax.ppermute(array, axis, [(i, i ^ distance) for i in range(lax.axis_size...]
    ppermute x108 -> x106, waiting for transfers between devices: 222 us -> 212 us  [swap(): lax.ppermute(array, axis, [(i, i ^ distance) for i in range(lax.axis_size...]
    pallas_call x32 -> x34, Pallas kernels: 114 us -> 124 us  [call(): pl.pallas_call(kernel, out_shape=tuple(outs), in_specs=[smem()] * len(sca...]
    convert_element_type x20 -> x14, other arithmetic: 20.9 us -> 13 us  [low(): return value.astype(LOW)]
    dot_general x38 -> x36, matrix products: 85.9 us -> 82.8 us  [product(): lax.dot_general(left, right, (((left_dim,), (right_dim,)), ((), ())), pre...]
    unnamed x331 -> x269, local copies, waits for them, and re-layouts: 15.8 us -> 14.2 us
  transfers between devices with their start and end apart: 117 -> 116, of which waited for: 57 -> 53; matrix products, arithmetic and copies ran while one was open for 22% -> 24% of each run, Pallas kernels for 13% -> 16%
where the time goes in v3:
time: 670 us; the launch traced here: 661 us
  waiting for transfers between devices  219 us (33%)
  Pallas kernels  124 us (19%)
  starting transfers between devices  112 us (17%)
  matrix products  111 us (17%)
  other arithmetic  49.6 us (7%)
  local copies, waits for them, and re-layouts  29.3 us (4%)
  between operations  16.5 us (2%)
    ppermute x106, waiting for transfers between devices, swap(): lax.ppermute(array, axis, [(i, i ^ distance) for i in range(lax.axis_size...  212 us
    pallas_call x34, Pallas kernels, call(): pl.pallas_call(kernel, out_shape=tuple(outs), in_specs=[smem()] * len(sca...  124 us
    ppermute x106, starting transfers between devices, swap(): lax.ppermute(array, axis, [(i, i ^ distance) for i in range(lax.axis_size...  109 us
    dot_general x36, matrix products, product(): lax.dot_general(left, right, (((left_dim,), (right_dim,)), ((), ())), pre...  82.8 us
    unnamed x269, local copies, waits for them, and re-layouts  14.2 us
  transfers between devices with their start and end apart: 116, of which 53 were waited for; matrix products, arithmetic and copies ran while one was open for 24% of the time, Pallas kernels for 16%

profile of v3, /device:TPU:0, one launch (start us, length us, event | category | flops | bytes accessed | tf_op | source)
XLA Modules:
  0.0 661.0 jit_solution(9516116323689076183)
XLA Ops:
  25.7 9.3 %collective-permute-done.1.refs_4_ = bf16[136,768]{1,0:T(8,128)(2,1)S(1)} collective-permute-done((bf16[136,768]{1,0:T(8,128)(2,1)}, bf16[136,768]{1,0:T(8,128)(2,1)S(1)}, u32[]{:S(2)}, u32[]{:S(2)}) %collective-permute-start.1) | collective-permute-done | bytes 208928 | tf_op jit(solution)/shard_map/ppermute | solution.py:21
  42.8 9.1 %shard_map.395 = (bf16[4,128,768]{2,1,0:T(8,128)(2,1)}, f32[128,16]{1,0:T(8,128)}, bf16[128,256]{1,0:T(8,128)(2,1)}, bf16[128,256]{1,0:T(8,128)(2,1)}, bf16[128,...) custom-call(s32[4]{0:T(128)} %gather_fusion.1, ...), custom_call_target="tpu_custom_call" | custom-call | flops 805306368 | bytes 4730880 | tf_op jit(solution)/shard_map/pallas_call | solution.py:40
  60.4 6.4 all-gather.7.cloned.1.call-done.weight_ref
  66.8 3.4 shard_map.396
  74.6 9.0 %collective-permute-done.13.refs_1_ = bf16[128,1024]{1,0:T(8,128)(2,1)S(1)} collective-permute-done((bf16[128,1024]{1,0:T(8,128)(2,1)}, bf16[128,1024]{1,0:T(8,128)(2,1)S(1)}, u32[]{:S(2)}, u32[]{:S(2)}) %collective-permute-start.13) | collective-permute-done | bytes 262176 | tf_op jit(solution)/shard_map/ppermute | solution.py:21
  83.6 9.6 %collective-permute-done.14.refs_2_ = bf16[128,1024]{1,0:T(8,128)(2,1)S(1)} collective-permute-done((bf16[128,1024]{1,0:T(8,128)(2,1)}, bf16[128,1024]{1,0:T(8,128)(2,1)S(1)}, u32[]{:S(2)}, u32[]{:S(2)}) %collective-permute-start.14) | collective-permute-done | bytes 262176 | tf_op jit(solution)/shard_map/ppermute | solution.py:21
  107.3 3.2 fusion.43
  110.6 4.5 collective-permute-done.20.refs_1_
  115.1 8.8 %collective-permute-done.21.refs_2_ = bf16[192,1024]{1,0:T(8,128)(2,1)S(1)} collective-permute-done((bf16[192,1024]{1,0:T(8,128)(2,1)S(1)}, bf16[192,1024]{1,0:T(8,128)(2,1)S(1)}, u32[]{:S(2)}, u32[]{:S(2)}) %collective-permute-start.21) | collective-permute-done | bytes 393248 | tf_op jit(solution)/shard_map/ppermute | solution.py:21
  127.5 5.5 multiply_convert_fusion.4
  139.2 8.7 %collective-permute-done.25 = bf16[192,1024]{1,0:T(8,128)(2,1)S(1)} collective-permute-done((bf16[192,1024]{1,0:T(8,128)(2,1)S(1)}, bf16[192,1024]{1,0:T(8,128)(2,1)S(1)}, u32[]{:S(2)}, u32[]{:S(2)}) %collective-permute-start.25) | collective-permute-done | bytes 393248 | tf_op jit(solution)/shard_map/ppermute | solution.py:21
  147.9 5.9 collective-permute-done.24
  163.1 4.4 collective-permute-start.28
  167.5 5.2 collective-permute-done.29
  172.7 16.1 %collective-permute-done.28 = bf16[128,1024]{1,0:T(8,128)(2,1)S(1)} collective-permute-done((bf16[128,1024]{1,0:T(8,128)(2,1)}, bf16[128,1024]{1,0:T(8,128)(2,1)S(1)}, u32[]{:S(2)}, u32[]{:S(2)}) %collective-permute-start.28) | collective-permute-done | bytes 262176 | tf_op jit(solution)/shard_map/ppermute | solution.py:21
  196.6 5.2 collective-permute-done.30.refs_1_
  201.7 5.3 collective-permute-done.31.refs_2_
  207.0 8.1 %shard_map.400 = (bf16[4,128,768]{2,1,0:T(8,128)(2,1)}, f32[128,16]{1,0:T(8,128)}, bf16[128,256]{1,0:T(8,128)(2,1)}, bf16[128,256]{1,0:T(8,128)(2,1)}, bf16[128,...) custom-call(s32[4]{0:T(128)} %gather_fusion.1, bf16[128,1024]{1,0:T(8,128)(2,1)} %copy-done.39, ...), custom_call_target="tpu_custom_call" | custom-call | flops 805306368 | bytes 3678208 | tf_op jit(solution)/shard_map/pallas_call | solution.py:40
  222.9 3.4 shard_map.401
  239.4 7.7 %collective-permute-done.37.refs_2_ = bf16[128,1024]{1,0:T(8,128)(2,1)S(1)} collective-permute-done((bf16[128,1024]{1,0:T(8,128)(2,1)}, bf16[128,1024]{1,0:T(8,128)(2,1)S(1)}, u32[]{:S(2)}, u32[]{:S(2)}) %collective-permute-start.37) | collective-permute-done | bytes 262176 | tf_op jit(solution)/shard_map/ppermute | solution.py:21
  252.9 4.5 collective-permute-done.41.refs_3_
  272.4 3.7 fusion.6
  281.4 4.4 fusion.2
  346.8 11.8 %collective-permute-done.57 = bf16[128,1024]{1,0:T(8,128)(2,1)} collective-permute-done((bf16[128,1024]{1,0:T(8,128)(2,1)}, bf16[128,1024]{1,0:T(8,128)(2,1)}, u32[]{:S(2)}, u32[]{:S(2)}) %collective-permute-start.57) | collective-permute-done | bytes 262176 | tf_op jit(solution)/shard_map/ppermute | solution.py:21
  376.2 7.5 %shard_map.410.grad_ref.refs_4_ = bf16[512,768]{1,0:T(8,128)(2,1)} custom-call(s32[4]{0:T(128)} %gather_fusion.1, bf16[4,128,768]{2,1,0:T(8,128)(2,1)} %get-tuple-element.307.packed_ref, f32[128,16]{1,0:T(8,128)} %get-tuple-element.308.level_ref, bf16[128,256]{1,0:T(8,128)(2,1)} %get-tuple-element.309.refs_0_, bf16[128,256]{1,0:T(8,128)(2,1)} %copy-done.94, ...), custom_call_target="tpu_custom_call" | custom-call | bytes 1843200 | tf_op jit(solution)/shard_map/pallas_call | solution.py:40
  383.7 3.6 shard_map.411
  390.8 7.5 %fusion.72 = f32[2048,1024]{1,0:T(8,128)} fusion(bf16[384,2048]{1,0:T(8,128)(2,1)} %copy-done.12, bf16[384,1024]{1,0:T(8,128)(2,1)} %shard_map.403, f32[384]{0:T(512)S(1)} %reduce.4), kind=kOutput, calls=%fused_computation.118 | convolution fusion | flops 1611792384 | bytes 10749440 | tf_op jit(solution)/shard_map/dot_general | solution.py:25
  408.3 6.0 collective-permute-done.65.refs_1_
  414.4 10.8 %collective-permute-done.66.refs_2_ = bf16[128,1024]{1,0:T(8,128)(2,1)} collective-permute-done((bf16[128,1024]{1,0:T(8,128)(2,1)}, bf16[128,1024]{1,0:T(8,128)(2,1)}, u32[]{:S(2)}, u32[]{:S(2)}) %collective-permute-start.66) | collective-permute-done | bytes 262176 | tf_op jit(solution)/shard_map/ppermute | solution.py:21
  437.0 5.8 multiply_reduce_fusion.5
  442.8 5.0 shard_map.414
  447.9 6.7 %collective-permute-done.74.refs_3_ = bf16[192,1024]{1,0:T(8,128)(2,1)} collective-permute-done((bf16[192,1024]{1,0:T(8,128)(2,1)}, bf16[192,1024]{1,0:T(8,128)(2,1)}, u32[]{:S(2)}, u32[]{:S(2)}) %collective-permute-start.74) | collective-permute-done | bytes 393248 | tf_op jit(solution)/shard_map/ppermute | solution.py:21
  460.0 7.6 %multiply_reduce_fusion.3 = (f32[768]{0:T(1024)S(1)}, bf16[768,1024]{1,0:T(8,128)(2,1)S(1)}) fusion(bf16[768,1024]{1,0:T(8,128)(2,1)} %copy-done.129, f32[768,1024]{1,0:T(8,128)} %get-tuple-element.546, f32[768]{0:T(1024)S(1)} %get-tuple-element.518, bf16[768,1024]{1,0:T(8,128)(2,1)} %shard_map.413, bf16[1,1024,1024]{2,1,0:T(8,128)(2,1)} %param.38), kind=kOutput, calls=%fused_computation.36 | convolution fusion | flops 1629486336 | bytes 9967616 | tf_op jit(solution)/shard_map/dot_general | solution.py:25
  467.6 3.5 fusion.178
  483.3 7.2 %fusion.180 = f32[1024,2048]{1,0:T(8,128)} fusion(bf16[384,1024]{1,0:T(8,128)(2,1)S(1)} %copy-done.11, bf16[384,2048]{1,0:T(8,128)(2,1)} %copy-done.14), kind=kOutput, calls=%fused_computation.333 | convolution fusion | flops 1610612736 | bytes 10747904 | tf_op jit(solution)/shard_map/dot_general | solution.py:25
  502.7 3.4 collective-permute-start.81
  511.5 4.0 fusion.66
  515.4 3.9 fusion.181
  519.3 3.8 shard_map.417
  523.1 7.1 %collective-permute-done.80 = bf16[128,1024]{1,0:T(8,128)(2,1)S(1)} collective-permute-done((bf16[128,1024]{1,0:T(8,128)(2,1)}, bf16[128,1024]{1,0:T(8,128)(2,1)S(1)}, u32[]{:S(2)}, u32[]{:S(2)}) %collective-permute-start.80) | collective-permute-done | bytes 262176 | tf_op jit(solution)/shard_map/ppermute | solution.py:21
  539.5 4.0 collective-permute-done.84.refs_3_
  556.8 7.5 %shard_map.420.refs_4_.grad_ref = bf16[512,768]{1,0:T(8,128)(2,1)} custom-call(s32[4]{0:T(128)} %gather_fusion.1, bf16[4,128,768]{2,1,0:T(8,128)(2,1)} %get-tuple-element.333.packed_ref, f32[128,16]{1,0:T(8,128)} %get-tuple-element.334.level_ref, bf16[128,256]{1,0:T(8,128)(2,1)} %get-tuple-element.390.refs_0_, bf16[128,256]{1,0:T(8,128)(2,1)} %copy-done.86, ...), custom_call_target="tpu_custom_call" | custom-call | bytes 1843200 | tf_op jit(solution)/shard_map/pallas_call | solution.py:40
  571.9 3.8 shard_map.421
  583.3 3.7 shard_map.422
  590.5 7.1 %collective-permute-done.90 = bf16[256,768]{1,0:T(8,128)(2,1)S(1)} collective-permute-done((bf16[256,768]{1,0:T(8,128)(2,1)S(1)}, bf16[256,768]{1,0:T(8,128)(2,1)S(1)}, u32[]{:S(2)}, u32[]{:S(2)}) %collective-permute-start.90) | collective-permute-done | bytes 393248 | tf_op jit(solution)/shard_map/ppermute | solution.py:21
  603.6 10.1 %collective-permute-done.94 = bf16[128,1024]{1,0:T(8,128)(2,1)S(1)} collective-permute-done((bf16[128,1024]{1,0:T(8,128)(2,1)}, bf16[128,1024]{1,0:T(8,128)(2,1)S(1)}, u32[]{:S(2)}, u32[]{:S(2)}) %collective-permute-start.94) | collective-permute-done | bytes 262176 | tf_op jit(solution)/shard_map/ppermute | solution.py:21
  635.7 8.9 %collective-permute-done.105 = bf16[128,1024]{1,0:T(8,128)(2,1)S(1)} collective-permute-done((bf16[128,1024]{1,0:T(8,128)(2,1)S(1)}, bf16[128,1024]{1,0:T(8,128)(2,1)S(1)}, u32[]{:S(2)}, u32[]{:S(2)}) %collective-permute-start.105) | collective-permute-done | bytes 262176 | tf_op jit(solution)/shard_map/ppermute | solution.py:21
  645.5 5.0 shard_map.424
  (678 shorter events, 338.1 us)
Async XLA Ops:
  7.2 59.6 %all-gather.7.cloned.1.call-start = ((), (), s32[]{:S(2)}) async-start(), calls=%async_computation.4 | async-start | bytes 2359296 | tf_op jit(solution)/shard_map/all_gather | solution.py:287
  14.3 20.7 %collective-permute-start.3 = (bf16[128,1024]{1,0:T(8,128)(2,1)}, bf16[128,1024]{1,0:T(8,128)(2,1)S(1)}, u32[]{:S(2)}, u32[]{:S(2)}) collective-permute-start(bf16[128,1024]{1,0:T(8,128)(2,1)} %refs_0_), channel_id=1, source_target_pairs={{0,1},{1,0},{2,3},{3,2},{4,5},{5,4},{6,7},{7,6},{8,9},{9,8},{10,11... | collective-permute-start | bytes 786440 | tf_op jit(solution)/shard_map/ppermute | solution.py:21
  15.8 19.3 %collective-permute-start.4 = (bf16[128,1024]{1,0:T(8,128)(2,1)}, bf16[128,1024]{1,0:T(8,128)(2,1)S(1)}, u32[]{:S(2)}, u32[]{:S(2)}) collective-permute-start(bf16[128,1024]{1,0:T(8,128)(2,1)} %refs_0_), channel_id=1, source_target_pairs={{0,2},{1,3},{2,0},{3,1},{4,6},{5,7},{6,4},{7,5},{8,10},{9,11},{10,... | collective-permute-start | bytes 786440 | tf_op jit(solution)/shard_map/ppermute | solution.py:21
  17.3 17.8 %collective-permute-start.5 = (bf16[128,1024]{1,0:T(8,128)(2,1)}, bf16[128,1024]{1,0:T(8,128)(2,1)S(1)}, u32[]{:S(2)}, u32[]{:S(2)}) collective-permute-start(bf16[128,1024]{1,0:T(8,128)(2,1)} %refs_0_), channel_id=1, source_target_pairs={{0,3},{1,2},{2,1},{3,0},{4,7},{5,6},{6,5},{7,4},{8,11},{9,10},{10,... | collective-permute-start | bytes 786440 | tf_op jit(solution)/shard_map/ppermute | solution.py:21
  17.8 17.2 %collective-permute-start.1 = (bf16[136,768]{1,0:T(8,128)(2,1)}, bf16[136,768]{1,0:T(8,128)(2,1)S(1)}, u32[]{:S(2)}, u32[]{:S(2)}) collective-permute-start(bf16[136,768]{1,0:T(8,128)(2,1)} %shard_map.392.refs_0_), channel_id=1, source_target_pairs={{0,16},{4,20},{8,24},{12,28},{16,0},{20,4},{24,8},{28,12},{1,17},{... | collective-permute-start | bytes 626696 | tf_op jit(solution)/shard_map/ppermute | solution.py:21
  35.1 171.8 %all-gather.11.cloned.1.call-start = ((), (), s32[]{:S(2)}) async-start(), calls=%async_computation.6 | async-start | bytes 1769472 | tf_op jit(solution)/shard_map/all_gather | solution.py:287
  71.7 21.5 %collective-permute-start.14 = (bf16[128,1024]{1,0:T(8,128)(2,1)}, bf16[128,1024]{1,0:T(8,128)(2,1)S(1)}, u32[]{:S(2)}, u32[]{:S(2)}) collective-permute-start(bf16[128,1024]{1,0:T(8,128)(2,1)} %get-tuple-element.248.refs_0_), channel_id=1, source_target_pairs={{0,16},{4,20},{8,24},{12,28},{16,0},{20,4},{24,8},{28,12},{1,17},{... | collective-permute-start | bytes 786440 | tf_op jit(solution)/shard_map/ppermute | solution.py:21
  72.6 20.6 %collective-permute-start.15 = (bf16[128,1024]{1,0:T(8,128)(2,1)}, bf16[128,1024]{1,0:T(8,128)(2,1)S(1)}, u32[]{:S(2)}, u32[]{:S(2)}) collective-permute-start(bf16[128,1024]{1,0:T(8,128)(2,1)} %get-tuple-element.248.refs_0_), channel_id=1, source_target_pairs={{0,24},{4,28},{8,16},{12,20},{16,8},{20,12},{24,0},{28,4},{1,25},{... | collective-permute-start | bytes 786440 | tf_op jit(solution)/shard_map/ppermute | solution.py:21
  74.6 19.1 %collective-permute-start.16 = (bf16[128,1024]{1,0:T(8,128)(2,1)}, bf16[128,1024]{1,0:T(8,128)(2,1)S(1)}, u32[]{:S(2)}, u32[]{:S(2)}) collective-permute-start(bf16[128,1024]{1,0:T(8,128)(2,1)} %get-tuple-element.248.refs_0_), channel_id=1, source_target_pairs={{0,4},{4,0},{8,12},{12,8},{16,20},{20,16},{24,28},{28,24},{1,5},{5... | collective-permute-start | bytes 786440 | tf_op jit(solution)/shard_map/ppermute | solution.py:21
  98.2 124.0 %all-gather.9.cloned.1.call-start = ((), (), s32[]{:S(2)}) async-start(), calls=%async_computation.5 | async-start | bytes 2359296 | tf_op jit(solution)/shard_map/all_gather | solution.py:287
  104.5 19.3 %collective-permute-start.21 = (bf16[192,1024]{1,0:T(8,128)(2,1)S(1)}, bf16[192,1024]{1,0:T(8,128)(2,1)S(1)}, u32[]{:S(2)}, u32[]{:S(2)}) collective-permute-start(bf16[192,1024]{1,0:T(8,128)(2,1)S(1)} %convolution_convert_fusion.3.refs_0_), channel_id=1, source_target_pairs={{0,2},{1,3},{2,0},{3,1},{4,6},{5,7},{6,4},{7,5},{8,10},{9,11},{10,... | collective-permute-start | bytes 1179656 | tf_op jit(solution)/shard_map/ppermute | solution.py:21
  106.0 17.8 %collective-permute-start.22 = (bf16[192,1024]{1,0:T(8,128)(2,1)S(1)}, bf16[192,1024]{1,0:T(8,128)(2,1)}, u32[]{:S(2)}, u32[]{:S(2)}) collective-permute-start(bf16[192,1024]{1,0:T(8,128)(2,1)S(1)} %convolution_convert_fusion.3.refs_0_), channel_id=1, source_target_pairs={{0,3},{1,2},{2,1},{3,0},{4,7},{5,6},{6,5},{7,4},{8,11},{9,10},{10,... | collective-permute-start | bytes 1179656 | tf_op jit(solution)/shard_map/ppermute | solution.py:21
  127.2 103.5 %all-gather.13.cloned.1.call-start = ((), (), s32[]{:S(2)}) async-start(), calls=%async_computation.7 | async-start | bytes 2359296 | tf_op jit(solution)/shard_map/all_gather | solution.py:287
  136.5 17.3 %collective-permute-start.24 = (bf16[192,1024]{1,0:T(8,128)(2,1)S(1)}, bf16[192,1024]{1,0:T(8,128)(2,1)S(1)}, u32[]{:S(2)}, u32[]{:S(2)}) collective-permute-start(bf16[192,1024]{1,0:T(8,128)(2,1)S(1)} %get-tuple-element.491), channel_id=1, source_target_pairs={{0,2},{1,3},{2,0},{3,1},{4,6},{5,7},{6,4},{7,5},{8,10},{9,11},{10,... | collective-permute-start | bytes 1179656 | tf_op jit(solution)/shard_map/ppermute | solution.py:21
  137.0 16.8 %collective-permute-start.23 = (bf16[192,1024]{1,0:T(8,128)(2,1)S(1)}, bf16[192,1024]{1,0:T(8,128)(2,1)S(1)}, u32[]{:S(2)}, u32[]{:S(2)}) collective-permute-start(bf16[192,1024]{1,0:T(8,128)(2,1)S(1)} %get-tuple-element.489), channel_id=1, source_target_pairs={{0,1},{1,0},{2,3},{3,2},{4,5},{5,4},{6,7},{7,6},{8,9},{9,8},{10,11... | collective-permute-start | bytes 1179656 | tf_op jit(solution)/shard_map/ppermute | solution.py:21
  163.1 25.6 %collective-permute-start.28 = (bf16[128,1024]{1,0:T(8,128)(2,1)}, bf16[128,1024]{1,0:T(8,128)(2,1)S(1)}, u32[]{:S(2)}, u32[]{:S(2)}) collective-permute-start(bf16[128,1024]{1,0:T(8,128)(2,1)} %get-tuple-element.256), channel_id=1, source_target_pairs={{0,16},{4,20},{8,24},{12,28},{16,0},{20,4},{24,8},{28,12},{1,17},{... | collective-permute-start | bytes 786440 | tf_op jit(solution)/shard_map/ppermute | solution.py:21
  167.5 21.2 %collective-permute-start.27 = (bf16[128,1024]{1,0:T(8,128)(2,1)}, bf16[128,1024]{1,0:T(8,128)(2,1)S(1)}, u32[]{:S(2)}, u32[]{:S(2)}) collective-permute-start(bf16[128,1024]{1,0:T(8,128)(2,1)} %get-tuple-element.255), channel_id=1, source_target_pairs={{0,8},{4,12},{8,0},{12,4},{16,24},{20,28},{24,16},{28,20},{1,9},{5... | collective-permute-start | bytes 786440 | tf_op jit(solution)/shard_map/ppermute | solution.py:21
  190.2 193.5 %reduce-scatter.5.cloned.1.call-start = ((), (), s32[]{:S(2)}) async-start(), calls=%async_computation.8 | async-start | bytes 2621440 | tf_op jit(solution)/shard_map/reduce_scatter | solution.py:265
  226.3 20.8 %collective-permute-start.37 = (bf16[128,1024]{1,0:T(8,128)(2,1)}, bf16[128,1024]{1,0:T(8,128)(2,1)S(1)}, u32[]{:S(2)}, u32[]{:S(2)}) collective-permute-start(bf16[128,1024]{1,0:T(8,128)(2,1)} %get-tuple-element.269.refs_0_), channel_id=1, source_target_pairs={{0,16},{4,20},{8,24},{12,28},{16,0},{20,4},{24,8},{28,12},{1,17},{... | collective-permute-start | bytes 786440 | tf_op jit(solution)/shard_map/ppermute | solution.py:21
  228.6 18.5 %collective-permute-start.38 = (bf16[128,1024]{1,0:T(8,128)(2,1)}, bf16[128,1024]{1,0:T(8,128)(2,1)S(1)}, u32[]{:S(2)}, u32[]{:S(2)}) collective-permute-start(bf16[128,1024]{1,0:T(8,128)(2,1)} %get-tuple-element.269.refs_0_), channel_id=1, source_target_pairs={{0,24},{4,28},{8,16},{12,20},{16,8},{20,12},{24,0},{28,4},{1,25},{... | collective-permute-start | bytes 786440 | tf_op jit(solution)/shard_map/ppermute | solution.py:21
  239.4 20.1 %collective-permute-start.42 = (bf16[128,1024]{1,0:T(8,128)(2,1)S(1)}, bf16[128,1024]{1,0:T(8,128)(2,1)}, u32[]{:S(2)}, u32[]{:S(2)}) collective-permute-start(bf16[128,1024]{1,0:T(8,128)(2,1)S(1)} %copy-done.55), channel_id=1, source_target_pairs={{0,4},{4,0},{8,12},{12,8},{16,20},{20,16},{24,28},{28,24},{1,5},{5... | collective-permute-start | bytes 786440 | tf_op jit(solution)/shard_map/ppermute | solution.py:21
  293.7 21.0 %collective-permute-start.49 = (bf16[96,1024]{1,0:T(8,128)(2,1)}, bf16[96,1024]{1,0:T(8,128)(2,1)}, u32[]{:S(2)}, u32[]{:S(2)}) collective-permute-start(bf16[96,1024]{1,0:T(8,128)(2,1)} %get-tuple-element.499), channel_id=1, source_target_pairs={{0,1},{1,0},{2,3},{3,2},{4,5},{5,4},{6,7},{7,6},{8,9},{9,8},{10,11... | collective-permute-start | bytes 589832 | tf_op jit(solution)/shard_map/ppermute | solution.py:21
  295.1 22.3 %collective-permute-start.51 = (bf16[96,1024]{1,0:T(8,128)(2,1)}, bf16[96,1024]{1,0:T(8,128)(2,1)}, u32[]{:S(2)}, u32[]{:S(2)}) collective-permute-start(bf16[96,1024]{1,0:T(8,128)(2,1)} %get-tuple-element.498), channel_id=1, source_target_pairs={{0,3},{1,2},{2,1},{3,0},{4,7},{5,6},{6,5},{7,4},{8,11},{9,10},{10,... | collective-permute-start | bytes 589832 | tf_op jit(solution)/shard_map/ppermute | solution.py:21
  296.8 20.5 %collective-permute-start.50 = (bf16[96,1024]{1,0:T(8,128)(2,1)S(1)}, bf16[96,1024]{1,0:T(8,128)(2,1)}, u32[]{:S(2)}, u32[]{:S(2)}) collective-permute-start(bf16[96,1024]{1,0:T(8,128)(2,1)S(1)} %get-tuple-element.497), channel_id=1, source_target_pairs={{0,2},{1,3},{2,0},{3,1},{4,6},{5,7},{6,4},{7,5},{8,10},{9,11},{10,... | collective-permute-start | bytes 589832 | tf_op jit(solution)/shard_map/ppermute | solution.py:21
  321.4 104.3 %reduce-scatter.7.cloned.1.call-start = ((), (), s32[]{:S(2)}) async-start(), calls=%async_computation.9 | async-start | bytes 2359296 | tf_op jit(solution)/shard_map/reduce_scatter | solution.py:869
  333.1 25.5 %collective-permute-start.57 = (bf16[128,1024]{1,0:T(8,128)(2,1)}, bf16[128,1024]{1,0:T(8,128)(2,1)}, u32[]{:S(2)}, u32[]{:S(2)}) collective-permute-start(bf16[128,1024]{1,0:T(8,128)(2,1)} %get-tuple-element.295), channel_id=1, source_target_pairs={{0,16},{4,20},{8,24},{12,28},{16,0},{20,4},{24,8},{28,12},{1,17},{... | collective-permute-start | bytes 786440 | tf_op jit(solution)/shard_map/ppermute | solution.py:21
  335.2 23.4 %collective-permute-start.56 = (bf16[128,1024]{1,0:T(8,128)(2,1)}, bf16[128,1024]{1,0:T(8,128)(2,1)}, u32[]{:S(2)}, u32[]{:S(2)}) collective-permute-start(bf16[128,1024]{1,0:T(8,128)(2,1)} %get-tuple-element.294), channel_id=1, source_target_pairs={{0,8},{4,12},{8,0},{12,4},{16,24},{20,28},{24,16},{28,20},{1,9},{5... | collective-permute-start | bytes 786440 | tf_op jit(solution)/shard_map/ppermute | solution.py:21
  360.7 158.6 %all-gather.15.cloned.1.call-start = ((), (), s32[]{:S(2)}) async-start(), calls=%async_computation.11 | async-start | bytes 2621440 | tf_op jit(solution)/shard_map/all_gather | solution.py:269
  403.4 128.0 %reduce-scatter.9.cloned.1.call-start = ((), (), s32[]{:S(2)}) async-start(), calls=%async_computation.10 | async-start | bytes 4128768 | tf_op jit(solution)/shard_map/reduce_scatter | solution.py:886
  404.0 21.2 %collective-permute-start.66 = (bf16[128,1024]{1,0:T(8,128)(2,1)}, bf16[128,1024]{1,0:T(8,128)(2,1)}, u32[]{:S(2)}, u32[]{:S(2)}) collective-permute-start(bf16[128,1024]{1,0:T(8,128)(2,1)} %get-tuple-element.336.refs_0_), channel_id=1, source_target_pairs={{0,16},{4,20},{8,24},{12,28},{16,0},{20,4},{24,8},{28,12},{1,17},{... | collective-permute-start | bytes 786440 | tf_op jit(solution)/shard_map/ppermute | solution.py:21
  405.9 19.3 %collective-permute-start.67 = (bf16[128,1024]{1,0:T(8,128)(2,1)}, bf16[128,1024]{1,0:T(8,128)(2,1)}, u32[]{:S(2)}, u32[]{:S(2)}) collective-permute-start(bf16[128,1024]{1,0:T(8,128)(2,1)} %get-tuple-element.336.refs_0_), channel_id=1, source_target_pairs={{0,24},{4,28},{8,16},{12,20},{16,8},{20,12},{24,0},{28,4},{1,25},{... | collective-permute-start | bytes 786440 | tf_op jit(solution)/shard_map/ppermute | solution.py:21
  408.3 17.4 %collective-permute-start.68 = (bf16[128,1024]{1,0:T(8,128)(2,1)}, bf16[128,1024]{1,0:T(8,128)(2,1)}, u32[]{:S(2)}, u32[]{:S(2)}) collective-permute-start(bf16[128,1024]{1,0:T(8,128)(2,1)} %get-tuple-element.336.refs_0_), channel_id=1, source_target_pairs={{0,4},{4,0},{8,12},{12,8},{16,20},{20,16},{24,28},{28,24},{1,5},{5... | collective-permute-start | bytes 786440 | tf_op jit(solution)/shard_map/ppermute | solution.py:21
  434.4 20.2 %collective-permute-start.74 = (bf16[192,1024]{1,0:T(8,128)(2,1)}, bf16[192,1024]{1,0:T(8,128)(2,1)}, u32[]{:S(2)}, u32[]{:S(2)}) collective-permute-start(bf16[192,1024]{1,0:T(8,128)(2,1)} %convolution_convert_fusion.2.refs_0_), channel_id=1, source_target_pairs={{0,3},{1,2},{2,1},{3,0},{4,7},{5,6},{6,5},{7,4},{8,11},{9,10},{10,... | collective-permute-start | bytes 1179656 | tf_op jit(solution)/shard_map/ppermute | solution.py:21
  457.3 95.9 %reduce-scatter.11.cloned.1.call-start = ((), (), s32[]{:S(2)}) async-start(), calls=%async_computation.12 | async-start | bytes 2621440 | tf_op jit(solution)/shard_map/reduce_scatter | solution.py:265
  472.2 18.4 %collective-permute-start.77 = (bf16[192,1024]{1,0:T(8,128)(2,1)}, bf16[192,1024]{1,0:T(8,128)(2,1)}, u32[]{:S(2)}, u32[]{:S(2)}) collective-permute-start(bf16[192,1024]{1,0:T(8,128)(2,1)} %get-tuple-element.487), channel_id=1, source_target_pairs={{0,3},{1,2},{2,1},{3,0},{4,7},{5,6},{6,5},{7,4},{8,11},{9,10},{10,... | collective-permute-start | bytes 1179656 | tf_op jit(solution)/shard_map/ppermute | solution.py:21
  472.4 19.2 %collective-permute-start.76 = (bf16[192,1024]{1,0:T(8,128)(2,1)}, bf16[192,1024]{1,0:T(8,128)(2,1)}, u32[]{:S(2)}, u32[]{:S(2)}) collective-permute-start(bf16[192,1024]{1,0:T(8,128)(2,1)} %get-tuple-element.488), channel_id=1, source_target_pairs={{0,2},{1,3},{2,0},{3,1},{4,6},{5,7},{6,4},{7,5},{8,10},{9,11},{10,... | collective-permute-start | bytes 1179656 | tf_op jit(solution)/shard_map/ppermute | solution.py:21
  473.9 17.8 %collective-permute-start.75 = (bf16[192,1024]{1,0:T(8,128)(2,1)}, bf16[192,1024]{1,0:T(8,128)(2,1)}, u32[]{:S(2)}, u32[]{:S(2)}) collective-permute-start(bf16[192,1024]{1,0:T(8,128)(2,1)} %get-tuple-element.486), channel_id=1, source_target_pairs={{0,1},{1,0},{2,3},{3,2},{4,5},{5,4},{6,7},{7,6},{8,9},{9,8},{10,11... | collective-permute-start | bytes 1179656 | tf_op jit(solution)/shard_map/ppermute | solution.py:21
  495.8 149.7 %all-gather.17.cloned.1.call-start = ((), (), s32[]{:S(2)}) async-start(), calls=%async_computation.13 | async-start | bytes 5242880 | tf_op jit(solution)/shard_map/all_gather | solution.py:269
  502.7 20.5 %collective-permute-start.81 = (bf16[128,1024]{1,0:T(8,128)(2,1)}, bf16[128,1024]{1,0:T(8,128)(2,1)S(1)}, u32[]{:S(2)}, u32[]{:S(2)}) collective-permute-start(bf16[128,1024]{1,0:T(8,128)(2,1)} %get-tuple-element.364), channel_id=1, source_target_pairs={{0,24},{4,28},{8,16},{12,20},{16,8},{20,12},{24,0},{28,4},{1,25},{... | collective-permute-start | bytes 786440 | tf_op jit(solution)/shard_map/ppermute | solution.py:21
  506.1 24.1 %collective-permute-start.80 = (bf16[128,1024]{1,0:T(8,128)(2,1)}, bf16[128,1024]{1,0:T(8,128)(2,1)S(1)}, u32[]{:S(2)}, u32[]{:S(2)}) collective-permute-start(bf16[128,1024]{1,0:T(8,128)(2,1)} %get-tuple-element.363), channel_id=1, source_target_pairs={{0,16},{4,20},{8,24},{12,28},{16,0},{20,4},{24,8},{28,12},{1,17},{... | collective-permute-start | bytes 786440 | tf_op jit(solution)/shard_map/ppermute | solution.py:21
  507.0 23.2 %collective-permute-start.79 = (bf16[128,1024]{1,0:T(8,128)(2,1)}, bf16[128,1024]{1,0:T(8,128)(2,1)}, u32[]{:S(2)}, u32[]{:S(2)}) collective-permute-start(bf16[128,1024]{1,0:T(8,128)(2,1)} %get-tuple-element.362), channel_id=1, source_target_pairs={{0,8},{4,12},{8,0},{12,4},{16,24},{20,28},{24,16},{28,20},{1,9},{5... | collective-permute-start | bytes 786440 | tf_op jit(solution)/shard_map/ppermute | solution.py:21
  580.8 16.8 %collective-permute-start.90 = (bf16[256,768]{1,0:T(8,128)(2,1)S(1)}, bf16[256,768]{1,0:T(8,128)(2,1)S(1)}, u32[]{:S(2)}, u32[]{:S(2)}) collective-permute-start(bf16[256,768]{1,0:T(8,128)(2,1)S(1)} %slice.567), channel_id=1, source_target_pairs={{0,8},{4,12},{8,0},{12,4},{16,24},{20,28},{24,16},{28,20},{1,9},{5... | collective-permute-start | bytes 1179656 | tf_op jit(solution)/shard_map/ppermute | solution.py:21
  581.3 41.2 %collective-permute-start.103 = (bf16[128,1024]{1,0:T(8,128)(2,1)}, bf16[128,1024]{1,0:T(8,128)(2,1)}, u32[]{:S(2)}, u32[]{:S(2)}) collective-permute-start(bf16[128,1024]{1,0:T(8,128)(2,1)} %slice.568), channel_id=1, source_target_pairs={{0,16},{4,20},{8,24},{12,28},{16,0},{20,4},{24,8},{28,12},{1,17},{... | collective-permute-start | bytes 786440 | tf_op jit(solution)/shard_map/ppermute | solution.py:21
  588.9 24.8 %collective-permute-start.94 = (bf16[128,1024]{1,0:T(8,128)(2,1)}, bf16[128,1024]{1,0:T(8,128)(2,1)S(1)}, u32[]{:S(2)}, u32[]{:S(2)}) collective-permute-start(bf16[128,1024]{1,0:T(8,128)(2,1)} %get-tuple-element.409), channel_id=1, source_target_pairs={{0,3},{1,2},{2,1},{3,0},{4,7},{5,6},{6,5},{7,4},{8,11},{9,10},{10,... | collective-permute-start | bytes 786440 | tf_op jit(solution)/shard_map/ppermute | solution.py:21
  598.8 16.3 %collective-permute-start.91 = (bf16[128,768]{1,0:T(8,128)(2,1)S(1)}, bf16[128,768]{1,0:T(8,128)(2,1)S(1)}, u32[]{:S(2)}, u32[]{:S(2)}) collective-permute-start(bf16[128,768]{1,0:T(8,128)(2,1)S(1)} %fusion.162), channel_id=1, source_target_pairs={{0,16},{4,20},{8,24},{12,28},{16,0},{20,4},{24,8},{28,12},{1,17},{... | collective-permute-start | bytes 589832 | tf_op jit(solution)/shard_map/ppermute | solution.py:21
  625.3 25.1 %collective-permute-start.100 = (bf16[128,768]{1,0:T(8,128)(2,1)S(1)}, bf16[128,768]{1,0:T(8,128)(2,1)S(1)}, u32[]{:S(2)}, u32[]{:S(2)}) collective-permute-start(bf16[128,768]{1,0:T(8,128)(2,1)S(1)} %add_convert_fusion.6.refs_0_), channel_id=1, source_target_pairs={{0,1},{1,0},{2,3},{3,2},{4,5},{5,4},{6,7},{7,6},{8,9},{9,8},{10,11... | collective-permute-start | bytes 589832 | tf_op jit(solution)/shard_map/ppermute | solution.py:21
  626.6 23.8 %collective-permute-start.101 = (bf16[128,768]{1,0:T(8,128)(2,1)S(1)}, bf16[128,768]{1,0:T(8,128)(2,1)S(1)}, u32[]{:S(2)}, u32[]{:S(2)}) collective-permute-start(bf16[128,768]{1,0:T(8,128)(2,1)S(1)} %add_convert_fusion.6.refs_0_), channel_id=1, source_target_pairs={{0,2},{1,3},{2,0},{3,1},{4,6},{5,7},{6,4},{7,5},{8,10},{9,11},{10,... | collective-permute-start | bytes 589832 | tf_op jit(solution)/shard_map/ppermute | solution.py:21
  627.7 22.8 %collective-permute-start.102 = (bf16[128,768]{1,0:T(8,128)(2,1)S(1)}, bf16[128,768]{1,0:T(8,128)(2,1)S(1)}, u32[]{:S(2)}, u32[]{:S(2)}) collective-permute-start(bf16[128,768]{1,0:T(8,128)(2,1)S(1)} %add_convert_fusion.6.refs_0_), channel_id=1, source_target_pairs={{0,3},{1,2},{2,1},{3,0},{4,7},{5,6},{6,5},{7,4},{8,11},{9,10},{10,... | collective-permute-start | bytes 589832 | tf_op jit(solution)/shard_map/ppermute | solution.py:21
  (202 other events, 1640.8 us)
Sparse Core Ops, SparseCore 0:
  35.3 31.4 all-gather.6
  98.4 28.0 all-gather.10
  128.1 30.1 all-gather.8
  190.3 27.5 all-gather.12
  321.5 34.7 reduce-scatter.4
  360.8 34.2 reduce-scatter.6
  403.5 33.7 all-gather.14
  457.4 44.3 reduce-scatter.8
  505.3 33.5 reduce-scatter.10
  555.6 63.4 all-gather.16

commit v4 on v3

--- a/solution.py
+++ b/solution.py
@@ -358,14 +358,6 @@
     bits = narrow.bit_length() - 1
     for b in range(bits):
         value = value + swap(low(value), "narrow", 1 << (b + first) % bits).astype(F32)
-    return value
-
-
-def narrow_rest(value):
-    distance = 2
-    while distance < lax.axis_size("narrow"):
-        value = value + swap(low(value), "narrow", distance).astype(F32)
-        distance *= 2
     return value
 
 
@@ -767,10 +759,16 @@
         in_pieces, split_gathered(after(gathered, in_sum), rows, narrow_columns)
     )
     vectors = axis_sum(jnp.concatenate([axis_sum(first, "narrow"), early], axis=0), "wide")
-    out_sum = narrow_rest(after(out_sum, in_sum))
-    return (
-        grad_inputs, (spread_columns(in_pieces, at_narrow), out_sum), vectors, gathered
-    )
+    spread = spread_columns(in_pieces, at_narrow)
+    out_sum = after(out_sum, in_sum)
+    distance = 2
+    while distance < narrow:
+        received = swap(low(out_sum), "narrow", distance)
+        distance *= 2
+        if distance >= narrow:
+            received = after(received, spread)
+        out_sum = out_sum + received.astype(F32)
+    return grad_inputs, (spread, out_sum), vectors, gathered
 
 
 def body(

time: 670 us -> 664 us (level)
  waiting for transfers between devices: 219 us -> 212 us
    unnamed x269 -> x265, local copies, waits for them, and re-layouts: 14.2 us -> 13.5 us
  transfers between devices with their start and end apart: 116 -> 116, of which waited for: 53 -> 55; matrix products, arithmetic and copies ran while one was open for 24% -> 24% of each run, Pallas kernels for 16% -> 17%
where the time goes in v4:
time: 664 us; the launch traced here: 655 us
  waiting for transfers between devices  212 us (32%)
  Pallas kernels  124 us (19%)
  starting transfers between devices  113 us (17%)
  matrix products  111 us (17%)
  other arithmetic  49.5 us (7%)
  local copies, waits for them, and re-layouts  28.5 us (4%)
  between operations  16.4 us (2%)
    ppermute x106, waiting for transfers between devices, swap(): lax.ppermute(array, axis, [(i, i ^ distance) for i in range(lax.axis_size...  205 us
    pallas_call x34, Pallas kernels, call(): pl.pallas_call(kernel, out_shape=tuple(outs), in_specs=[smem()] * len(sca...  124 us
    ppermute x106, starting transfers between devices, swap(): lax.ppermute(array, axis, [(i, i ^ distance) for i in range(lax.axis_size...  110 us
    dot_general x36, matrix products, product(): lax.dot_general(left, right, (((left_dim,), (right_dim,)), ((), ())), pre...  82.7 us
    unnamed x265, local copies, waits for them, and re-layouts  13.5 us
  transfers between devices with their start and end apart: 116, of which 55 were waited for; matrix products, arithmetic and copies ran while one was open for 24% of the time, Pallas kernels for 17%

profile of v4, /device:TPU:0, one launch (start us, length us, event | category | flops | bytes accessed | tf_op | source)
XLA Modules:
  0.0 654.7 jit_solution(15239332602092815622)
XLA Ops:
  25.7 9.3 %collective-permute-done.1.refs_4_ = bf16[136,768]{1,0:T(8,128)(2,1)S(1)} collective-permute-done((bf16[136,768]{1,0:T(8,128)(2,1)}, bf16[136,768]{1,0:T(8,128)(2,1)S(1)}, u32[]{:S(2)}, u32[]{:S(2)}) %collective-permute-start.1) | collective-permute-done | bytes 208928 | tf_op jit(solution)/shard_map/ppermute | solution.py:21
  42.8 9.1 %shard_map.395 = (bf16[4,128,768]{2,1,0:T(8,128)(2,1)}, f32[128,16]{1,0:T(8,128)}, bf16[128,256]{1,0:T(8,128)(2,1)}, bf16[128,256]{1,0:T(8,128)(2,1)}, bf16[128,...) custom-call(s32[4]{0:T(128)} %gather_fusion.1, ...), custom_call_target="tpu_custom_call" | custom-call | flops 805306368 | bytes 4730880 | tf_op jit(solution)/shard_map/pallas_call | solution.py:40
  60.4 6.4 all-gather.7.cloned.1.call-done.weight_ref
  66.8 3.4 shard_map.396
  74.6 9.0 %collective-permute-done.13.refs_1_ = bf16[128,1024]{1,0:T(8,128)(2,1)S(1)} collective-permute-done((bf16[128,1024]{1,0:T(8,128)(2,1)}, bf16[128,1024]{1,0:T(8,128)(2,1)S(1)}, u32[]{:S(2)}, u32[]{:S(2)}) %collective-permute-start.13) | collective-permute-done | bytes 262176 | tf_op jit(solution)/shard_map/ppermute | solution.py:21
  83.6 9.6 %collective-permute-done.14.refs_2_ = bf16[128,1024]{1,0:T(8,128)(2,1)S(1)} collective-permute-done((bf16[128,1024]{1,0:T(8,128)(2,1)}, bf16[128,1024]{1,0:T(8,128)(2,1)S(1)}, u32[]{:S(2)}, u32[]{:S(2)}) %collective-permute-start.14) | collective-permute-done | bytes 262176 | tf_op jit(solution)/shard_map/ppermute | solution.py:21
  107.3 3.2 fusion.43
  110.5 4.5 collective-permute-done.20.refs_1_
  115.0 8.8 %collective-permute-done.21.refs_2_ = bf16[192,1024]{1,0:T(8,128)(2,1)S(1)} collective-permute-done((bf16[192,1024]{1,0:T(8,128)(2,1)S(1)}, bf16[192,1024]{1,0:T(8,128)(2,1)S(1)}, u32[]{:S(2)}, u32[]{:S(2)}) %collective-permute-start.21) | collective-permute-done | bytes 393248 | tf_op jit(solution)/shard_map/ppermute | solution.py:21
  127.5 5.5 multiply_convert_fusion.4
  139.2 8.7 %collective-permute-done.25 = bf16[192,1024]{1,0:T(8,128)(2,1)S(1)} collective-permute-done((bf16[192,1024]{1,0:T(8,128)(2,1)S(1)}, bf16[192,1024]{1,0:T(8,128)(2,1)S(1)}, u32[]{:S(2)}, u32[]{:S(2)}) %collective-permute-start.25) | collective-permute-done | bytes 393248 | tf_op jit(solution)/shard_map/ppermute | solution.py:21
  147.9 5.9 collective-permute-done.24
  163.2 4.3 collective-permute-start.28
  167.5 5.2 collective-permute-done.29
  172.7 16.1 %collective-permute-done.28 = bf16[128,1024]{1,0:T(8,128)(2,1)S(1)} collective-permute-done((bf16[128,1024]{1,0:T(8,128)(2,1)}, bf16[128,1024]{1,0:T(8,128)(2,1)S(1)}, u32[]{:S(2)}, u32[]{:S(2)}) %collective-permute-start.28) | collective-permute-done | bytes 262176 | tf_op jit(solution)/shard_map/ppermute | solution.py:21
  196.6 5.2 collective-permute-done.30.refs_1_
  201.7 5.3 collective-permute-done.31.refs_2_
  207.0 8.1 %shard_map.400 = (bf16[4,128,768]{2,1,0:T(8,128)(2,1)}, f32[128,16]{1,0:T(8,128)}, bf16[128,256]{1,0:T(8,128)(2,1)}, bf16[128,256]{1,0:T(8,128)(2,1)}, bf16[128,...) custom-call(s32[4]{0:T(128)} %gather_fusion.1, bf16[128,1024]{1,0:T(8,128)(2,1)} %copy-done.39, ...), custom_call_target="tpu_custom_call" | custom-call | flops 805306368 | bytes 3678208 | tf_op jit(solution)/shard_map/pallas_call | solution.py:40
  222.9 3.4 shard_map.401
  239.4 7.7 %collective-permute-done.37.refs_2_ = bf16[128,1024]{1,0:T(8,128)(2,1)S(1)} collective-permute-done((bf16[128,1024]{1,0:T(8,128)(2,1)}, bf16[128,1024]{1,0:T(8,128)(2,1)S(1)}, u32[]{:S(2)}, u32[]{:S(2)}) %collective-permute-start.37) | collective-permute-done | bytes 262176 | tf_op jit(solution)/shard_map/ppermute | solution.py:21
  252.9 4.5 collective-permute-done.41.refs_3_
  272.5 3.7 fusion.6
  281.4 4.4 fusion.2
  346.8 11.8 %collective-permute-done.57 = bf16[128,1024]{1,0:T(8,128)(2,1)} collective-permute-done((bf16[128,1024]{1,0:T(8,128)(2,1)}, bf16[128,1024]{1,0:T(8,128)(2,1)}, u32[]{:S(2)}, u32[]{:S(2)}) %collective-permute-start.57) | collective-permute-done | bytes 262176 | tf_op jit(solution)/shard_map/ppermute | solution.py:21
  376.3 7.5 %shard_map.410.grad_ref.refs_4_ = bf16[512,768]{1,0:T(8,128)(2,1)} custom-call(s32[4]{0:T(128)} %gather_fusion.1, bf16[4,128,768]{2,1,0:T(8,128)(2,1)} %get-tuple-element.308.packed_ref, f32[128,16]{1,0:T(8,128)} %get-tuple-element.309.level_ref, bf16[128,256]{1,0:T(8,128)(2,1)} %get-tuple-element.310.refs_0_, bf16[128,256]{1,0:T(8,128)(2,1)} %copy-done.92, ...), custom_call_target="tpu_custom_call" | custom-call | bytes 1843200 | tf_op jit(solution)/shard_map/pallas_call | solution.py:40
  383.8 3.6 shard_map.411
  391.0 7.5 %fusion.72 = f32[2048,1024]{1,0:T(8,128)} fusion(bf16[384,2048]{1,0:T(8,128)(2,1)} %copy-done.12, bf16[384,1024]{1,0:T(8,128)(2,1)} %shard_map.403, f32[384]{0:T(512)S(1)} %reduce.4), kind=kOutput, calls=%fused_computation.118 | convolution fusion | flops 1611792384 | bytes 10749440 | tf_op jit(solution)/shard_map/dot_general | solution.py:25
  408.5 5.9 collective-permute-done.65.refs_1_
  414.4 10.8 %collective-permute-done.66.refs_2_ = bf16[128,1024]{1,0:T(8,128)(2,1)} collective-permute-done((bf16[128,1024]{1,0:T(8,128)(2,1)}, bf16[128,1024]{1,0:T(8,128)(2,1)}, u32[]{:S(2)}, u32[]{:S(2)}) %collective-permute-start.66) | collective-permute-done | bytes 262176 | tf_op jit(solution)/shard_map/ppermute | solution.py:21
  437.0 5.8 multiply_reduce_fusion.5
  442.8 5.0 shard_map.414
  447.9 6.8 %collective-permute-done.74.refs_3_ = bf16[192,1024]{1,0:T(8,128)(2,1)} collective-permute-done((bf16[192,1024]{1,0:T(8,128)(2,1)}, bf16[192,1024]{1,0:T(8,128)(2,1)}, u32[]{:S(2)}, u32[]{:S(2)}) %collective-permute-start.74) | collective-permute-done | bytes 393248 | tf_op jit(solution)/shard_map/ppermute | solution.py:21
  460.0 7.6 %multiply_reduce_fusion.3 = (f32[768]{0:T(1024)S(1)}, bf16[768,1024]{1,0:T(8,128)(2,1)S(1)}) fusion(bf16[768,1024]{1,0:T(8,128)(2,1)} %copy-done.127, f32[768,1024]{1,0:T(8,128)} %get-tuple-element.548, f32[768]{0:T(1024)S(1)} %get-tuple-element.520, bf16[768,1024]{1,0:T(8,128)(2,1)} %shard_map.413, bf16[1,1024,1024]{2,1,0:T(8,128)(2,1)} %param.38), kind=kOutput, calls=%fused_computation.36 | convolution fusion | flops 1629486336 | bytes 9967616 | tf_op jit(solution)/shard_map/dot_general | solution.py:25
  467.6 3.5 fusion.178
  483.3 7.2 %fusion.180 = f32[1024,2048]{1,0:T(8,128)} fusion(bf16[384,1024]{1,0:T(8,128)(2,1)S(1)} %copy-done.11, bf16[384,2048]{1,0:T(8,128)(2,1)} %copy-done.14), kind=kOutput, calls=%fused_computation.333 | convolution fusion | flops 1610612736 | bytes 10747904 | tf_op jit(solution)/shard_map/dot_general | solution.py:25
  502.6 3.5 collective-permute-start.81
  511.3 4.0 fusion.66
  515.3 3.9 fusion.181
  519.1 3.9 shard_map.417
  523.0 7.2 %collective-permute-done.80 = bf16[128,1024]{1,0:T(8,128)(2,1)S(1)} collective-permute-done((bf16[128,1024]{1,0:T(8,128)(2,1)}, bf16[128,1024]{1,0:T(8,128)(2,1)S(1)}, u32[]{:S(2)}, u32[]{:S(2)}) %collective-permute-start.80) | collective-permute-done | bytes 262176 | tf_op jit(solution)/shard_map/ppermute | solution.py:21
  539.5 3.9 collective-permute-done.84.refs_3_
  556.9 7.5 %shard_map.420.refs_4_.grad_ref = bf16[512,768]{1,0:T(8,128)(2,1)} custom-call(s32[4]{0:T(128)} %gather_fusion.1, bf16[4,128,768]{2,1,0:T(8,128)(2,1)} %get-tuple-element.334.packed_ref, f32[128,16]{1,0:T(8,128)} %get-tuple-element.335.level_ref, bf16[128,256]{1,0:T(8,128)(2,1)} %get-tuple-element.391.refs_0_, bf16[128,256]{1,0:T(8,128)(2,1)} %copy-done.84, ...), custom_call_target="tpu_custom_call" | custom-call | bytes 1843200 | tf_op jit(solution)/shard_map/pallas_call | solution.py:40
  564.4 5.2 collective-permute-done.86
  574.3 3.8 shard_map.421
  585.6 3.5 shard_map.422
  592.7 7.3 %collective-permute-done.90 = bf16[256,768]{1,0:T(8,128)(2,1)S(1)} collective-permute-done((bf16[256,768]{1,0:T(8,128)(2,1)S(1)}, bf16[256,768]{1,0:T(8,128)(2,1)S(1)}, u32[]{:S(2)}, u32[]{:S(2)}) %collective-permute-start.90) | collective-permute-done | bytes 393248 | tf_op jit(solution)/shard_map/ppermute | solution.py:21
  605.4 10.1 %collective-permute-done.94 = bf16[128,1024]{1,0:T(8,128)(2,1)S(1)} collective-permute-done((bf16[128,1024]{1,0:T(8,128)(2,1)}, bf16[128,1024]{1,0:T(8,128)(2,1)S(1)}, u32[]{:S(2)}, u32[]{:S(2)}) %collective-permute-start.94) | collective-permute-done | bytes 262176 | tf_op jit(solution)/shard_map/ppermute | solution.py:21
  637.7 5.0 shard_map.424
  (674 shorter events, 335.2 us)
Async XLA Ops:
  7.2 59.6 %all-gather.7.cloned.1.call-start = ((), (), s32[]{:S(2)}) async-start(), calls=%async_computation.4 | async-start | bytes 2359296 | tf_op jit(solution)/shard_map/all_gather | solution.py:287
  14.3 20.7 %collective-permute-start.3 = (bf16[128,1024]{1,0:T(8,128)(2,1)}, bf16[128,1024]{1,0:T(8,128)(2,1)S(1)}, u32[]{:S(2)}, u32[]{:S(2)}) collective-permute-start(bf16[128,1024]{1,0:T(8,128)(2,1)} %refs_0_), channel_id=1, source_target_pairs={{0,1},{1,0},{2,3},{3,2},{4,5},{5,4},{6,7},{7,6},{8,9},{9,8},{10,11... | collective-permute-start | bytes 786440 | tf_op jit(solution)/shard_map/ppermute | solution.py:21
  15.8 19.3 %collective-permute-start.4 = (bf16[128,1024]{1,0:T(8,128)(2,1)}, bf16[128,1024]{1,0:T(8,128)(2,1)S(1)}, u32[]{:S(2)}, u32[]{:S(2)}) collective-permute-start(bf16[128,1024]{1,0:T(8,128)(2,1)} %refs_0_), channel_id=1, source_target_pairs={{0,2},{1,3},{2,0},{3,1},{4,6},{5,7},{6,4},{7,5},{8,10},{9,11},{10,... | collective-permute-start | bytes 786440 | tf_op jit(solution)/shard_map/ppermute | solution.py:21
  17.3 17.8 %collective-permute-start.5 = (bf16[128,1024]{1,0:T(8,128)(2,1)}, bf16[128,1024]{1,0:T(8,128)(2,1)S(1)}, u32[]{:S(2)}, u32[]{:S(2)}) collective-permute-start(bf16[128,1024]{1,0:T(8,128)(2,1)} %refs_0_), channel_id=1, source_target_pairs={{0,3},{1,2},{2,1},{3,0},{4,7},{5,6},{6,5},{7,4},{8,11},{9,10},{10,... | collective-permute-start | bytes 786440 | tf_op jit(solution)/shard_map/ppermute | solution.py:21
  17.8 17.2 %collective-permute-start.1 = (bf16[136,768]{1,0:T(8,128)(2,1)}, bf16[136,768]{1,0:T(8,128)(2,1)S(1)}, u32[]{:S(2)}, u32[]{:S(2)}) collective-permute-start(bf16[136,768]{1,0:T(8,128)(2,1)} %shard_map.392.refs_0_), channel_id=1, source_target_pairs={{0,16},{4,20},{8,24},{12,28},{16,0},{20,4},{24,8},{28,12},{1,17},{... | collective-permute-start | bytes 626696 | tf_op jit(solution)/shard_map/ppermute | solution.py:21
  35.1 171.9 %all-gather.11.cloned.1.call-start = ((), (), s32[]{:S(2)}) async-start(), calls=%async_computation.6 | async-start | bytes 1769472 | tf_op jit(solution)/shard_map/all_gather | solution.py:287
  71.7 21.5 %collective-permute-start.14 = (bf16[128,1024]{1,0:T(8,128)(2,1)}, bf16[128,1024]{1,0:T(8,128)(2,1)S(1)}, u32[]{:S(2)}, u32[]{:S(2)}) collective-permute-start(bf16[128,1024]{1,0:T(8,128)(2,1)} %get-tuple-element.249.refs_0_), channel_id=1, source_target_pairs={{0,16},{4,20},{8,24},{12,28},{16,0},{20,4},{24,8},{28,12},{1,17},{... | collective-permute-start | bytes 786440 | tf_op jit(solution)/shard_map/ppermute | solution.py:21
  72.6 20.6 %collective-permute-start.15 = (bf16[128,1024]{1,0:T(8,128)(2,1)}, bf16[128,1024]{1,0:T(8,128)(2,1)S(1)}, u32[]{:S(2)}, u32[]{:S(2)}) collective-permute-start(bf16[128,1024]{1,0:T(8,128)(2,1)} %get-tuple-element.249.refs_0_), channel_id=1, source_target_pairs={{0,24},{4,28},{8,16},{12,20},{16,8},{20,12},{24,0},{28,4},{1,25},{... | collective-permute-start | bytes 786440 | tf_op jit(solution)/shard_map/ppermute | solution.py:21
  74.6 19.1 %collective-permute-start.16 = (bf16[128,1024]{1,0:T(8,128)(2,1)}, bf16[128,1024]{1,0:T(8,128)(2,1)S(1)}, u32[]{:S(2)}, u32[]{:S(2)}) collective-permute-start(bf16[128,1024]{1,0:T(8,128)(2,1)} %get-tuple-element.249.refs_0_), channel_id=1, source_target_pairs={{0,4},{4,0},{8,12},{12,8},{16,20},{20,16},{24,28},{28,24},{1,5},{5... | collective-permute-start | bytes 786440 | tf_op jit(solution)/shard_map/ppermute | solution.py:21
  98.2 124.0 %all-gather.9.cloned.1.call-start = ((), (), s32[]{:S(2)}) async-start(), calls=%async_computation.5 | async-start | bytes 2359296 | tf_op jit(solution)/shard_map/all_gather | solution.py:287
  104.5 19.3 %collective-permute-start.21 = (bf16[192,1024]{1,0:T(8,128)(2,1)S(1)}, bf16[192,1024]{1,0:T(8,128)(2,1)S(1)}, u32[]{:S(2)}, u32[]{:S(2)}) collective-permute-start(bf16[192,1024]{1,0:T(8,128)(2,1)S(1)} %convolution_convert_fusion.3.refs_0_), channel_id=1, source_target_pairs={{0,2},{1,3},{2,0},{3,1},{4,6},{5,7},{6,4},{7,5},{8,10},{9,11},{10,... | collective-permute-start | bytes 1179656 | tf_op jit(solution)/shard_map/ppermute | solution.py:21
  106.0 17.8 %collective-permute-start.22 = (bf16[192,1024]{1,0:T(8,128)(2,1)S(1)}, bf16[192,1024]{1,0:T(8,128)(2,1)}, u32[]{:S(2)}, u32[]{:S(2)}) collective-permute-start(bf16[192,1024]{1,0:T(8,128)(2,1)S(1)} %convolution_convert_fusion.3.refs_0_), channel_id=1, source_target_pairs={{0,3},{1,2},{2,1},{3,0},{4,7},{5,6},{6,5},{7,4},{8,11},{9,10},{10,... | collective-permute-start | bytes 1179656 | tf_op jit(solution)/shard_map/ppermute | solution.py:21
  127.2 103.5 %all-gather.13.cloned.1.call-start = ((), (), s32[]{:S(2)}) async-start(), calls=%async_computation.7 | async-start | bytes 2359296 | tf_op jit(solution)/shard_map/all_gather | solution.py:287
  136.4 17.3 %collective-permute-start.24 = (bf16[192,1024]{1,0:T(8,128)(2,1)S(1)}, bf16[192,1024]{1,0:T(8,128)(2,1)S(1)}, u32[]{:S(2)}, u32[]{:S(2)}) collective-permute-start(bf16[192,1024]{1,0:T(8,128)(2,1)S(1)} %get-tuple-element.493), channel_id=1, source_target_pairs={{0,2},{1,3},{2,0},{3,1},{4,6},{5,7},{6,4},{7,5},{8,10},{9,11},{10,... | collective-permute-start | bytes 1179656 | tf_op jit(solution)/shard_map/ppermute | solution.py:21
  137.0 16.8 %collective-permute-start.23 = (bf16[192,1024]{1,0:T(8,128)(2,1)S(1)}, bf16[192,1024]{1,0:T(8,128)(2,1)S(1)}, u32[]{:S(2)}, u32[]{:S(2)}) collective-permute-start(bf16[192,1024]{1,0:T(8,128)(2,1)S(1)} %get-tuple-element.491), channel_id=1, source_target_pairs={{0,1},{1,0},{2,3},{3,2},{4,5},{5,4},{6,7},{7,6},{8,9},{9,8},{10,11... | collective-permute-start | bytes 1179656 | tf_op jit(solution)/shard_map/ppermute | solution.py:21
  163.2 25.6 %collective-permute-start.28 = (bf16[128,1024]{1,0:T(8,128)(2,1)}, bf16[128,1024]{1,0:T(8,128)(2,1)S(1)}, u32[]{:S(2)}, u32[]{:S(2)}) collective-permute-start(bf16[128,1024]{1,0:T(8,128)(2,1)} %get-tuple-element.257), channel_id=1, source_target_pairs={{0,16},{4,20},{8,24},{12,28},{16,0},{20,4},{24,8},{28,12},{1,17},{... | collective-permute-start | bytes 786440 | tf_op jit(solution)/shard_map/ppermute | solution.py:21
  167.5 21.2 %collective-permute-start.27 = (bf16[128,1024]{1,0:T(8,128)(2,1)}, bf16[128,1024]{1,0:T(8,128)(2,1)S(1)}, u32[]{:S(2)}, u32[]{:S(2)}) collective-permute-start(bf16[128,1024]{1,0:T(8,128)(2,1)} %get-tuple-element.256), channel_id=1, source_target_pairs={{0,8},{4,12},{8,0},{12,4},{16,24},{20,28},{24,16},{28,20},{1,9},{5... | collective-permute-start | bytes 786440 | tf_op jit(solution)/shard_map/ppermute | solution.py:21
  190.2 193.6 %reduce-scatter.5.cloned.1.call-start = ((), (), s32[]{:S(2)}) async-start(), calls=%async_computation.8 | async-start | bytes 2621440 | tf_op jit(solution)/shard_map/reduce_scatter | solution.py:265
  226.3 20.9 %collective-permute-start.37 = (bf16[128,1024]{1,0:T(8,128)(2,1)}, bf16[128,1024]{1,0:T(8,128)(2,1)S(1)}, u32[]{:S(2)}, u32[]{:S(2)}) collective-permute-start(bf16[128,1024]{1,0:T(8,128)(2,1)} %get-tuple-element.270.refs_0_), channel_id=1, source_target_pairs={{0,16},{4,20},{8,24},{12,28},{16,0},{20,4},{24,8},{28,12},{1,17},{... | collective-permute-start | bytes 786440 | tf_op jit(solution)/shard_map/ppermute | solution.py:21
  228.7 18.5 %collective-permute-start.38 = (bf16[128,1024]{1,0:T(8,128)(2,1)}, bf16[128,1024]{1,0:T(8,128)(2,1)S(1)}, u32[]{:S(2)}, u32[]{:S(2)}) collective-permute-start(bf16[128,1024]{1,0:T(8,128)(2,1)} %get-tuple-element.270.refs_0_), channel_id=1, source_target_pairs={{0,24},{4,28},{8,16},{12,20},{16,8},{20,12},{24,0},{28,4},{1,25},{... | collective-permute-start | bytes 786440 | tf_op jit(solution)/shard_map/ppermute | solution.py:21
  239.4 20.2 %collective-permute-start.42 = (bf16[128,1024]{1,0:T(8,128)(2,1)S(1)}, bf16[128,1024]{1,0:T(8,128)(2,1)}, u32[]{:S(2)}, u32[]{:S(2)}) collective-permute-start(bf16[128,1024]{1,0:T(8,128)(2,1)S(1)} %copy-done.55), channel_id=1, source_target_pairs={{0,4},{4,0},{8,12},{12,8},{16,20},{20,16},{24,28},{28,24},{1,5},{5... | collective-permute-start | bytes 786440 | tf_op jit(solution)/shard_map/ppermute | solution.py:21
  293.8 20.9 %collective-permute-start.49 = (bf16[96,1024]{1,0:T(8,128)(2,1)}, bf16[96,1024]{1,0:T(8,128)(2,1)}, u32[]{:S(2)}, u32[]{:S(2)}) collective-permute-start(bf16[96,1024]{1,0:T(8,128)(2,1)} %get-tuple-element.501), channel_id=1, source_target_pairs={{0,1},{1,0},{2,3},{3,2},{4,5},{5,4},{6,7},{7,6},{8,9},{9,8},{10,11... | collective-permute-start | bytes 589832 | tf_op jit(solution)/shard_map/ppermute | solution.py:21
  295.2 22.2 %collective-permute-start.51 = (bf16[96,1024]{1,0:T(8,128)(2,1)}, bf16[96,1024]{1,0:T(8,128)(2,1)}, u32[]{:S(2)}, u32[]{:S(2)}) collective-permute-start(bf16[96,1024]{1,0:T(8,128)(2,1)} %get-tuple-element.500), channel_id=1, source_target_pairs={{0,3},{1,2},{2,1},{3,0},{4,7},{5,6},{6,5},{7,4},{8,11},{9,10},{10,... | collective-permute-start | bytes 589832 | tf_op jit(solution)/shard_map/ppermute | solution.py:21
  296.8 20.6 %collective-permute-start.50 = (bf16[96,1024]{1,0:T(8,128)(2,1)S(1)}, bf16[96,1024]{1,0:T(8,128)(2,1)}, u32[]{:S(2)}, u32[]{:S(2)}) collective-permute-start(bf16[96,1024]{1,0:T(8,128)(2,1)S(1)} %get-tuple-element.499), channel_id=1, source_target_pairs={{0,2},{1,3},{2,0},{3,1},{4,6},{5,7},{6,4},{7,5},{8,10},{9,11},{10,... | collective-permute-start | bytes 589832 | tf_op jit(solution)/shard_map/ppermute | solution.py:21
  321.4 104.3 %reduce-scatter.7.cloned.1.call-start = ((), (), s32[]{:S(2)}) async-start(), calls=%async_computation.9 | async-start | bytes 2359296 | tf_op jit(solution)/shard_map/reduce_scatter | solution.py:867
  330.9 15.9 %collective-permute-start.58 = (bf16[128,1024]{1,0:T(8,128)(2,1)}, bf16[128,1024]{1,0:T(8,128)(2,1)}, u32[]{:S(2)}, u32[]{:S(2)}) collective-permute-start(bf16[128,1024]{1,0:T(8,128)(2,1)} %get-tuple-element.297), channel_id=1, source_target_pairs={{0,24},{4,28},{8,16},{12,20},{16,8},{20,12},{24,0},{28,4},{1,25},{... | collective-permute-start | bytes 786440 | tf_op jit(solution)/shard_map/ppermute | solution.py:21
  333.1 25.5 %collective-permute-start.57 = (bf16[128,1024]{1,0:T(8,128)(2,1)}, bf16[128,1024]{1,0:T(8,128)(2,1)}, u32[]{:S(2)}, u32[]{:S(2)}) collective-permute-start(bf16[128,1024]{1,0:T(8,128)(2,1)} %get-tuple-element.296), channel_id=1, source_target_pairs={{0,16},{4,20},{8,24},{12,28},{16,0},{20,4},{24,8},{28,12},{1,17},{... | collective-permute-start | bytes 786440 | tf_op jit(solution)/shard_map/ppermute | solution.py:21
  335.2 23.4 %collective-permute-start.56 = (bf16[128,1024]{1,0:T(8,128)(2,1)}, bf16[128,1024]{1,0:T(8,128)(2,1)}, u32[]{:S(2)}, u32[]{:S(2)}) collective-permute-start(bf16[128,1024]{1,0:T(8,128)(2,1)} %get-tuple-element.295), channel_id=1, source_target_pairs={{0,8},{4,12},{8,0},{12,4},{16,24},{20,28},{24,16},{28,20},{1,9},{5... | collective-permute-start | bytes 786440 | tf_op jit(solution)/shard_map/ppermute | solution.py:21
  360.7 158.5 %all-gather.15.cloned.1.call-start = ((), (), s32[]{:S(2)}) async-start(), calls=%async_computation.11 | async-start | bytes 2621440 | tf_op jit(solution)/shard_map/all_gather | solution.py:269
  403.5 127.8 %reduce-scatter.9.cloned.1.call-start = ((), (), s32[]{:S(2)}) async-start(), calls=%async_computation.10 | async-start | bytes 4128768 | tf_op jit(solution)/shard_map/reduce_scatter | solution.py:884
  404.1 21.1 %collective-permute-start.66 = (bf16[128,1024]{1,0:T(8,128)(2,1)}, bf16[128,1024]{1,0:T(8,128)(2,1)}, u32[]{:S(2)}, u32[]{:S(2)}) collective-permute-start(bf16[128,1024]{1,0:T(8,128)(2,1)} %get-tuple-element.337.refs_0_), channel_id=1, source_target_pairs={{0,16},{4,20},{8,24},{12,28},{16,0},{20,4},{24,8},{28,12},{1,17},{... | collective-permute-start | bytes 786440 | tf_op jit(solution)/shard_map/ppermute | solution.py:21
  406.0 19.2 %collective-permute-start.67 = (bf16[128,1024]{1,0:T(8,128)(2,1)}, bf16[128,1024]{1,0:T(8,128)(2,1)}, u32[]{:S(2)}, u32[]{:S(2)}) collective-permute-start(bf16[128,1024]{1,0:T(8,128)(2,1)} %get-tuple-element.337.refs_0_), channel_id=1, source_target_pairs={{0,24},{4,28},{8,16},{12,20},{16,8},{20,12},{24,0},{28,4},{1,25},{... | collective-permute-start | bytes 786440 | tf_op jit(solution)/shard_map/ppermute | solution.py:21
  408.5 17.3 %collective-permute-start.68 = (bf16[128,1024]{1,0:T(8,128)(2,1)}, bf16[128,1024]{1,0:T(8,128)(2,1)}, u32[]{:S(2)}, u32[]{:S(2)}) collective-permute-start(bf16[128,1024]{1,0:T(8,128)(2,1)} %get-tuple-element.337.refs_0_), channel_id=1, source_target_pairs={{0,4},{4,0},{8,12},{12,8},{16,20},{20,16},{24,28},{28,24},{1,5},{5... | collective-permute-start | bytes 786440 | tf_op jit(solution)/shard_map/ppermute | solution.py:21
  434.5 20.2 %collective-permute-start.74 = (bf16[192,1024]{1,0:T(8,128)(2,1)}, bf16[192,1024]{1,0:T(8,128)(2,1)}, u32[]{:S(2)}, u32[]{:S(2)}) collective-permute-start(bf16[192,1024]{1,0:T(8,128)(2,1)} %convolution_convert_fusion.2.refs_0_), channel_id=1, source_target_pairs={{0,3},{1,2},{2,1},{3,0},{4,7},{5,6},{6,5},{7,4},{8,11},{9,10},{10,... | collective-permute-start | bytes 1179656 | tf_op jit(solution)/shard_map/ppermute | solution.py:21
  457.3 95.7 %reduce-scatter.11.cloned.1.call-start = ((), (), s32[]{:S(2)}) async-start(), calls=%async_computation.12 | async-start | bytes 2621440 | tf_op jit(solution)/shard_map/reduce_scatter | solution.py:265
  472.2 18.4 %collective-permute-start.77 = (bf16[192,1024]{1,0:T(8,128)(2,1)}, bf16[192,1024]{1,0:T(8,128)(2,1)}, u32[]{:S(2)}, u32[]{:S(2)}) collective-permute-start(bf16[192,1024]{1,0:T(8,128)(2,1)} %get-tuple-element.489), channel_id=1, source_target_pairs={{0,3},{1,2},{2,1},{3,0},{4,7},{5,6},{6,5},{7,4},{8,11},{9,10},{10,... | collective-permute-start | bytes 1179656 | tf_op jit(solution)/shard_map/ppermute | solution.py:21
  472.4 19.1 %collective-permute-start.76 = (bf16[192,1024]{1,0:T(8,128)(2,1)}, bf16[192,1024]{1,0:T(8,128)(2,1)}, u32[]{:S(2)}, u32[]{:S(2)}) collective-permute-start(bf16[192,1024]{1,0:T(8,128)(2,1)} %get-tuple-element.490), channel_id=1, source_target_pairs={{0,2},{1,3},{2,0},{3,1},{4,6},{5,7},{6,4},{7,5},{8,10},{9,11},{10,... | collective-permute-start | bytes 1179656 | tf_op jit(solution)/shard_map/ppermute | solution.py:21
  473.9 17.7 %collective-permute-start.75 = (bf16[192,1024]{1,0:T(8,128)(2,1)}, bf16[192,1024]{1,0:T(8,128)(2,1)}, u32[]{:S(2)}, u32[]{:S(2)}) collective-permute-start(bf16[192,1024]{1,0:T(8,128)(2,1)} %get-tuple-element.488), channel_id=1, source_target_pairs={{0,1},{1,0},{2,3},{3,2},{4,5},{5,4},{6,7},{7,6},{8,9},{9,8},{10,11... | collective-permute-start | bytes 1179656 | tf_op jit(solution)/shard_map/ppermute | solution.py:21
  495.7 142.0 %all-gather.17.cloned.1.call-start = ((), (), s32[]{:S(2)}) async-start(), calls=%async_computation.13 | async-start | bytes 5242880 | tf_op jit(solution)/shard_map/all_gather | solution.py:269
  502.6 20.4 %collective-permute-start.81 = (bf16[128,1024]{1,0:T(8,128)(2,1)}, bf16[128,1024]{1,0:T(8,128)(2,1)S(1)}, u32[]{:S(2)}, u32[]{:S(2)}) collective-permute-start(bf16[128,1024]{1,0:T(8,128)(2,1)} %get-tuple-element.365), channel_id=1, source_target_pairs={{0,24},{4,28},{8,16},{12,20},{16,8},{20,12},{24,0},{28,4},{1,25},{... | collective-permute-start | bytes 786440 | tf_op jit(solution)/shard_map/ppermute | solution.py:21
  506.1 24.1 %collective-permute-start.80 = (bf16[128,1024]{1,0:T(8,128)(2,1)}, bf16[128,1024]{1,0:T(8,128)(2,1)S(1)}, u32[]{:S(2)}, u32[]{:S(2)}) collective-permute-start(bf16[128,1024]{1,0:T(8,128)(2,1)} %get-tuple-element.364), channel_id=1, source_target_pairs={{0,16},{4,20},{8,24},{12,28},{16,0},{20,4},{24,8},{28,12},{1,17},{... | collective-permute-start | bytes 786440 | tf_op jit(solution)/shard_map/ppermute | solution.py:21
  507.0 23.2 %collective-permute-start.79 = (bf16[128,1024]{1,0:T(8,128)(2,1)}, bf16[128,1024]{1,0:T(8,128)(2,1)}, u32[]{:S(2)}, u32[]{:S(2)}) collective-permute-start(bf16[128,1024]{1,0:T(8,128)(2,1)} %get-tuple-element.363), channel_id=1, source_target_pairs={{0,8},{4,12},{8,0},{12,4},{16,24},{20,28},{24,16},{28,20},{1,9},{5... | collective-permute-start | bytes 786440 | tf_op jit(solution)/shard_map/ppermute | solution.py:21
  583.2 16.8 %collective-permute-start.90 = (bf16[256,768]{1,0:T(8,128)(2,1)S(1)}, bf16[256,768]{1,0:T(8,128)(2,1)S(1)}, u32[]{:S(2)}, u32[]{:S(2)}) collective-permute-start(bf16[256,768]{1,0:T(8,128)(2,1)S(1)} %slice.567), channel_id=1, source_target_pairs={{0,8},{4,12},{8,0},{12,4},{16,24},{20,28},{24,16},{28,20},{1,9},{5... | collective-permute-start | bytes 1179656 | tf_op jit(solution)/shard_map/ppermute | solution.py:21
  583.8 40.6 %collective-permute-start.103 = (bf16[128,1024]{1,0:T(8,128)(2,1)}, bf16[128,1024]{1,0:T(8,128)(2,1)}, u32[]{:S(2)}, u32[]{:S(2)}) collective-permute-start(bf16[128,1024]{1,0:T(8,128)(2,1)} %slice.568), channel_id=1, source_target_pairs={{0,16},{4,20},{8,24},{12,28},{16,0},{20,4},{24,8},{28,12},{1,17},{... | collective-permute-start | bytes 786440 | tf_op jit(solution)/shard_map/ppermute | solution.py:21
  590.1 15.3 %collective-permute-start.93 = (bf16[128,1024]{1,0:T(8,128)(2,1)}, bf16[128,1024]{1,0:T(8,128)(2,1)S(1)}, u32[]{:S(2)}, u32[]{:S(2)}) collective-permute-start(bf16[128,1024]{1,0:T(8,128)(2,1)} %get-tuple-element.409), channel_id=1, source_target_pairs={{0,2},{1,3},{2,0},{3,1},{4,6},{5,7},{6,4},{7,5},{8,10},{9,11},{10,... | collective-permute-start | bytes 786440 | tf_op jit(solution)/shard_map/ppermute | solution.py:21
  591.0 24.5 %collective-permute-start.94 = (bf16[128,1024]{1,0:T(8,128)(2,1)}, bf16[128,1024]{1,0:T(8,128)(2,1)S(1)}, u32[]{:S(2)}, u32[]{:S(2)}) collective-permute-start(bf16[128,1024]{1,0:T(8,128)(2,1)} %get-tuple-element.410), channel_id=1, source_target_pairs={{0,3},{1,2},{2,1},{3,0},{4,7},{5,6},{6,5},{7,4},{8,11},{9,10},{10,... | collective-permute-start | bytes 786440 | tf_op jit(solution)/shard_map/ppermute | solution.py:21
  601.2 15.7 %collective-permute-start.91 = (bf16[128,768]{1,0:T(8,128)(2,1)S(1)}, bf16[128,768]{1,0:T(8,128)(2,1)S(1)}, u32[]{:S(2)}, u32[]{:S(2)}) collective-permute-start(bf16[128,768]{1,0:T(8,128)(2,1)S(1)} %fusion.162), channel_id=1, source_target_pairs={{0,16},{4,20},{8,24},{12,28},{16,0},{20,4},{24,8},{28,12},{1,17},{... | collective-permute-start | bytes 589832 | tf_op jit(solution)/shard_map/ppermute | solution.py:21
  627.6 15.0 %collective-permute-start.100 = (bf16[128,768]{1,0:T(8,128)(2,1)S(1)}, bf16[128,768]{1,0:T(8,128)(2,1)S(1)}, u32[]{:S(2)}, u32[]{:S(2)}) collective-permute-start(bf16[128,768]{1,0:T(8,128)(2,1)S(1)} %add_convert_fusion.6.refs_0_), channel_id=1, source_target_pairs={{0,1},{1,0},{2,3},{3,2},{4,5},{5,4},{6,7},{7,6},{8,9},{9,8},{10,11... | collective-permute-start | bytes 589832 | tf_op jit(solution)/shard_map/ppermute | solution.py:21
  (200 other events, 1636.1 us)
Sparse Core Ops, SparseCore 0:
  35.3 31.4 all-gather.6
  98.4 28.0 all-gather.10
  128.1 30.2 all-gather.8
  190.3 27.5 all-gather.12
  321.6 34.8 reduce-scatter.4
  360.8 34.1 reduce-scatter.6
  403.6 33.7 all-gather.14
  457.4 44.4 reduce-scatter.8
  505.5 33.5 reduce-scatter.10
  555.4 63.0 all-gather.16

commit v5 on v4

--- a/solution.py
+++ b/solution.py
@@ -801,7 +801,7 @@
     shallow_in, small = join_slab(
         in_pieces, rows_own, [narrow_columns], at_wide, small.shape[0]
     )
-    shallow_out = gather_wide(after(shallow_attention_out, in_pieces[0][-1]))
+    shallow_out = gather_wide(after(shallow_attention_out, across[1]))
     small = jnp.transpose(small.reshape(wide, 8, -1), (1, 0, 2)).reshape(8, features)
     gains = small[:4].astype(F32)
     def selects_of(routes, slices):

time: 664 us -> 664 us (level)
  transfers between devices with their start and end apart: 116 -> 116, of which waited for: 55 -> 54; matrix products, arithmetic and copies ran while one was open for 24% -> 24% of each run, Pallas kernels for 17% -> 17%
where the time goes in v5:
time: 664 us; the launch traced here: 655 us
  waiting for transfers between devices  212 us (32%)
  Pallas kernels  124 us (19%)
  starting transfers between devices  113 us (17%)
  matrix products  111 us (17%)
  other arithmetic  49.5 us (7%)
  local copies, waits for them, and re-layouts  28.5 us (4%)
  between operations  16.4 us (2%)
    ppermute x106, waiting for transfers between devices, swap(): lax.ppermute(array, axis, [(i, i ^ distance) for i in range(lax.axis_size...  206 us
    pallas_call x34, Pallas kernels, call(): pl.pallas_call(kernel, out_shape=tuple(outs), in_specs=[smem()] * len(sca...  124 us
    ppermute x106, starting transfers between devices, swap(): lax.ppermute(array, axis, [(i, i ^ distance) for i in range(lax.axis_size...  110 us
    dot_general x36, matrix products, product(): lax.dot_general(left, right, (((left_dim,), (right_dim,)), ((), ())), pre...  82.7 us
    unnamed x265, local copies, waits for them, and re-layouts  13.5 us
  transfers between devices with their start and end apart: 116, of which 54 were waited for; matrix products, arithmetic and copies ran while one was open for 24% of the time, Pallas kernels for 17%

profile of v5, /device:TPU:0, one launch (start us, length us, event | category | flops | bytes accessed | tf_op | source)
XLA Modules:
  0.0 654.6 jit_solution(10128664884864862890)
XLA Ops:
  25.7 9.3 %collective-permute-done.1.refs_4_ = bf16[136,768]{1,0:T(8,128)(2,1)S(1)} collective-permute-done((bf16[136,768]{1,0:T(8,128)(2,1)}, bf16[136,768]{1,0:T(8,128)(2,1)S(1)}, u32[]{:S(2)}, u32[]{:S(2)}) %collective-permute-start.1) | collective-permute-done | bytes 208928 | tf_op jit(solution)/shard_map/ppermute | solution.py:21
  43.0 9.2 %shard_map.395 = (bf16[4,128,768]{2,1,0:T(8,128)(2,1)}, f32[128,16]{1,0:T(8,128)}, bf16[128,256]{1,0:T(8,128)(2,1)}, bf16[128,256]{1,0:T(8,128)(2,1)}, bf16[128,...) custom-call(s32[4]{0:T(128)} %gather_fusion.1, ...), custom_call_target="tpu_custom_call" | custom-call | flops 805306368 | bytes 4730880 | tf_op jit(solution)/shard_map/pallas_call | solution.py:40
  60.6 6.1 all-gather.7.cloned.1.call-done.weight_ref
  66.8 3.4 shard_map.396
  74.6 9.0 %collective-permute-done.13.refs_1_ = bf16[128,1024]{1,0:T(8,128)(2,1)S(1)} collective-permute-done((bf16[128,1024]{1,0:T(8,128)(2,1)}, bf16[128,1024]{1,0:T(8,128)(2,1)S(1)}, u32[]{:S(2)}, u32[]{:S(2)}) %collective-permute-start.13) | collective-permute-done | bytes 262176 | tf_op jit(solution)/shard_map/ppermute | solution.py:21
  83.6 9.6 %collective-permute-done.14.refs_2_ = bf16[128,1024]{1,0:T(8,128)(2,1)S(1)} collective-permute-done((bf16[128,1024]{1,0:T(8,128)(2,1)}, bf16[128,1024]{1,0:T(8,128)(2,1)S(1)}, u32[]{:S(2)}, u32[]{:S(2)}) %collective-permute-start.14) | collective-permute-done | bytes 262176 | tf_op jit(solution)/shard_map/ppermute | solution.py:21
  107.3 3.2 fusion.43
  110.5 4.5 collective-permute-done.20.refs_1_
  115.1 8.8 %collective-permute-done.21.refs_2_ = bf16[192,1024]{1,0:T(8,128)(2,1)S(1)} collective-permute-done((bf16[192,1024]{1,0:T(8,128)(2,1)S(1)}, bf16[192,1024]{1,0:T(8,128)(2,1)S(1)}, u32[]{:S(2)}, u32[]{:S(2)}) %collective-permute-start.21) | collective-permute-done | bytes 393248 | tf_op jit(solution)/shard_map/ppermute | solution.py:21
  127.5 5.5 multiply_convert_fusion.4
  139.2 8.7 %collective-permute-done.25 = bf16[192,1024]{1,0:T(8,128)(2,1)S(1)} collective-permute-done((bf16[192,1024]{1,0:T(8,128)(2,1)S(1)}, bf16[192,1024]{1,0:T(8,128)(2,1)S(1)}, u32[]{:S(2)}, u32[]{:S(2)}) %collective-permute-start.25) | collective-permute-done | bytes 393248 | tf_op jit(solution)/shard_map/ppermute | solution.py:21
  147.9 5.9 collective-permute-done.24
  163.2 4.3 collective-permute-start.28
  167.5 5.2 collective-permute-done.29
  172.7 16.1 %collective-permute-done.28 = bf16[128,1024]{1,0:T(8,128)(2,1)S(1)} collective-permute-done((bf16[128,1024]{1,0:T(8,128)(2,1)}, bf16[128,1024]{1,0:T(8,128)(2,1)S(1)}, u32[]{:S(2)}, u32[]{:S(2)}) %collective-permute-start.28) | collective-permute-done | bytes 262176 | tf_op jit(solution)/shard_map/ppermute | solution.py:21
  196.6 5.2 collective-permute-done.30.refs_1_
  201.7 5.3 collective-permute-done.31.refs_2_
  207.0 8.1 %shard_map.400 = (bf16[4,128,768]{2,1,0:T(8,128)(2,1)}, f32[128,16]{1,0:T(8,128)}, bf16[128,256]{1,0:T(8,128)(2,1)}, bf16[128,256]{1,0:T(8,128)(2,1)}, bf16[128,...) custom-call(s32[4]{0:T(128)} %gather_fusion.1, bf16[128,1024]{1,0:T(8,128)(2,1)} %copy-done.39, ...), custom_call_target="tpu_custom_call" | custom-call | flops 805306368 | bytes 3678208 | tf_op jit(solution)/shard_map/pallas_call | solution.py:40
  222.9 3.4 shard_map.401
  239.4 7.7 %collective-permute-done.37.refs_2_ = bf16[128,1024]{1,0:T(8,128)(2,1)S(1)} collective-permute-done((bf16[128,1024]{1,0:T(8,128)(2,1)}, bf16[128,1024]{1,0:T(8,128)(2,1)S(1)}, u32[]{:S(2)}, u32[]{:S(2)}) %collective-permute-start.37) | collective-permute-done | bytes 262176 | tf_op jit(solution)/shard_map/ppermute | solution.py:21
  252.9 4.5 collective-permute-done.41.refs_3_
  272.5 3.7 fusion.6
  281.4 4.4 fusion.2
  346.8 11.8 %collective-permute-done.57 = bf16[128,1024]{1,0:T(8,128)(2,1)} collective-permute-done((bf16[128,1024]{1,0:T(8,128)(2,1)}, bf16[128,1024]{1,0:T(8,128)(2,1)}, u32[]{:S(2)}, u32[]{:S(2)}) %collective-permute-start.57) | collective-permute-done | bytes 262176 | tf_op jit(solution)/shard_map/ppermute | solution.py:21
  376.3 7.5 %shard_map.410.grad_ref.refs_4_ = bf16[512,768]{1,0:T(8,128)(2,1)} custom-call(s32[4]{0:T(128)} %gather_fusion.1, bf16[4,128,768]{2,1,0:T(8,128)(2,1)} %get-tuple-element.308.packed_ref, f32[128,16]{1,0:T(8,128)} %get-tuple-element.309.level_ref, bf16[128,256]{1,0:T(8,128)(2,1)} %get-tuple-element.310.refs_0_, bf16[128,256]{1,0:T(8,128)(2,1)} %copy-done.92, ...), custom_call_target="tpu_custom_call" | custom-call | bytes 1843200 | tf_op jit(solution)/shard_map/pallas_call | solution.py:40
  383.8 3.6 shard_map.411
  391.0 7.5 %fusion.72 = f32[2048,1024]{1,0:T(8,128)} fusion(bf16[384,2048]{1,0:T(8,128)(2,1)} %copy-done.12, bf16[384,1024]{1,0:T(8,128)(2,1)} %shard_map.403, f32[384]{0:T(512)S(1)} %reduce.4), kind=kOutput, calls=%fused_computation.118 | convolution fusion | flops 1611792384 | bytes 10749440 | tf_op jit(solution)/shard_map/dot_general | solution.py:25
  408.5 5.9 collective-permute-done.65.refs_1_
  414.3 10.8 %collective-permute-done.66.refs_2_ = bf16[128,1024]{1,0:T(8,128)(2,1)} collective-permute-done((bf16[128,1024]{1,0:T(8,128)(2,1)}, bf16[128,1024]{1,0:T(8,128)(2,1)}, u32[]{:S(2)}, u32[]{:S(2)}) %collective-permute-start.66) | collective-permute-done | bytes 262176 | tf_op jit(solution)/shard_map/ppermute | solution.py:21
  437.0 5.8 multiply_reduce_fusion.5
  442.8 5.0 shard_map.414
  447.9 6.8 %collective-permute-done.74.refs_3_ = bf16[192,1024]{1,0:T(8,128)(2,1)} collective-permute-done((bf16[192,1024]{1,0:T(8,128)(2,1)}, bf16[192,1024]{1,0:T(8,128)(2,1)}, u32[]{:S(2)}, u32[]{:S(2)}) %collective-permute-start.74) | collective-permute-done | bytes 393248 | tf_op jit(solution)/shard_map/ppermute | solution.py:21
  460.0 7.6 %multiply_reduce_fusion.3 = (f32[768]{0:T(1024)S(1)}, bf16[768,1024]{1,0:T(8,128)(2,1)S(1)}) fusion(bf16[768,1024]{1,0:T(8,128)(2,1)} %copy-done.127, f32[768,1024]{1,0:T(8,128)} %get-tuple-element.548, f32[768]{0:T(1024)S(1)} %get-tuple-element.520, bf16[768,1024]{1,0:T(8,128)(2,1)} %shard_map.413, bf16[1,1024,1024]{2,1,0:T(8,128)(2,1)} %param.38), kind=kOutput, calls=%fused_computation.36 | convolution fusion | flops 1629486336 | bytes 9967616 | tf_op jit(solution)/shard_map/dot_general | solution.py:25
  467.6 3.5 fusion.178
  483.3 7.2 %fusion.180 = f32[1024,2048]{1,0:T(8,128)} fusion(bf16[384,1024]{1,0:T(8,128)(2,1)S(1)} %copy-done.11, bf16[384,2048]{1,0:T(8,128)(2,1)} %copy-done.14), kind=kOutput, calls=%fused_computation.333 | convolution fusion | flops 1610612736 | bytes 10747904 | tf_op jit(solution)/shard_map/dot_general | solution.py:25
  502.6 3.5 collective-permute-start.81
  511.3 4.0 fusion.66
  515.2 3.9 fusion.181
  519.1 3.9 shard_map.417
  523.0 7.2 %collective-permute-done.80 = bf16[128,1024]{1,0:T(8,128)(2,1)S(1)} collective-permute-done((bf16[128,1024]{1,0:T(8,128)(2,1)}, bf16[128,1024]{1,0:T(8,128)(2,1)S(1)}, u32[]{:S(2)}, u32[]{:S(2)}) %collective-permute-start.80) | collective-permute-done | bytes 262176 | tf_op jit(solution)/shard_map/ppermute | solution.py:21
  539.5 3.9 collective-permute-done.84.refs_3_
  556.8 7.5 %shard_map.420.refs_4_.grad_ref = bf16[512,768]{1,0:T(8,128)(2,1)} custom-call(s32[4]{0:T(128)} %gather_fusion.1, bf16[4,128,768]{2,1,0:T(8,128)(2,1)} %get-tuple-element.334.packed_ref, f32[128,16]{1,0:T(8,128)} %get-tuple-element.335.level_ref, bf16[128,256]{1,0:T(8,128)(2,1)} %get-tuple-element.391.refs_0_, bf16[128,256]{1,0:T(8,128)(2,1)} %copy-done.84, ...), custom_call_target="tpu_custom_call" | custom-call | bytes 1843200 | tf_op jit(solution)/shard_map/pallas_call | solution.py:40
  564.3 5.2 collective-permute-done.86
  574.3 3.8 shard_map.421
  585.6 3.5 shard_map.422
  592.7 7.3 %collective-permute-done.90 = bf16[256,768]{1,0:T(8,128)(2,1)S(1)} collective-permute-done((bf16[256,768]{1,0:T(8,128)(2,1)S(1)}, bf16[256,768]{1,0:T(8,128)(2,1)S(1)}, u32[]{:S(2)}, u32[]{:S(2)}) %collective-permute-start.90) | collective-permute-done | bytes 393248 | tf_op jit(solution)/shard_map/ppermute | solution.py:21
  605.4 10.1 %collective-permute-done.94 = bf16[128,1024]{1,0:T(8,128)(2,1)S(1)} collective-permute-done((bf16[128,1024]{1,0:T(8,128)(2,1)}, bf16[128,1024]{1,0:T(8,128)(2,1)S(1)}, u32[]{:S(2)}, u32[]{:S(2)}) %collective-permute-start.94) | collective-permute-done | bytes 262176 | tf_op jit(solution)/shard_map/ppermute | solution.py:21
  637.7 5.0 shard_map.424
  (674 shorter events, 335.5 us)
Async XLA Ops:
  7.2 59.6 %all-gather.7.cloned.1.call-start = ((), (), s32[]{:S(2)}) async-start(), calls=%async_computation.4 | async-start | bytes 2359296 | tf_op jit(solution)/shard_map/all_gather | solution.py:287
  14.3 20.7 %collective-permute-start.3 = (bf16[128,1024]{1,0:T(8,128)(2,1)}, bf16[128,1024]{1,0:T(8,128)(2,1)S(1)}, u32[]{:S(2)}, u32[]{:S(2)}) collective-permute-start(bf16[128,1024]{1,0:T(8,128)(2,1)} %refs_0_), channel_id=1, source_target_pairs={{0,1},{1,0},{2,3},{3,2},{4,5},{5,4},{6,7},{7,6},{8,9},{9,8},{10,11... | collective-permute-start | bytes 786440 | tf_op jit(solution)/shard_map/ppermute | solution.py:21
  15.8 19.3 %collective-permute-start.4 = (bf16[128,1024]{1,0:T(8,128)(2,1)}, bf16[128,1024]{1,0:T(8,128)(2,1)S(1)}, u32[]{:S(2)}, u32[]{:S(2)}) collective-permute-start(bf16[128,1024]{1,0:T(8,128)(2,1)} %refs_0_), channel_id=1, source_target_pairs={{0,2},{1,3},{2,0},{3,1},{4,6},{5,7},{6,4},{7,5},{8,10},{9,11},{10,... | collective-permute-start | bytes 786440 | tf_op jit(solution)/shard_map/ppermute | solution.py:21
  17.3 17.8 %collective-permute-start.5 = (bf16[128,1024]{1,0:T(8,128)(2,1)}, bf16[128,1024]{1,0:T(8,128)(2,1)S(1)}, u32[]{:S(2)}, u32[]{:S(2)}) collective-permute-start(bf16[128,1024]{1,0:T(8,128)(2,1)} %refs_0_), channel_id=1, source_target_pairs={{0,3},{1,2},{2,1},{3,0},{4,7},{5,6},{6,5},{7,4},{8,11},{9,10},{10,... | collective-permute-start | bytes 786440 | tf_op jit(solution)/shard_map/ppermute | solution.py:21
  17.8 17.2 %collective-permute-start.1 = (bf16[136,768]{1,0:T(8,128)(2,1)}, bf16[136,768]{1,0:T(8,128)(2,1)S(1)}, u32[]{:S(2)}, u32[]{:S(2)}) collective-permute-start(bf16[136,768]{1,0:T(8,128)(2,1)} %shard_map.392.refs_0_), channel_id=1, source_target_pairs={{0,16},{4,20},{8,24},{12,28},{16,0},{20,4},{24,8},{28,12},{1,17},{... | collective-permute-start | bytes 626696 | tf_op jit(solution)/shard_map/ppermute | solution.py:21
  35.1 171.8 %all-gather.11.cloned.1.call-start = ((), (), s32[]{:S(2)}) async-start(), calls=%async_computation.6 | async-start | bytes 1769472 | tf_op jit(solution)/shard_map/all_gather | solution.py:287
  71.7 21.5 %collective-permute-start.14 = (bf16[128,1024]{1,0:T(8,128)(2,1)}, bf16[128,1024]{1,0:T(8,128)(2,1)S(1)}, u32[]{:S(2)}, u32[]{:S(2)}) collective-permute-start(bf16[128,1024]{1,0:T(8,128)(2,1)} %get-tuple-element.249.refs_0_), channel_id=1, source_target_pairs={{0,16},{4,20},{8,24},{12,28},{16,0},{20,4},{24,8},{28,12},{1,17},{... | collective-permute-start | bytes 786440 | tf_op jit(solution)/shard_map/ppermute | solution.py:21
  72.6 20.6 %collective-permute-start.15 = (bf16[128,1024]{1,0:T(8,128)(2,1)}, bf16[128,1024]{1,0:T(8,128)(2,1)S(1)}, u32[]{:S(2)}, u32[]{:S(2)}) collective-permute-start(bf16[128,1024]{1,0:T(8,128)(2,1)} %get-tuple-element.249.refs_0_), channel_id=1, source_target_pairs={{0,24},{4,28},{8,16},{12,20},{16,8},{20,12},{24,0},{28,4},{1,25},{... | collective-permute-start | bytes 786440 | tf_op jit(solution)/shard_map/ppermute | solution.py:21
  74.6 19.1 %collective-permute-start.16 = (bf16[128,1024]{1,0:T(8,128)(2,1)}, bf16[128,1024]{1,0:T(8,128)(2,1)S(1)}, u32[]{:S(2)}, u32[]{:S(2)}) collective-permute-start(bf16[128,1024]{1,0:T(8,128)(2,1)} %get-tuple-element.249.refs_0_), channel_id=1, source_target_pairs={{0,4},{4,0},{8,12},{12,8},{16,20},{20,16},{24,28},{28,24},{1,5},{5... | collective-permute-start | bytes 786440 | tf_op jit(solution)/shard_map/ppermute | solution.py:21
  98.2 124.0 %all-gather.9.cloned.1.call-start = ((), (), s32[]{:S(2)}) async-start(), calls=%async_computation.5 | async-start | bytes 2359296 | tf_op jit(solution)/shard_map/all_gather | solution.py:287
  104.5 19.3 %collective-permute-start.21 = (bf16[192,1024]{1,0:T(8,128)(2,1)S(1)}, bf16[192,1024]{1,0:T(8,128)(2,1)S(1)}, u32[]{:S(2)}, u32[]{:S(2)}) collective-permute-start(bf16[192,1024]{1,0:T(8,128)(2,1)S(1)} %convolution_convert_fusion.3.refs_0_), channel_id=1, source_target_pairs={{0,2},{1,3},{2,0},{3,1},{4,6},{5,7},{6,4},{7,5},{8,10},{9,11},{10,... | collective-permute-start | bytes 1179656 | tf_op jit(solution)/shard_map/ppermute | solution.py:21
  106.0 17.8 %collective-permute-start.22 = (bf16[192,1024]{1,0:T(8,128)(2,1)S(1)}, bf16[192,1024]{1,0:T(8,128)(2,1)}, u32[]{:S(2)}, u32[]{:S(2)}) collective-permute-start(bf16[192,1024]{1,0:T(8,128)(2,1)S(1)} %convolution_convert_fusion.3.refs_0_), channel_id=1, source_target_pairs={{0,3},{1,2},{2,1},{3,0},{4,7},{5,6},{6,5},{7,4},{8,11},{9,10},{10,... | collective-permute-start | bytes 1179656 | tf_op jit(solution)/shard_map/ppermute | solution.py:21
  127.2 103.5 %all-gather.13.cloned.1.call-start = ((), (), s32[]{:S(2)}) async-start(), calls=%async_computation.7 | async-start | bytes 2359296 | tf_op jit(solution)/shard_map/all_gather | solution.py:287
  136.4 17.3 %collective-permute-start.24 = (bf16[192,1024]{1,0:T(8,128)(2,1)S(1)}, bf16[192,1024]{1,0:T(8,128)(2,1)S(1)}, u32[]{:S(2)}, u32[]{:S(2)}) collective-permute-start(bf16[192,1024]{1,0:T(8,128)(2,1)S(1)} %get-tuple-element.493), channel_id=1, source_target_pairs={{0,2},{1,3},{2,0},{3,1},{4,6},{5,7},{6,4},{7,5},{8,10},{9,11},{10,... | collective-permute-start | bytes 1179656 | tf_op jit(solution)/shard_map/ppermute | solution.py:21
  137.0 16.8 %collective-permute-start.23 = (bf16[192,1024]{1,0:T(8,128)(2,1)S(1)}, bf16[192,1024]{1,0:T(8,128)(2,1)S(1)}, u32[]{:S(2)}, u32[]{:S(2)}) collective-permute-start(bf16[192,1024]{1,0:T(8,128)(2,1)S(1)} %get-tuple-element.491), channel_id=1, source_target_pairs={{0,1},{1,0},{2,3},{3,2},{4,5},{5,4},{6,7},{7,6},{8,9},{9,8},{10,11... | collective-permute-start | bytes 1179656 | tf_op jit(solution)/shard_map/ppermute | solution.py:21
  163.2 25.6 %collective-permute-start.28 = (bf16[128,1024]{1,0:T(8,128)(2,1)}, bf16[128,1024]{1,0:T(8,128)(2,1)S(1)}, u32[]{:S(2)}, u32[]{:S(2)}) collective-permute-start(bf16[128,1024]{1,0:T(8,128)(2,1)} %get-tuple-element.257), channel_id=1, source_target_pairs={{0,16},{4,20},{8,24},{12,28},{16,0},{20,4},{24,8},{28,12},{1,17},{... | collective-permute-start | bytes 786440 | tf_op jit(solution)/shard_map/ppermute | solution.py:21
  167.5 21.3 %collective-permute-start.27 = (bf16[128,1024]{1,0:T(8,128)(2,1)}, bf16[128,1024]{1,0:T(8,128)(2,1)S(1)}, u32[]{:S(2)}, u32[]{:S(2)}) collective-permute-start(bf16[128,1024]{1,0:T(8,128)(2,1)} %get-tuple-element.256), channel_id=1, source_target_pairs={{0,8},{4,12},{8,0},{12,4},{16,24},{20,28},{24,16},{28,20},{1,9},{5... | collective-permute-start | bytes 786440 | tf_op jit(solution)/shard_map/ppermute | solution.py:21
  190.2 193.6 %reduce-scatter.5.cloned.1.call-start = ((), (), s32[]{:S(2)}) async-start(), calls=%async_computation.8 | async-start | bytes 2621440 | tf_op jit(solution)/shard_map/reduce_scatter | solution.py:265
  226.3 20.9 %collective-permute-start.37 = (bf16[128,1024]{1,0:T(8,128)(2,1)}, bf16[128,1024]{1,0:T(8,128)(2,1)S(1)}, u32[]{:S(2)}, u32[]{:S(2)}) collective-permute-start(bf16[128,1024]{1,0:T(8,128)(2,1)} %get-tuple-element.270.refs_0_), channel_id=1, source_target_pairs={{0,16},{4,20},{8,24},{12,28},{16,0},{20,4},{24,8},{28,12},{1,17},{... | collective-permute-start | bytes 786440 | tf_op jit(solution)/shard_map/ppermute | solution.py:21
  228.7 18.5 %collective-permute-start.38 = (bf16[128,1024]{1,0:T(8,128)(2,1)}, bf16[128,1024]{1,0:T(8,128)(2,1)S(1)}, u32[]{:S(2)}, u32[]{:S(2)}) collective-permute-start(bf16[128,1024]{1,0:T(8,128)(2,1)} %get-tuple-element.270.refs_0_), channel_id=1, source_target_pairs={{0,24},{4,28},{8,16},{12,20},{16,8},{20,12},{24,0},{28,4},{1,25},{... | collective-permute-start | bytes 786440 | tf_op jit(solution)/shard_map/ppermute | solution.py:21
  239.3 20.2 %collective-permute-start.42 = (bf16[128,1024]{1,0:T(8,128)(2,1)S(1)}, bf16[128,1024]{1,0:T(8,128)(2,1)}, u32[]{:S(2)}, u32[]{:S(2)}) collective-permute-start(bf16[128,1024]{1,0:T(8,128)(2,1)S(1)} %copy-done.55), channel_id=1, source_target_pairs={{0,4},{4,0},{8,12},{12,8},{16,20},{20,16},{24,28},{28,24},{1,5},{5... | collective-permute-start | bytes 786440 | tf_op jit(solution)/shard_map/ppermute | solution.py:21
  293.8 20.9 %collective-permute-start.49 = (bf16[96,1024]{1,0:T(8,128)(2,1)}, bf16[96,1024]{1,0:T(8,128)(2,1)}, u32[]{:S(2)}, u32[]{:S(2)}) collective-permute-start(bf16[96,1024]{1,0:T(8,128)(2,1)} %get-tuple-element.501), channel_id=1, source_target_pairs={{0,1},{1,0},{2,3},{3,2},{4,5},{5,4},{6,7},{7,6},{8,9},{9,8},{10,11... | collective-permute-start | bytes 589832 | tf_op jit(solution)/shard_map/ppermute | solution.py:21
  295.2 22.2 %collective-permute-start.51 = (bf16[96,1024]{1,0:T(8,128)(2,1)}, bf16[96,1024]{1,0:T(8,128)(2,1)}, u32[]{:S(2)}, u32[]{:S(2)}) collective-permute-start(bf16[96,1024]{1,0:T(8,128)(2,1)} %get-tuple-element.500), channel_id=1, source_target_pairs={{0,3},{1,2},{2,1},{3,0},{4,7},{5,6},{6,5},{7,4},{8,11},{9,10},{10,... | collective-permute-start | bytes 589832 | tf_op jit(solution)/shard_map/ppermute | solution.py:21
  296.8 20.6 %collective-permute-start.50 = (bf16[96,1024]{1,0:T(8,128)(2,1)S(1)}, bf16[96,1024]{1,0:T(8,128)(2,1)}, u32[]{:S(2)}, u32[]{:S(2)}) collective-permute-start(bf16[96,1024]{1,0:T(8,128)(2,1)S(1)} %get-tuple-element.499), channel_id=1, source_target_pairs={{0,2},{1,3},{2,0},{3,1},{4,6},{5,7},{6,4},{7,5},{8,10},{9,11},{10,... | collective-permute-start | bytes 589832 | tf_op jit(solution)/shard_map/ppermute | solution.py:21
  321.4 104.3 %reduce-scatter.7.cloned.1.call-start = ((), (), s32[]{:S(2)}) async-start(), calls=%async_computation.9 | async-start | bytes 2359296 | tf_op jit(solution)/shard_map/reduce_scatter | solution.py:867
  330.9 15.9 %collective-permute-start.58 = (bf16[128,1024]{1,0:T(8,128)(2,1)}, bf16[128,1024]{1,0:T(8,128)(2,1)}, u32[]{:S(2)}, u32[]{:S(2)}) collective-permute-start(bf16[128,1024]{1,0:T(8,128)(2,1)} %get-tuple-element.297), channel_id=1, source_target_pairs={{0,24},{4,28},{8,16},{12,20},{16,8},{20,12},{24,0},{28,4},{1,25},{... | collective-permute-start | bytes 786440 | tf_op jit(solution)/shard_map/ppermute | solution.py:21
  333.1 25.5 %collective-permute-start.57 = (bf16[128,1024]{1,0:T(8,128)(2,1)}, bf16[128,1024]{1,0:T(8,128)(2,1)}, u32[]{:S(2)}, u32[]{:S(2)}) collective-permute-start(bf16[128,1024]{1,0:T(8,128)(2,1)} %get-tuple-element.296), channel_id=1, source_target_pairs={{0,16},{4,20},{8,24},{12,28},{16,0},{20,4},{24,8},{28,12},{1,17},{... | collective-permute-start | bytes 786440 | tf_op jit(solution)/shard_map/ppermute | solution.py:21
  335.2 23.4 %collective-permute-start.56 = (bf16[128,1024]{1,0:T(8,128)(2,1)}, bf16[128,1024]{1,0:T(8,128)(2,1)}, u32[]{:S(2)}, u32[]{:S(2)}) collective-permute-start(bf16[128,1024]{1,0:T(8,128)(2,1)} %get-tuple-element.295), channel_id=1, source_target_pairs={{0,8},{4,12},{8,0},{12,4},{16,24},{20,28},{24,16},{28,20},{1,9},{5... | collective-permute-start | bytes 786440 | tf_op jit(solution)/shard_map/ppermute | solution.py:21
  360.6 158.5 %all-gather.15.cloned.1.call-start = ((), (), s32[]{:S(2)}) async-start(), calls=%async_computation.11 | async-start | bytes 2621440 | tf_op jit(solution)/shard_map/all_gather | solution.py:269
  403.5 127.8 %reduce-scatter.9.cloned.1.call-start = ((), (), s32[]{:S(2)}) async-start(), calls=%async_computation.10 | async-start | bytes 4128768 | tf_op jit(solution)/shard_map/reduce_scatter | solution.py:884
  404.1 21.1 %collective-permute-start.66 = (bf16[128,1024]{1,0:T(8,128)(2,1)}, bf16[128,1024]{1,0:T(8,128)(2,1)}, u32[]{:S(2)}, u32[]{:S(2)}) collective-permute-start(bf16[128,1024]{1,0:T(8,128)(2,1)} %get-tuple-element.337.refs_0_), channel_id=1, source_target_pairs={{0,16},{4,20},{8,24},{12,28},{16,0},{20,4},{24,8},{28,12},{1,17},{... | collective-permute-start | bytes 786440 | tf_op jit(solution)/shard_map/ppermute | solution.py:21
  406.0 19.2 %collective-permute-start.67 = (bf16[128,1024]{1,0:T(8,128)(2,1)}, bf16[128,1024]{1,0:T(8,128)(2,1)}, u32[]{:S(2)}, u32[]{:S(2)}) collective-permute-start(bf16[128,1024]{1,0:T(8,128)(2,1)} %get-tuple-element.337.refs_0_), channel_id=1, source_target_pairs={{0,24},{4,28},{8,16},{12,20},{16,8},{20,12},{24,0},{28,4},{1,25},{... | collective-permute-start | bytes 786440 | tf_op jit(solution)/shard_map/ppermute | solution.py:21
  408.4 17.3 %collective-permute-start.68 = (bf16[128,1024]{1,0:T(8,128)(2,1)}, bf16[128,1024]{1,0:T(8,128)(2,1)}, u32[]{:S(2)}, u32[]{:S(2)}) collective-permute-start(bf16[128,1024]{1,0:T(8,128)(2,1)} %get-tuple-element.337.refs_0_), channel_id=1, source_target_pairs={{0,4},{4,0},{8,12},{12,8},{16,20},{20,16},{24,28},{28,24},{1,5},{5... | collective-permute-start | bytes 786440 | tf_op jit(solution)/shard_map/ppermute | solution.py:21
  434.5 20.2 %collective-permute-start.74 = (bf16[192,1024]{1,0:T(8,128)(2,1)}, bf16[192,1024]{1,0:T(8,128)(2,1)}, u32[]{:S(2)}, u32[]{:S(2)}) collective-permute-start(bf16[192,1024]{1,0:T(8,128)(2,1)} %convolution_convert_fusion.2.refs_0_), channel_id=1, source_target_pairs={{0,3},{1,2},{2,1},{3,0},{4,7},{5,6},{6,5},{7,4},{8,11},{9,10},{10,... | collective-permute-start | bytes 1179656 | tf_op jit(solution)/shard_map/ppermute | solution.py:21
  457.3 95.7 %reduce-scatter.11.cloned.1.call-start = ((), (), s32[]{:S(2)}) async-start(), calls=%async_computation.12 | async-start | bytes 2621440 | tf_op jit(solution)/shard_map/reduce_scatter | solution.py:265
  472.2 18.4 %collective-permute-start.77 = (bf16[192,1024]{1,0:T(8,128)(2,1)}, bf16[192,1024]{1,0:T(8,128)(2,1)}, u32[]{:S(2)}, u32[]{:S(2)}) collective-permute-start(bf16[192,1024]{1,0:T(8,128)(2,1)} %get-tuple-element.489), channel_id=1, source_target_pairs={{0,3},{1,2},{2,1},{3,0},{4,7},{5,6},{6,5},{7,4},{8,11},{9,10},{10,... | collective-permute-start | bytes 1179656 | tf_op jit(solution)/shard_map/ppermute | solution.py:21
  472.4 19.1 %collective-permute-start.76 = (bf16[192,1024]{1,0:T(8,128)(2,1)}, bf16[192,1024]{1,0:T(8,128)(2,1)}, u32[]{:S(2)}, u32[]{:S(2)}) collective-permute-start(bf16[192,1024]{1,0:T(8,128)(2,1)} %get-tuple-element.490), channel_id=1, source_target_pairs={{0,2},{1,3},{2,0},{3,1},{4,6},{5,7},{6,4},{7,5},{8,10},{9,11},{10,... | collective-permute-start | bytes 1179656 | tf_op jit(solution)/shard_map/ppermute | solution.py:21
  473.9 17.7 %collective-permute-start.75 = (bf16[192,1024]{1,0:T(8,128)(2,1)}, bf16[192,1024]{1,0:T(8,128)(2,1)}, u32[]{:S(2)}, u32[]{:S(2)}) collective-permute-start(bf16[192,1024]{1,0:T(8,128)(2,1)} %get-tuple-element.488), channel_id=1, source_target_pairs={{0,1},{1,0},{2,3},{3,2},{4,5},{5,4},{6,7},{7,6},{8,9},{9,8},{10,11... | collective-permute-start | bytes 1179656 | tf_op jit(solution)/shard_map/ppermute | solution.py:21
  495.7 142.0 %all-gather.17.cloned.1.call-start = ((), (), s32[]{:S(2)}) async-start(), calls=%async_computation.13 | async-start | bytes 5242880 | tf_op jit(solution)/shard_map/all_gather | solution.py:269
  502.6 20.4 %collective-permute-start.81 = (bf16[128,1024]{1,0:T(8,128)(2,1)}, bf16[128,1024]{1,0:T(8,128)(2,1)S(1)}, u32[]{:S(2)}, u32[]{:S(2)}) collective-permute-start(bf16[128,1024]{1,0:T(8,128)(2,1)} %get-tuple-element.365), channel_id=1, source_target_pairs={{0,24},{4,28},{8,16},{12,20},{16,8},{20,12},{24,0},{28,4},{1,25},{... | collective-permute-start | bytes 786440 | tf_op jit(solution)/shard_map/ppermute | solution.py:21
  506.1 24.1 %collective-permute-start.80 = (bf16[128,1024]{1,0:T(8,128)(2,1)}, bf16[128,1024]{1,0:T(8,128)(2,1)S(1)}, u32[]{:S(2)}, u32[]{:S(2)}) collective-permute-start(bf16[128,1024]{1,0:T(8,128)(2,1)} %get-tuple-element.364), channel_id=1, source_target_pairs={{0,16},{4,20},{8,24},{12,28},{16,0},{20,4},{24,8},{28,12},{1,17},{... | collective-permute-start | bytes 786440 | tf_op jit(solution)/shard_map/ppermute | solution.py:21
  507.0 23.1 %collective-permute-start.79 = (bf16[128,1024]{1,0:T(8,128)(2,1)}, bf16[128,1024]{1,0:T(8,128)(2,1)}, u32[]{:S(2)}, u32[]{:S(2)}) collective-permute-start(bf16[128,1024]{1,0:T(8,128)(2,1)} %get-tuple-element.363), channel_id=1, source_target_pairs={{0,8},{4,12},{8,0},{12,4},{16,24},{20,28},{24,16},{28,20},{1,9},{5... | collective-permute-start | bytes 786440 | tf_op jit(solution)/shard_map/ppermute | solution.py:21
  583.1 16.8 %collective-permute-start.90 = (bf16[256,768]{1,0:T(8,128)(2,1)S(1)}, bf16[256,768]{1,0:T(8,128)(2,1)S(1)}, u32[]{:S(2)}, u32[]{:S(2)}) collective-permute-start(bf16[256,768]{1,0:T(8,128)(2,1)S(1)} %slice.567), channel_id=1, source_target_pairs={{0,8},{4,12},{8,0},{12,4},{16,24},{20,28},{24,16},{28,20},{1,9},{5... | collective-permute-start | bytes 1179656 | tf_op jit(solution)/shard_map/ppermute | solution.py:21
  583.7 40.6 %collective-permute-start.103 = (bf16[128,1024]{1,0:T(8,128)(2,1)}, bf16[128,1024]{1,0:T(8,128)(2,1)}, u32[]{:S(2)}, u32[]{:S(2)}) collective-permute-start(bf16[128,1024]{1,0:T(8,128)(2,1)} %slice.568), channel_id=1, source_target_pairs={{0,16},{4,20},{8,24},{12,28},{16,0},{20,4},{24,8},{28,12},{1,17},{... | collective-permute-start | bytes 786440 | tf_op jit(solution)/shard_map/ppermute | solution.py:21
  590.1 15.3 %collective-permute-start.93 = (bf16[128,1024]{1,0:T(8,128)(2,1)}, bf16[128,1024]{1,0:T(8,128)(2,1)S(1)}, u32[]{:S(2)}, u32[]{:S(2)}) collective-permute-start(bf16[128,1024]{1,0:T(8,128)(2,1)} %get-tuple-element.409), channel_id=1, source_target_pairs={{0,2},{1,3},{2,0},{3,1},{4,6},{5,7},{6,4},{7,5},{8,10},{9,11},{10,... | collective-permute-start | bytes 786440 | tf_op jit(solution)/shard_map/ppermute | solution.py:21
  591.0 24.5 %collective-permute-start.94 = (bf16[128,1024]{1,0:T(8,128)(2,1)}, bf16[128,1024]{1,0:T(8,128)(2,1)S(1)}, u32[]{:S(2)}, u32[]{:S(2)}) collective-permute-start(bf16[128,1024]{1,0:T(8,128)(2,1)} %get-tuple-element.410), channel_id=1, source_target_pairs={{0,3},{1,2},{2,1},{3,0},{4,7},{5,6},{6,5},{7,4},{8,11},{9,10},{10,... | collective-permute-start | bytes 786440 | tf_op jit(solution)/shard_map/ppermute | solution.py:21
  601.2 15.7 %collective-permute-start.91 = (bf16[128,768]{1,0:T(8,128)(2,1)S(1)}, bf16[128,768]{1,0:T(8,128)(2,1)S(1)}, u32[]{:S(2)}, u32[]{:S(2)}) collective-permute-start(bf16[128,768]{1,0:T(8,128)(2,1)S(1)} %fusion.162), channel_id=1, source_target_pairs={{0,16},{4,20},{8,24},{12,28},{16,0},{20,4},{24,8},{28,12},{1,17},{... | collective-permute-start | bytes 589832 | tf_op jit(solution)/shard_map/ppermute | solution.py:21
  627.6 15.0 %collective-permute-start.100 = (bf16[128,768]{1,0:T(8,128)(2,1)S(1)}, bf16[128,768]{1,0:T(8,128)(2,1)S(1)}, u32[]{:S(2)}, u32[]{:S(2)}) collective-permute-start(bf16[128,768]{1,0:T(8,128)(2,1)S(1)} %add_convert_fusion.6.refs_0_), channel_id=1, source_target_pairs={{0,1},{1,0},{2,3},{3,2},{4,5},{5,4},{6,7},{7,6},{8,9},{9,8},{10,11... | collective-permute-start | bytes 589832 | tf_op jit(solution)/shard_map/ppermute | solution.py:21
  (200 other events, 1636.6 us)
Sparse Core Ops, SparseCore 0:
  35.3 31.4 all-gather.6
  98.4 28.0 all-gather.10
  128.1 30.2 all-gather.8
  190.3 27.5 all-gather.12
  321.5 34.8 reduce-scatter.4
  360.8 34.4 reduce-scatter.6
  403.6 33.7 all-gather.14
  457.4 44.4 reduce-scatter.8
  505.5 33.5 reduce-scatter.10
  555.4 63.0 all-gather.16
